TPU v7x, 32 devices: a whole 2x2x4 slice. The times are simulated.
32 devices in a mesh: draws: 2 (over x), rows: 16 (over z, y, core).
Axes of the slice: x: 2, y: 2, z: 4, core: 2. Of those that a mesh axis runs over, the one named last changes fastest.
Arguments:
- leaf_rhs: bfloat16 [192, 256, 256], P('rows'), may hold values from -6 to 6
- separator_rhs: bfloat16 [4, 16, 256, 256], P(None, 'rows'), may hold values from -6 to 6
- leaf_inverse: bfloat16 [384, 256, 256], P(('draws', 'rows')), parts along dimension 0, as said below
- leaf_factor: bfloat16 [256, 4, 256, 256], P(('draws', 'rows')), parts along dimension 0, may hold values from -0.125 to 0.125
- separator_inverse: bfloat16 [4, 32, 256, 256], P(None, ('draws', 'rows')), parts along dimension 1, as said below
- separator_factor: bfloat16 [4, 32, 2, 256, 256], P(None, ('draws', 'rows')), parts along dimension 1, may hold values from -0.1875 to 0.1875
- block_pattern: int32 [128, 4], P('rows'), may hold values from 0 to 7, as said below
- link_row: int32 [16], P('rows'), may hold values from 8 to 11
Outputs:
- leaf_solution: bfloat16 [384, 256, 256], P(('draws', 'rows')), parts along dimension 0
- separator_solution: bfloat16 [4, 32, 256, 256], P(None, ('draws', 'rows')), parts along dimension 1
There are 2 independent parts, one for each index of `draws`. A program takes and returns all parts, laid end to end along the dimension named above; an argument that names none is the same for every part. Nothing has to cross between parts.
Inputs may be any that keep to these rules, and one draw needn't show every extreme that they name: `block_pattern`: for a block row on leaf level v >= 1 the 4 entries are distinct and below v * 4. `leaf_inverse`: every block is invertible. `separator_inverse`: every block is invertible.
All inputs are finite; a program needn't handle non-finite values.
Results may differ from a plain program's by a relative error of at most 0.011.
Values may be sent and summed in bfloat16 or wider, within the bound.
No kernel may reach another device: no remote copies, remote signals or barrier semaphores. Data moves between devices by JAX's collectives and lax.ppermute only.
A program may use at most 64 MiB of HBM per device.

v0:
```python
import jax
import jax.numpy as jnp
from jax import lax
from jax.sharding import PartitionSpec as P

LEVEL_ROWS = 4
LEAF_LEVELS = 3


def passed_along(value, axis, by):
    length = lax.axis_size(axis)
    return lax.ppermute(value, axis, [(i, (i + by) % length) for i in range(length)])


def leaf_solve(rhs_piece, leaf_inverse, leaf_factor, block_pattern):
    solved = jnp.einsum(
        "nij,njr->nir",
        leaf_inverse[:LEVEL_ROWS],
        rhs_piece[:LEVEL_ROWS],
        preferred_element_type=jnp.float32,
    ).astype(jnp.bfloat16)
    for height in range(1, LEAF_LEVELS):
        low_row = (height - 1) * LEVEL_ROWS
        top_row = height * LEVEL_ROWS
        picked = jnp.take(solved, block_pattern[low_row:top_row], axis=0)
        accumulated = jnp.einsum(
            "nkij,nkjr->nir",
            leaf_factor[low_row:top_row],
            picked,
            preferred_element_type=jnp.float32,
        )
        residual = (
            rhs_piece[top_row : top_row + LEVEL_ROWS].astype(jnp.float32) - accumulated
        ).astype(jnp.bfloat16)
        fresh_rows = jnp.einsum(
            "nij,njr->nir",
            leaf_inverse[top_row : top_row + LEVEL_ROWS],
            residual,
            preferred_element_type=jnp.float32,
        ).astype(jnp.bfloat16)
        solved = jnp.concatenate([solved, fresh_rows], axis=0)
    return solved


def node_solve(lower_in, upper_in, rhs_node, inverse_node, factor_node):
    accumulated = jnp.dot(factor_node[0], lower_in, preferred_element_type=jnp.float32)
    accumulated = accumulated + jnp.dot(
        factor_node[1], upper_in, preferred_element_type=jnp.float32
    )
    residual = (rhs_node.astype(jnp.float32) - accumulated).astype(jnp.bfloat16)
    return jnp.dot(inverse_node, residual, preferred_element_type=jnp.float32).astype(jnp.bfloat16)


def level_solve(solved, link_row, separator_rhs, separator_inverse, separator_factor):
    depth = separator_rhs.shape[0]
    edge_block = lax.dynamic_index_in_dim(solved, link_row[0], 0, keepdims=False)
    from_lower = passed_along(edge_block, "rows", 1)
    level_block = node_solve(
        from_lower, edge_block, separator_rhs[0, 0], separator_inverse[0, 0], separator_factor[0, 0]
    )
    levels = [level_block]
    for height in range(1, depth):
        stride = 2 ** (height - 1)
        lower_child = passed_along(level_block, "rows", stride)
        upper_child = passed_along(level_block, "rows", -stride)
        level_block = node_solve(
            lower_child,
            upper_child,
            separator_rhs[height, 0],
            separator_inverse[height, 0],
            separator_factor[height, 0],
        )
        levels.append(level_block)
    return jnp.stack(levels, axis=0)[:, None]


def shards(
    leaf_rhs,
    separator_rhs,
    leaf_inverse,
    leaf_factor,
    separator_inverse,
    separator_factor,
    block_pattern,
    link_row,
):
    solved = leaf_solve(leaf_rhs, leaf_inverse, leaf_factor, block_pattern)
    return (
        solved,
        level_solve(solved, link_row, separator_rhs, separator_inverse, separator_factor),
    )


def solution(mesh):
    placed = (
        P("rows", None, None),
        P(None, "rows", None, None),
        P(("draws", "rows"), None, None),
        P(("draws", "rows"), None, None, None),
        P(None, ("draws", "rows"), None, None),
        P(None, ("draws", "rows"), None, None, None),
        P("rows", None),
        P("rows"),
    )
    return jax.shard_map(
        shards,
        mesh=mesh,
        in_specs=placed,
        out_specs=(P(("draws", "rows"), None, None), P(None, ("draws", "rows"), None, None)),
        check_vma=False,
    )
```

profile of v0, /device:TPU:0, one launch (start us, length us, event | category | flops | bytes accessed | tf_op | source)
XLA Modules:
  0.0 58.9 jit_solution(13481023518071097909)
XLA Ops:
  0.6 0.8 %compare_select_fusion = (s32[4,4]{0,1:T(4,128)S(1)}, s32[4,4]{0,1:T(4,128)S(1)}) fusion(s32[8,4]{0,1:T(4,128)} %param.14), kind=kLoop, calls=%fused_computation.95 | loop fusion | flops 96 | bytes 256 | tf_op jit(solution)/shard_map/jit(_take)/jit(_where)/select_n | solution.py:25
  1.5 0.8 %compare_and_fusion = (pred[4,4]{0,1:T(4,128)(4,1)S(1)}, pred[4,4]{0,1:T(4,128)(4,1)S(1)}) fusion(s32[8,4]{0,1:T(4,128)} %param.14), kind=kLoop, calls=%fused_computation.99 | loop fusion | flops 192 | bytes 160 | tf_op jit(solution)/shard_map/jit(_take)/and | solution.py:25
  2.6 1.5 %convolution_convert_fusion.2 = bf16[4,256,256]{2,1,0:T(8,128)(2,1)S(1)} fusion(bf16[12,256,256]{2,1,0:T(8,128)(2,1)} %param.10, bf16[12,256,256]{2,1,0:T(8,128)(2,1)} %param.8), kind=kOutput, calls=%fused_computation.19 | convolution fusion | flops 134479872 | bytes 2621440 | tf_op jit(solution)/shard_map/nij,njr->nir/dot_general | solution.py:16
  4.8 2.9 %fusion.38 = bf16[4,256,256]{2,1,0:T(8,128)(2,1)S(1)} fusion(bf16[4,4,256,256]{3,2,1,0:T(8,128)(2,1)S(1)} %bitcast.157, pred[4,4]{1,0:T(4,128)(4,1)S(1)} %copy.10, bf16[8,4,256,256]{3,2,1,0:T(8,128)(2,1)} %param.11, bf16[12,256,256]{2,1,0:T(8,128)(2,1)} %param.10, bf16[12,256,256]{2,1,0:T(8,128)(2,1)} %param.8), kind=kOutput, calls=%fused_computation.20 | convolution fusion | flops 673185792 | bytes 5767184 | tf_op jit(solution)/shard_map/nij,njr->nir/dot_general | solution.py:35
  8.1 2.0 %gather_fusion.1 = bf16[16,256,256]{2,1,0:T(8,128)(2,1)} fusion(bf16[8,256,256]{2,1,0:T(8,128)(2,1)S(1)} %pad_maximum_fusion.1, s32[1024]{0:T(1024)S(1)} %pad_clamp_fusion), kind=kCustom, calls=%fused_computation.1 | custom fusion | bytes 4194368 | tf_op jit(solution)/shard_map/jit(_take)/gather | solution.py:25
  10.1 4.3 %fusion.39 = bf16[4,256,256]{2,1,0:T(8,128)(2,1)} fusion(bf16[4,4,256,256]{3,2,1,0:T(8,128)(2,1)} %bitcast.156, pred[4,4]{1,0:T(4,128)(4,1)S(1)} %copy.14, bf16[8,4,256,256]{3,2,1,0:T(8,128)(2,1)} %param.11, bf16[12,256,256]{2,1,0:T(8,128)(2,1)} %param.10, bf16[12,256,256]{2,1,0:T(8,128)(2,1)} %param.8), kind=kOutput, calls=%fused_computation.21 | convolution fusion | flops 673185792 | bytes 5767184 | tf_op jit(solution)/shard_map/nij,njr->nir/dot_general | solution.py:35
  14.3 1.3 %pad_maximum_fusion = bf16[12,256,256]{2,1,0:T(8,128)(2,1)S(1)} fusion(bf16[4,256,256]{2,1,0:T(8,128)(2,1)} %fusion.39, bf16[4,256,256]{2,1,0:T(8,128)(2,1)S(1)} %fusion.38, bf16[4,256,256]{2,1,0:T(8,128)(2,1)S(1)} %convolution_convert_fusion.2), kind=kLoop, calls=%fused_computation.10 | loop fusion | flops 1572864 | bytes 3145728 | tf_op jit(solution)/shard_map/concatenate | solution.py:41
  16.9 1.1 %fusion.96 = f32[256,256]{0,1:T(8,128)S(1)} fusion(bf16[256,256]{1,0:T(8,128)(2,1)S(1)} %dynamic-slice_bitcast_fusion, bf16[4,1,2,256,256]{4,3,2,1,0:T(8,128)(2,1)} %param.13), kind=kOutput, calls=%fused_computation.75 | convolution fusion | flops 33554432 | bytes 524288 | tf_op jit(solution)/shard_map/dot_general | solution.py:47
  18.0 6.7 %collective-permute-done = bf16[256,256]{1,0:T(8,128)(2,1)} collective-permute-done((bf16[256,256]{1,0:T(8,128)(2,1)S(1)}, bf16[256,256]{1,0:T(8,128)(2,1)}, u32[]{:S(2)}, u32[]{:S(2)}) %collective-permute-start) | collective-permute-done | bytes 131104 | tf_op jit(solution)/shard_map/ppermute | solution.py:12
  24.7 1.5 %convolution_convert_fusion.6 = bf16[256,256]{1,0:T(8,128)(2,1)S(1)} fusion(f32[256,256]{0,1:T(8,128)S(1)} %fusion.96, bf16[256,256]{1,0:T(8,128)(2,1)} %collective-permute-done, bf16[4,1,256,256]{3,2,1,0:T(8,128)(2,1)S(1)} %copy-done.2, bf16[4,1,2,256,256]{4,3,2,1,0:T(8,128)(2,1)} %param.13, bf16[4,1,256,256]{3,2,1,0:T(8,128)(2,1)} %param.9), kind=kOutput, calls=%fused_computation.41 | convolution fusion | flops 67436544 | bytes 917504 | tf_op jit(solution)/shard_map/dot_general | solution.py:51
  26.7 2.0 %collective-permute-done.2 = bf16[256,256]{0,1:T(8,128)(2,1)S(1)} collective-permute-done((bf16[256,256]{0,1:T(8,128)(2,1)S(1)}, bf16[256,256]{0,1:T(8,128)(2,1)S(1)}, u32[]{:S(2)}, u32[]{:S(2)}) %collective-permute-start.2) | collective-permute-done | bytes 131104 | tf_op jit(solution)/shard_map/ppermute | solution.py:12
  28.7 1.1 %fusion.91 = f32[256,256]{0,1:T(8,128)S(1)} fusion(bf16[256,256]{0,1:T(8,128)(2,1)S(1)} %collective-permute-done.2, bf16[4,1,2,256,256]{4,3,2,1,0:T(8,128)(2,1)} %param.13), kind=kOutput, calls=%fused_computation.71 | convolution fusion | flops 33554432 | bytes 524288 | tf_op jit(solution)/shard_map/dot_general | solution.py:47
  29.9 3.6 %collective-permute-done.1 = bf16[256,256]{0,1:T(8,128)(2,1)} collective-permute-done((bf16[256,256]{0,1:T(8,128)(2,1)S(1)}, bf16[256,256]{0,1:T(8,128)(2,1)}, u32[]{:S(2)}, u32[]{:S(2)}) %collective-permute-start.1) | collective-permute-done | bytes 131104 | tf_op jit(solution)/shard_map/ppermute | solution.py:12
  33.5 2.1 %convolution_convert_fusion.5 = bf16[256,256]{1,0:T(8,128)(2,1)} fusion(f32[256,256]{0,1:T(8,128)S(1)} %fusion.91, bf16[256,256]{0,1:T(8,128)(2,1)} %collective-permute-done.1, bf16[4,1,256,256]{3,2,1,0:T(8,128)(2,1)S(1)} %copy-done.2, bf16[4,1,2,256,256]{4,3,2,1,0:T(8,128)(2,1)S(1)} %copy-done.1, bf16[4,1,256,256]{3,2,1,0:T(8,128)(2,1)} %param.9), kind=kOutput, calls=%fused_computation.40 | convolution fusion | flops 67436544 | bytes 917504 | tf_op jit(solution)/shard_map/dot_general | solution.py:51
  35.6 1.0 %collective-permute-start.4 = (bf16[256,256]{0,1:T(8,128)(2,1)}, bf16[256,256]{0,1:T(8,128)(2,1)S(1)}, u32[]{:S(2)}, u32[]{:S(2)}) collective-permute-start(bf16[256,256]{0,1:T(8,128)(2,1)} %bitcast.161), channel_id=1, source_target_pairs={{0,14},{1,15},{2,0},{3,1},{4,2},{5,3},{6,4},{7,5},{8,6},{9,7},{10,... | collective-permute-start | bytes 393224 | tf_op jit(solution)/shard_map/ppermute | solution.py:12
  36.6 1.0 %collective-permute-start.3 = (bf16[256,256]{0,1:T(8,128)(2,1)}, bf16[256,256]{0,1:T(8,128)(2,1)}, u32[]{:S(2)}, u32[]{:S(2)}) collective-permute-start(bf16[256,256]{0,1:T(8,128)(2,1)} %bitcast.162), channel_id=1, source_target_pairs={{0,2},{1,3},{2,4},{3,5},{4,6},{5,7},{6,8},{7,9},{8,10},{9,11},{10,... | collective-permute-start | bytes 393224 | tf_op jit(solution)/shard_map/ppermute | solution.py:12
  37.6 3.2 %collective-permute-done.4 = bf16[256,256]{0,1:T(8,128)(2,1)S(1)} collective-permute-done((bf16[256,256]{0,1:T(8,128)(2,1)}, bf16[256,256]{0,1:T(8,128)(2,1)S(1)}, u32[]{:S(2)}, u32[]{:S(2)}) %collective-permute-start.4) | collective-permute-done | bytes 131104 | tf_op jit(solution)/shard_map/ppermute | solution.py:12
  41.0 4.2 %collective-permute-done.3 = bf16[256,256]{0,1:T(8,128)(2,1)} collective-permute-done((bf16[256,256]{0,1:T(8,128)(2,1)}, bf16[256,256]{0,1:T(8,128)(2,1)}, u32[]{:S(2)}, u32[]{:S(2)}) %collective-permute-start.3) | collective-permute-done | bytes 131104 | tf_op jit(solution)/shard_map/ppermute | solution.py:12
  45.2 2.1 %convolution_convert_fusion.4 = bf16[256,256]{1,0:T(8,128)(2,1)} fusion(f32[256,256]{0,1:T(8,128)S(1)} %fusion.86, bf16[256,256]{0,1:T(8,128)(2,1)} %collective-permute-done.3, bf16[4,1,256,256]{3,2,1,0:T(8,128)(2,1)S(1)} %copy-done.2, bf16[4,1,2,256,256]{4,3,2,1,0:T(8,128)(2,1)S(1)} %copy-done.1, bf16[4,1,256,256]{3,2,1,0:T(8,128)(2,1)} %param.9), kind=kOutput, calls=%fused_computation.39 | convolution fusion | flops 67436544 | bytes 917504 | tf_op jit(solution)/shard_map/dot_general | solution.py:51
  47.3 2.0 %collective-permute-start.5 = (bf16[256,256]{0,1:T(8,128)(2,1)}, bf16[256,256]{0,1:T(8,128)(2,1)S(1)}, u32[]{:S(2)}, u32[]{:S(2)}) collective-permute-start(bf16[256,256]{0,1:T(8,128)(2,1)} %bitcast.165), channel_id=1, source_target_pairs={{0,4},{1,5},{2,6},{3,7},{4,8},{5,9},{6,10},{7,11},{8,12},{9,13},{1... | collective-permute-start | bytes 393224 | tf_op jit(solution)/shard_map/ppermute | solution.py:12
  49.3 6.0 %collective-permute-done.6 = bf16[256,256]{0,1:T(8,128)(2,1)S(1)} collective-permute-done((bf16[256,256]{0,1:T(8,128)(2,1)}, bf16[256,256]{0,1:T(8,128)(2,1)S(1)}, u32[]{:S(2)}, u32[]{:S(2)}) %collective-permute-start.6) | collective-permute-done | bytes 131104 | tf_op jit(solution)/shard_map/ppermute | solution.py:12
  55.5 1.4 %fusion.60 = bf16[1,256,256]{1,2,0:T(8,128)(2,1)S(1)} fusion(f32[256,256]{0,1:T(8,128)S(1)} %fusion.81, bf16[256,256]{0,1:T(8,128)(2,1)S(1)} %collective-permute-done.5, bf16[4,1,256,256]{3,2,1,0:T(8,128)(2,1)S(1)} %copy-done.2, bf16[4,1,2,256,256]{4,3,2,1,0:T(8,128)(2,1)S(1)} %copy-done.1, bf16[4,1,256,256]{3,2,1,0:T(8,128)(2,1)} %param.9), kind=kOutput, calls=%fused_computation.42 | convolution fusion | flops 67436544 | bytes 917504 | tf_op jit(solution)/shard_map/dot_general | solution.py:51
  56.9 1.0 %maximum_bitcast_fusion = bf16[4,1,256,256]{2,3,0,1:T(8,128)(2,1)S(1)} fusion(bf16[1,256,256]{1,2,0:T(8,128)(2,1)S(1)} %fusion.60, bf16[1,256,256]{1,2,0:T(8,128)(2,1)} %bitcast.166, bf16[1,256,256]{1,2,0:T(8,128)(2,1)} %bitcast.163, bf16[1,256,256]{1,2,0:T(8,128)(2,1)S(1)} %bitcast.160), kind=kLoop, calls=%fused_computation.48 | loop fusion | flops 786432 | bytes 1048576 | tf_op jit(solution)/shard_map/broadcast_in_dim | solution.py:74
  57.9 1.0 %copy.18 = bf16[4,1,256,256]{3,2,1,0:T(8,128)(2,1)} copy(bf16[4,1,256,256]{2,3,0,1:T(8,128)(2,1)S(1)} %maximum_bitcast_fusion) | data formatting | bytes 1048576
  (24 shorter events, 2.9 us)
Async XLA Ops:
  14.3 10.3 %copy-start.2 = (bf16[4,1,256,256]{3,2,1,0:T(8,128)(2,1)S(1)}, bf16[4,1,256,256]{3,2,1,0:T(8,128)(2,1)}, u32[]{:S(2)}) copy-start(bf16[4,1,256,256]{3,2,1,0:T(8,128)(2,1)} %param.12) | copy-start | bytes 1572868
  15.6 31.7 %copy-start = (bf16[12,256,256]{2,1,0:T(8,128)(2,1)}, bf16[12,256,256]{2,1,0:T(8,128)(2,1)S(1)}, u32[]{:S(2)}) copy-start(bf16[12,256,256]{2,1,0:T(8,128)(2,1)S(1)} %pad_maximum_fusion) | copy-start | bytes 4718596
  15.6 17.8 %copy-start.1 = (bf16[4,1,2,256,256]{4,3,2,1,0:T(8,128)(2,1)S(1)}, bf16[4,1,2,256,256]{4,3,2,1,0:T(8,128)(2,1)}, u32[]{:S(2)}) copy-start(bf16[4,1,2,256,256]{4,3,2,1,0:T(8,128)(2,1)} %param.13) | copy-start | bytes 3145732
  16.4 8.3 %collective-permute-start = (bf16[256,256]{1,0:T(8,128)(2,1)S(1)}, bf16[256,256]{1,0:T(8,128)(2,1)}, u32[]{:S(2)}, u32[]{:S(2)}) collective-permute-start(bf16[256,256]{1,0:T(8,128)(2,1)S(1)} %dynamic-slice_bitcast_fusion), channel_id=1, source_target_pairs={{0,1},{1,2},{2,3},{3,4},{4,5},{5,6},{6,7},{7,8},{8,9},{9,10},{10,1... | collective-permute-start | bytes 393224 | tf_op jit(solution)/shard_map/ppermute | solution.py:12
  26.2 2.6 %collective-permute-start.2 = (bf16[256,256]{0,1:T(8,128)(2,1)S(1)}, bf16[256,256]{0,1:T(8,128)(2,1)S(1)}, u32[]{:S(2)}, u32[]{:S(2)}) collective-permute-start(bf16[256,256]{0,1:T(8,128)(2,1)S(1)} %bitcast.158), channel_id=1, source_target_pairs={{0,15},{1,0},{2,1},{3,2},{4,3},{5,4},{6,5},{7,6},{8,7},{9,8},{10,9... | collective-permute-start | bytes 393224 | tf_op jit(solution)/shard_map/ppermute | solution.py:12
  26.2 7.2 %collective-permute-start.1 = (bf16[256,256]{0,1:T(8,128)(2,1)S(1)}, bf16[256,256]{0,1:T(8,128)(2,1)}, u32[]{:S(2)}, u32[]{:S(2)}) collective-permute-start(bf16[256,256]{0,1:T(8,128)(2,1)S(1)} %bitcast.159), channel_id=1, source_target_pairs={{0,1},{1,2},{2,3},{3,4},{4,5},{5,6},{6,7},{7,8},{8,9},{9,10},{10,1... | collective-permute-start | bytes 393224 | tf_op jit(solution)/shard_map/ppermute | solution.py:12
  35.6 5.2 %collective-permute-start.4 = (bf16[256,256]{0,1:T(8,128)(2,1)}, bf16[256,256]{0,1:T(8,128)(2,1)S(1)}, u32[]{:S(2)}, u32[]{:S(2)}) collective-permute-start(bf16[256,256]{0,1:T(8,128)(2,1)} %bitcast.161), channel_id=1, source_target_pairs={{0,14},{1,15},{2,0},{3,1},{4,2},{5,3},{6,4},{7,5},{8,6},{9,7},{10,... | collective-permute-start | bytes 393224 | tf_op jit(solution)/shard_map/ppermute | solution.py:12
  36.6 8.6 %collective-permute-start.3 = (bf16[256,256]{0,1:T(8,128)(2,1)}, bf16[256,256]{0,1:T(8,128)(2,1)}, u32[]{:S(2)}, u32[]{:S(2)}) collective-permute-start(bf16[256,256]{0,1:T(8,128)(2,1)} %bitcast.162), channel_id=1, source_target_pairs={{0,2},{1,3},{2,4},{3,5},{4,6},{5,7},{6,8},{7,9},{8,10},{9,11},{10,... | collective-permute-start | bytes 393224 | tf_op jit(solution)/shard_map/ppermute | solution.py:12
  47.3 8.0 %collective-permute-start.6 = (bf16[256,256]{0,1:T(8,128)(2,1)}, bf16[256,256]{0,1:T(8,128)(2,1)S(1)}, u32[]{:S(2)}, u32[]{:S(2)}) collective-permute-start(bf16[256,256]{0,1:T(8,128)(2,1)} %bitcast.164), channel_id=1, source_target_pairs={{0,12},{1,13},{2,14},{3,15},{4,0},{5,1},{6,2},{7,3},{8,4},{9,5},{1... | collective-permute-start | bytes 393224 | tf_op jit(solution)/shard_map/ppermute | solution.py:12
  47.3 8.2 %collective-permute-start.5 = (bf16[256,256]{0,1:T(8,128)(2,1)}, bf16[256,256]{0,1:T(8,128)(2,1)S(1)}, u32[]{:S(2)}, u32[]{:S(2)}) collective-permute-start(bf16[256,256]{0,1:T(8,128)(2,1)} %bitcast.165), channel_id=1, source_target_pairs={{0,4},{1,5},{2,6},{3,7},{4,8},{5,9},{6,10},{7,11},{8,12},{9,13},{1... | collective-permute-start | bytes 393224 | tf_op jit(solution)/shard_map/ppermute | solution.py:12
where the time goes:
time: 59.3 us; the launch traced here: 58.9 us
  waiting for transfers between devices  25.6 us (43%)
  matrix products  18.3 us (31%)
  starting transfers between devices  5.11 us (9%)
  local copies, waits for them, and re-layouts  4.29 us (7%)
  other arithmetic  4.08 us (7%)
  between operations  1.54 us (3%)
    ppermute x7, waiting for transfers between devices, passed_along(): lax.ppermute(value, axis, [(i, (i + by) % length) for i in range(length)])  25.6 us
    dot_general x2, matrix products, leaf_solve(): jnp.einsum('nij,njr->nir', leaf_inverse[top_row:top_row + LEVEL_ROWS], re...  7.14 us
    dot_general x4, matrix products, node_solve(): jnp.dot(inverse_node, residual, preferred_element_type=jnp.float32)  7.03 us
    ppermute x7, starting transfers between devices, passed_along(): lax.ppermute(value, axis, [(i, (i + by) % length) for i in range(length)])  5.11 us
    gather x2, local copies, waits for them, and re-layouts, leaf_solve(): picked = jnp.take(solved, block_pattern[low_row:top_row], axis=0)  2.69 us
    dot_general x4, matrix products, node_solve(): jnp.dot(factor_node[1], upper_in, preferred_element_type=jnp.float32)  2.63 us
    dot_general x1, matrix products, leaf_solve(): jnp.einsum('nij,njr->nir', leaf_inverse[:LEVEL_ROWS], rhs_piece[:LEVEL_RO...  1.5 us
    concatenate x2, other arithmetic, leaf_solve(): solved = jnp.concatenate([solved, fresh_rows], axis=0)  1.36 us
  transfers between devices with their start and end apart: 7, of which 6 were waited for; matrix products, arithmetic and copies ran while one was open for 4% of the time, Pallas kernels for 0%

commit v1 on v0

v1 whole, which is shorter than its diff:
```python
import functools

import jax
import jax.numpy as jnp
from jax import lax
from jax.experimental import pallas as pl
from jax.experimental.pallas import tpu as pltpu
from jax.sharding import PartitionSpec as P

LEVEL_ROWS = 4
LEAF_LEVELS = 3
F32 = jnp.float32
BF16 = jnp.bfloat16

VMEM = pl.BlockSpec(memory_space=pltpu.VMEM)
HBM = pl.BlockSpec(memory_space=pltpu.HBM)
SMEM = pl.BlockSpec(memory_space=pltpu.SMEM)


def passed_along(value, axis, by):
    length = lax.axis_size(axis)
    return lax.ppermute(value, axis, [(i, (i + by) % length) for i in range(length)])


def mm(a, b):
    return jnp.dot(a, b, preferred_element_type=F32)


def leaf_row(factor, solved, pattern, row, coupled, rhs, inverse):
    total = rhs.astype(F32)
    for k in range(coupled):
        total = total - mm(factor[k], solved[pattern[row, k]])
    return mm(inverse, total.astype(BF16)).astype(BF16)


def edge_kernel(pattern, link, rhs, inverse, factor, solved, edge, rhs_v, inv_v, fac_v, top_fac, sem):
    coupled = factor.shape[1]
    n = LEVEL_ROWS
    low = 2 * n
    top = link[0]

    def load(src, dst, slot):
        copy = pltpu.make_async_copy(src, dst, sem.at[slot])
        copy.start()
        return copy

    first_inv = load(inverse.at[pl.ds(0, n)], inv_v.at[pl.ds(0, n)], 0)
    first_rhs = load(rhs.at[pl.ds(0, n)], rhs_v.at[pl.ds(0, n)], 1)
    rows = []
    for r in range(n):
        rows.append(
            (
                load(factor.at[r], fac_v.at[r], 2 + 3 * r),
                load(rhs.at[n + r], rhs_v.at[n + r], 3 + 3 * r),
                load(inverse.at[n + r], inv_v.at[n + r], 4 + 3 * r),
            )
        )
    base = 2 + 3 * n
    last = (
        load(factor.at[top - n], top_fac, base),
        load(rhs.at[top], rhs_v.at[low], base + 1),
        load(inverse.at[top], inv_v.at[low], base + 2),
    )
    first_inv.wait()
    first_rhs.wait()
    for r in range(n):
        solved[r] = mm(inv_v[r], rhs_v[r]).astype(BF16)
    for r in range(n):
        for copy in rows[r]:
            copy.wait()
        solved[n + r] = leaf_row(
            fac_v[r], solved, pattern, r, coupled, rhs_v[n + r], inv_v[n + r]
        )
    for copy in last:
        copy.wait()
    edge[...] = leaf_row(top_fac, solved, pattern, top - n, coupled, rhs_v[low], inv_v[low])


def edge_call(pattern, link, rhs, inverse, factor):
    n = LEVEL_ROWS
    coupled, block = factor.shape[1], factor.shape[2]
    loads = rhs.shape[-1]
    return pl.pallas_call(
        edge_kernel,
        out_shape=(
            jax.ShapeDtypeStruct((2 * n, block, loads), BF16),
            jax.ShapeDtypeStruct((block, loads), BF16),
        ),
        in_specs=[SMEM, SMEM, HBM, HBM, HBM],
        out_specs=(VMEM, VMEM),
        scratch_shapes=[
            pltpu.VMEM((2 * n + 1, block, loads), BF16),
            pltpu.VMEM((2 * n + 1, block, block), BF16),
            pltpu.VMEM((n, coupled, block, block), BF16),
            pltpu.VMEM((coupled, block, block), BF16),
            pltpu.SemaphoreType.DMA((5 + 3 * n,)),
        ],
        compiler_params=pltpu.CompilerParams(vmem_limit_bytes=16 << 20),
        name="leaf_edge",
    )(pattern, link, rhs, inverse, factor)


def rest_kernel(pattern, rhs, inverse, factor, low, solved, rhs_v, inv_v, fac_v, top, sem):
    coupled = factor.shape[1]
    n = LEVEL_ROWS

    def start(src, dst, slot):
        copy = pltpu.make_async_copy(src, dst, sem.at[slot])
        copy.start()
        return copy

    rhs_in = start(rhs.at[pl.ds(2 * n, n)], rhs_v, 0)
    inv_in = start(inverse.at[pl.ds(2 * n, n)], inv_v, 1)
    fac_in = [start(factor.at[n + r], fac_v.at[r], 3 + r) for r in range(n)]
    low_out = start(low, solved.at[pl.ds(0, 2 * n)], 2)
    rhs_in.wait()
    inv_in.wait()
    for r in range(n):
        fac_in[r].wait()
        top[r] = leaf_row(fac_v[r], low, pattern, n + r, coupled, rhs_v[r], inv_v[r])
    start(top, solved.at[pl.ds(2 * n, n)], 0).wait()
    low_out.wait()


def rest_call(pattern, rhs, inverse, factor, low):
    n = LEVEL_ROWS
    coupled, block = factor.shape[1], factor.shape[2]
    loads = rhs.shape[-1]
    flops = 2 * n * (coupled + 1) * block * block * loads
    return pl.pallas_call(
        rest_kernel,
        out_shape=jax.ShapeDtypeStruct((LEAF_LEVELS * n, block, loads), BF16),
        in_specs=[SMEM, HBM, HBM, HBM, VMEM],
        out_specs=HBM,
        scratch_shapes=[
            pltpu.VMEM((n, block, loads), BF16),
            pltpu.VMEM((n, block, block), BF16),
            pltpu.VMEM((n, coupled, block, block), BF16),
            pltpu.VMEM((n, block, loads), BF16),
            pltpu.SemaphoreType.DMA((3 + n,)),
        ],
        cost_estimate=pl.CostEstimate(
            flops=flops, bytes_accessed=36 * block * block * 2, transcendentals=0
        ),
        compiler_params=pltpu.CompilerParams(vmem_limit_bytes=16 << 20),
        name="leaf_rest",
    )(pattern, rhs, inverse, factor, low)


def fold_kernel(rhs, inverse, factor, lower_mat, upper_mat, const):
    for h in range(rhs.shape[0]):
        inv = inverse[h, 0]
        lower_mat[h] = mm(inv, factor[h, 0, 0]).astype(BF16)
        upper_mat[h] = mm(inv, factor[h, 0, 1]).astype(BF16)
        const[h] = mm(inv, rhs[h, 0])


def fold_call(rhs, inverse, factor):
    depth, _, block, loads = rhs.shape
    return pl.pallas_call(
        fold_kernel,
        out_shape=(
            jax.ShapeDtypeStruct((depth, block, block), BF16),
            jax.ShapeDtypeStruct((depth, block, block), BF16),
            jax.ShapeDtypeStruct((depth, block, loads), F32),
        ),
        in_specs=[VMEM, VMEM, VMEM],
        out_specs=(VMEM, VMEM, VMEM),
        cost_estimate=pl.CostEstimate(
            flops=6 * depth * block * block * loads,
            bytes_accessed=8 * depth * block * block * 2,
            transcendentals=0,
        ),
        compiler_params=pltpu.CompilerParams(vmem_limit_bytes=16 << 20),
        name="fold",
    )(rhs, inverse, factor)


def node_kernel(h, lower, upper, lower_mat, upper_mat, const, out):
    total = const[h] - mm(upper_mat[h], upper[...]) - mm(lower_mat[h], lower[...])
    out[...] = total.astype(BF16)


def node_call(h, lower, upper, lower_mat, upper_mat, const):
    return pl.pallas_call(
        functools.partial(node_kernel, h),
        out_shape=jax.ShapeDtypeStruct(lower.shape, BF16),
        in_specs=[VMEM] * 5,
        out_specs=VMEM,
        compiler_params=pltpu.CompilerParams(vmem_limit_bytes=8 << 20),
        name=f"node{h}",
    )(lower, upper, lower_mat, upper_mat, const)


def shards(
    leaf_rhs,
    separator_rhs,
    leaf_inverse,
    leaf_factor,
    separator_inverse,
    separator_factor,
    block_pattern,
    link_row,
):
    low, edge = edge_call(block_pattern, link_row, leaf_rhs, leaf_inverse, leaf_factor)
    lower = passed_along(edge, "rows", 1)
    solved = rest_call(block_pattern, leaf_rhs, leaf_inverse, leaf_factor, low)
    mats = fold_call(separator_rhs, separator_inverse, separator_factor)
    block = node_call(0, lower, edge, *mats)
    levels = [block]
    for height in range(1, separator_rhs.shape[0]):
        stride = 2 ** (height - 1)
        lower = passed_along(block, "rows", stride)
        upper = passed_along(block, "rows", -stride)
        block = node_call(height, lower, upper, *mats)
        levels.append(block)
    return solved, jnp.stack(levels, axis=0)[:, None]


def solution(mesh):
    placed = (
        P("rows", None, None),
        P(None, "rows", None, None),
        P(("draws", "rows"), None, None),
        P(("draws", "rows"), None, None, None),
        P(None, ("draws", "rows"), None, None),
        P(None, ("draws", "rows"), None, None, None),
        P("rows", None),
        P("rows"),
    )
    return jax.shard_map(
        shards,
        mesh=mesh,
        in_specs=placed,
        out_specs=(P(("draws", "rows"), None, None), P(None, ("draws", "rows"), None, None)),
        check_vma=False,
    )
```

time: 59.3 us -> 46.8 us (0.79)
  matrix products: 18.3 us -> 0 us
  waiting for transfers between devices: 25.6 us -> 14.2 us
  Pallas kernels: 0 us -> 10.7 us
  starting transfers between devices: 5.11 us -> 13.6 us
  other arithmetic: 4.08 us -> 0.86 us
  local copies, waits for them, and re-layouts: 4.29 us -> 5.78 us
    dot_general x11 -> x0, matrix products: 18.3 us -> none  [the longest x2 7.14 us: leaf_solve(): jnp.einsum('nij,njr->nir', leaf_inverse[top_row:top_row + LEVEL_ROWS], re...]
    ppermute x7, waiting for transfers between devices: 25.6 us -> 14.2 us  [passed_along(): lax.ppermute(value, axis, [(i, (i + by) % length) for i in range(length)])]
    pallas_call x0 -> x7, Pallas kernels: none -> 10.7 us  [the longest x1 5.53 us: edge_call(): pl.pallas_call(edge_kernel, out_shape=(jax.ShapeDtypeStruct((2 * n, block...]
    ppermute x7, starting transfers between devices: 5.11 us -> 13.6 us  [passed_along(): lax.ppermute(value, axis, [(i, (i + by) % length) for i in range(length)])]
    unnamed x7 -> x19, local copies, waits for them, and re-layouts: 1.02 us -> 5.78 us
    gather x2 -> x0, local copies, waits for them, and re-layouts: 2.69 us -> none  [leaf_solve(): picked = jnp.take(solved, block_pattern[low_row:top_row], axis=0)]
    concatenate x2 -> x0, other arithmetic: 1.36 us -> none  [leaf_solve(): solved = jnp.concatenate([solved, fresh_rows], axis=0)]
    broadcast_in_dim x1 -> x0, other arithmetic: 1.04 us -> none  [level_solve(): return jnp.stack(levels, axis=0)[:, None]]
  transfers between devices with their start and end apart: 7 -> 7, of which waited for: 6 -> 4; matrix products, arithmetic and copies ran while one was open for 4% -> 0% of each run, Pallas kernels for 0% -> 9%
where the time goes in v1:
time: 46.8 us; the launch traced here: 46.5 us
  waiting for transfers between devices  14.2 us (30%)
  starting transfers between devices  13.6 us (29%)
  Pallas kernels  10.7 us (23%)
  local copies, waits for them, and re-layouts  5.78 us (12%)
  between operations  1.38 us (3%)
  other arithmetic  0.86 us (2%)
    ppermute x7, waiting for transfers between devices, passed_along(): lax.ppermute(value, axis, [(i, (i + by) % length) for i in range(length)])  14.2 us
    ppermute x7, starting transfers between devices, passed_along(): lax.ppermute(value, axis, [(i, (i + by) % length) for i in range(length)])  13.6 us
    unnamed x19, local copies, waits for them, and re-layouts  5.78 us
    pallas_call x1, Pallas kernels, edge_call(): pl.pallas_call(edge_kernel, out_shape=(jax.ShapeDtypeStruct((2 * n, block...  5.53 us
    pallas_call x1, Pallas kernels, rest_call(): pl.pallas_call(rest_kernel, out_shape=jax.ShapeDtypeStruct((LEAF_LEVELS *...  3.66 us
  transfers between devices with their start and end apart: 7, of which 4 were waited for; matrix products, arithmetic and copies ran while one was open for 0% of the time, Pallas kernels for 9%

profile of v1, /device:TPU:0, one launch (start us, length us, event | category | flops | bytes accessed | tf_op | source)
XLA Modules:
  0.0 46.5 jit_solution(15378277452754503084)
XLA Ops:
  0.6 0.8 %copy.11.pattern = s32[8,4]{1,0:T(8,128)S(1)} copy(s32[8,4]{0,1:T(4,128)} %param.14) | data formatting | bytes 256 | tf_op args[6]
  2.0 0.0 copy-start
  2.0 2.2 %copy-done = bf16[8,4,256,256]{3,2,1,0:T(8,128)(2,1)S(1)} copy-done((bf16[8,4,256,256]{3,2,1,0:T(8,128)(2,1)S(1)}, bf16[8,4,256,256]{3,2,1,0:T(8,128)(2,1)}, u32[]{:S(2)}) %copy-start) | copy-done | bytes 4194328
  4.2 1.4 %copy-done.2 = bf16[12,256,256]{2,1,0:T(8,128)(2,1)S(1)} copy-done((bf16[12,256,256]{2,1,0:T(8,128)(2,1)S(1)}, bf16[12,256,256]{2,1,0:T(8,128)(2,1)}, u32[]{:S(2)}) %copy-start.2) | copy-done | bytes 1572888
  5.6 1.4 %copy-done.4 = bf16[12,256,256]{2,1,0:T(8,128)(2,1)S(1)} copy-done((bf16[12,256,256]{2,1,0:T(8,128)(2,1)S(1)}, bf16[12,256,256]{2,1,0:T(8,128)(2,1)}, u32[]{:S(2)}) %copy-start.4) | copy-done | bytes 1572888
  7.1 5.5 %leaf_edge.1 = (bf16[8,256,256]{2,1,0:T(8,128)(2,1)S(1)}, bf16[256,256]{1,0:T(8,128)(2,1)S(1)}) custom-call(s32[8,4]{1,0:T(8,128)S(1)} %copy.11.pattern, s32[1]{0:T(128)S(6)} %copy.13.link, bf16[12,256,256]{2,1,0:T(8,128)(2,1)S(1)} %copy-done.2, bf16[12,256,256]{2,1,0:T(8,128)(2,1)S(1)} %copy-done.4, bf16[8,4,256,256]{3,2,1,0:T(8,128)(2,1)S(1)} %copy-done), custom_call_target="tpu_custom_call" | custom-call | tf_op jit(solution)/shard_map/leaf_edge/pallas_call | solution.py:83
  12.6 0.5 %collective-permute-start = (bf16[256,256]{1,0:T(8,128)(2,1)S(1)}, bf16[256,256]{1,0:T(8,128)(2,1)S(1)}, u32[]{:S(2)}, u32[]{:S(2)}) collective-permute-start(bf16[256,256]{1,0:T(8,128)(2,1)S(1)} %get-tuple-element.8.upper), channel_id=1, source_target_pairs={{0,1},{1,2},{2,3},{3,4},{4,5},{5,6},{6,7},{7,8},{8,9},{9,10},{10,1... | collective-permute-start | bytes 393224 | tf_op jit(solution)/shard_map/ppermute | solution.py:22
  13.1 0.6 %fold.1 = (bf16[4,256,256]{2,1,0:T(8,128)(2,1)S(1)}, bf16[4,256,256]{2,1,0:T(8,128)(2,1)S(1)}, f32[4,256,256]{2,1,0:T(8,128)S(1)}) custom-call(bf16[4,1,256,256]{3,2,1,0:T(8,128)(2,1)S(1)} %copy-done.7, bf16[4,1,256,256]{3,2,1,0:T(8,128)(2,1)S(1)} %copy-done.8, bf16[4,1,2,256,256]{4,3,2,1,0:T(8,128)(2,1)S(1)} %copy-done.6), custom_call_target="tpu_custom_call" | custom-call | flops 402653184 | bytes 4194304 | tf_op jit(solution)/shard_map/fold/pallas_call | solution.py:160
  13.7 7.1 %collective-permute-done.lower = bf16[256,256]{1,0:T(8,128)(2,1)S(1)} collective-permute-done((bf16[256,256]{1,0:T(8,128)(2,1)S(1)}, bf16[256,256]{1,0:T(8,128)(2,1)S(1)}, u32[]{:S(2)}, u32[]{:S(2)}) %collective-permute-start) | collective-permute-done | bytes 131104 | tf_op jit(solution)/shard_map/ppermute | solution.py:22
  20.7 0.2 node0.1
  21.0 0.1 collective-permute-start.1
  21.0 4.4 %collective-permute-start.2 = (bf16[256,256]{1,0:T(8,128)(2,1)S(1)}, bf16[256,256]{1,0:T(8,128)(2,1)S(1)}, u32[]{:S(2)}, u32[]{:S(2)}) collective-permute-start(bf16[256,256]{1,0:T(8,128)(2,1)S(1)} %node0.1), channel_id=1, source_target_pairs={{0,15},{1,0},{2,1},{3,2},{4,3},{5,4},{6,5},{7,6},{8,7},{9,8},{10,9... | collective-permute-start | bytes 393224 | tf_op jit(solution)/shard_map/ppermute | solution.py:22
  25.5 2.6 %collective-permute-done.1.lower = bf16[256,256]{1,0:T(8,128)(2,1)S(1)} collective-permute-done((bf16[256,256]{1,0:T(8,128)(2,1)S(1)}, bf16[256,256]{1,0:T(8,128)(2,1)S(1)}, u32[]{:S(2)}, u32[]{:S(2)}) %collective-permute-start.1) | collective-permute-done | bytes 131104 | tf_op jit(solution)/shard_map/ppermute | solution.py:22
  28.1 0.2 node1.1
  28.4 0.1 collective-permute-start.3
  28.4 4.7 %collective-permute-start.4 = (bf16[256,256]{1,0:T(8,128)(2,1)S(1)}, bf16[256,256]{1,0:T(8,128)(2,1)S(1)}, u32[]{:S(2)}, u32[]{:S(2)}) collective-permute-start(bf16[256,256]{1,0:T(8,128)(2,1)S(1)} %node1.1), channel_id=1, source_target_pairs={{0,14},{1,15},{2,0},{3,1},{4,2},{5,3},{6,4},{7,5},{8,6},{9,7},{10,... | collective-permute-start | bytes 393224 | tf_op jit(solution)/shard_map/ppermute | solution.py:22
  33.1 3.8 %collective-permute-done.3.lower = bf16[256,256]{1,0:T(8,128)(2,1)S(1)} collective-permute-done((bf16[256,256]{1,0:T(8,128)(2,1)S(1)}, bf16[256,256]{1,0:T(8,128)(2,1)S(1)}, u32[]{:S(2)}, u32[]{:S(2)}) %collective-permute-start.3) | collective-permute-done | bytes 131104 | tf_op jit(solution)/shard_map/ppermute | solution.py:22
  36.9 0.2 node2.1
  37.2 0.1 collective-permute-start.5
  37.2 3.8 %collective-permute-start.6 = (bf16[256,256]{1,0:T(8,128)(2,1)S(1)}, bf16[256,256]{1,0:T(8,128)(2,1)S(1)}, u32[]{:S(2)}, u32[]{:S(2)}) collective-permute-start(bf16[256,256]{1,0:T(8,128)(2,1)S(1)} %node2.1), channel_id=1, source_target_pairs={{0,12},{1,13},{2,14},{3,15},{4,0},{5,1},{6,2},{7,3},{8,4},{9,5},{1... | collective-permute-start | bytes 393224 | tf_op jit(solution)/shard_map/ppermute | solution.py:22
  41.1 3.7 %leaf_rest.1 = bf16[12,256,256]{2,1,0:T(8,128)(2,1)} custom-call(s32[8,4]{1,0:T(8,128)S(1)} %copy.11.pattern, bf16[12,256,256]{2,1,0:T(8,128)(2,1)S(1)} %copy-done.3, bf16[12,256,256]{2,1,0:T(8,128)(2,1)S(1)} %copy-done.5, bf16[8,4,256,256]{3,2,1,0:T(8,128)(2,1)S(1)} %copy-done.1, bf16[8,256,256]{2,1,0:T(8,128)(2,1)S(1)} %get-tuple-element.7.low), custom_call_target="tpu_custom_call" | custom-call | flops 671088640 | bytes 4718592 | tf_op jit(solution)/shard_map/leaf_rest/pallas_call | solution.py:130
  44.7 0.7 %collective-permute-done.5.lower = bf16[256,256]{1,0:T(8,128)(2,1)S(1)} collective-permute-done((bf16[256,256]{1,0:T(8,128)(2,1)S(1)}, bf16[256,256]{1,0:T(8,128)(2,1)S(1)}, u32[]{:S(2)}, u32[]{:S(2)}) %collective-permute-start.5) | collective-permute-done | bytes 131104 | tf_op jit(solution)/shard_map/ppermute | solution.py:22
  45.4 0.2 node3.1
  45.7 0.9 %maximum_bitcast_fusion = bf16[4,1,256,256]{3,2,1,0:T(8,128)(2,1)} fusion(bf16[1,256,256]{2,1,0:T(8,128)(2,1)S(1)} %bitcast.11, bf16[1,256,256]{2,1,0:T(8,128)(2,1)S(1)} %bitcast.10, bf16[1,256,256]{2,1,0:T(8,128)(2,1)S(1)} %bitcast.9, bf16[1,256,256]{2,1,0:T(8,128)(2,1)S(1)} %bitcast.8), kind=kLoop, calls=%fused_computation | loop fusion | flops 786432 | bytes 1048576
  (17 shorter events, 0.0 us)
Async XLA Ops:
  2.0 2.2 %copy-start = (bf16[8,4,256,256]{3,2,1,0:T(8,128)(2,1)S(1)}, bf16[8,4,256,256]{3,2,1,0:T(8,128)(2,1)}, u32[]{:S(2)}) copy-start(bf16[8,4,256,256]{3,2,1,0:T(8,128)(2,1)} %factor.4) | copy-start | bytes 12582916
  4.2 1.4 %copy-start.2 = (bf16[12,256,256]{2,1,0:T(8,128)(2,1)S(1)}, bf16[12,256,256]{2,1,0:T(8,128)(2,1)}, u32[]{:S(2)}) copy-start(bf16[12,256,256]{2,1,0:T(8,128)(2,1)} %rhs.4) | copy-start | bytes 4718596
  5.6 1.4 %copy-start.4 = (bf16[12,256,256]{2,1,0:T(8,128)(2,1)S(1)}, bf16[12,256,256]{2,1,0:T(8,128)(2,1)}, u32[]{:S(2)}) copy-start(bf16[12,256,256]{2,1,0:T(8,128)(2,1)} %inverse.4) | copy-start | bytes 4718596
  7.0 6.1 %copy-start.6 = (bf16[4,1,2,256,256]{4,3,2,1,0:T(8,128)(2,1)S(1)}, bf16[4,1,2,256,256]{4,3,2,1,0:T(8,128)(2,1)}, u32[]{:S(2)}) copy-start(bf16[4,1,2,256,256]{4,3,2,1,0:T(8,128)(2,1)} %factor.5) | copy-start | bytes 3145732
  7.0 6.1 %copy-start.7 = (bf16[4,1,256,256]{3,2,1,0:T(8,128)(2,1)S(1)}, bf16[4,1,256,256]{3,2,1,0:T(8,128)(2,1)}, u32[]{:S(2)}) copy-start(bf16[4,1,256,256]{3,2,1,0:T(8,128)(2,1)} %rhs.5) | copy-start | bytes 1572868
  7.0 6.1 %copy-start.8 = (bf16[4,1,256,256]{3,2,1,0:T(8,128)(2,1)S(1)}, bf16[4,1,256,256]{3,2,1,0:T(8,128)(2,1)}, u32[]{:S(2)}) copy-start(bf16[4,1,256,256]{3,2,1,0:T(8,128)(2,1)} %inverse.5) | copy-start | bytes 1572868
  12.6 8.1 %collective-permute-start = (bf16[256,256]{1,0:T(8,128)(2,1)S(1)}, bf16[256,256]{1,0:T(8,128)(2,1)S(1)}, u32[]{:S(2)}, u32[]{:S(2)}) collective-permute-start(bf16[256,256]{1,0:T(8,128)(2,1)S(1)} %get-tuple-element.8.upper), channel_id=1, source_target_pairs={{0,1},{1,2},{2,3},{3,4},{4,5},{5,6},{6,7},{7,8},{8,9},{9,10},{10,1... | collective-permute-start | bytes 393224 | tf_op jit(solution)/shard_map/ppermute | solution.py:22
  20.7 20.3 %copy-start.3 = (bf16[12,256,256]{2,1,0:T(8,128)(2,1)S(1)}, bf16[12,256,256]{2,1,0:T(8,128)(2,1)}, u32[]{:S(2)}) copy-start(bf16[12,256,256]{2,1,0:T(8,128)(2,1)} %rhs.4) | copy-start | bytes 4718596
  20.7 20.3 %copy-start.5 = (bf16[12,256,256]{2,1,0:T(8,128)(2,1)S(1)}, bf16[12,256,256]{2,1,0:T(8,128)(2,1)}, u32[]{:S(2)}) copy-start(bf16[12,256,256]{2,1,0:T(8,128)(2,1)} %inverse.4) | copy-start | bytes 4718596
  21.0 7.1 %collective-permute-start.1 = (bf16[256,256]{1,0:T(8,128)(2,1)S(1)}, bf16[256,256]{1,0:T(8,128)(2,1)S(1)}, u32[]{:S(2)}, u32[]{:S(2)}) collective-permute-start(bf16[256,256]{1,0:T(8,128)(2,1)S(1)} %node0.1), channel_id=1, source_target_pairs={{0,1},{1,2},{2,3},{3,4},{4,5},{5,6},{6,7},{7,8},{8,9},{9,10},{10,1... | collective-permute-start | bytes 393224 | tf_op jit(solution)/shard_map/ppermute | solution.py:22
  21.0 7.1 %collective-permute-start.2 = (bf16[256,256]{1,0:T(8,128)(2,1)S(1)}, bf16[256,256]{1,0:T(8,128)(2,1)S(1)}, u32[]{:S(2)}, u32[]{:S(2)}) collective-permute-start(bf16[256,256]{1,0:T(8,128)(2,1)S(1)} %node0.1), channel_id=1, source_target_pairs={{0,15},{1,0},{2,1},{3,2},{4,3},{5,4},{6,5},{7,6},{8,7},{9,8},{10,9... | collective-permute-start | bytes 393224 | tf_op jit(solution)/shard_map/ppermute | solution.py:22
  28.1 12.9 %copy-start.1 = (bf16[8,4,256,256]{3,2,1,0:T(8,128)(2,1)S(1)}, bf16[8,4,256,256]{3,2,1,0:T(8,128)(2,1)}, u32[]{:S(2)}) copy-start(bf16[8,4,256,256]{3,2,1,0:T(8,128)(2,1)} %factor.4) | copy-start | bytes 12582916
  28.4 8.6 %collective-permute-start.3 = (bf16[256,256]{1,0:T(8,128)(2,1)S(1)}, bf16[256,256]{1,0:T(8,128)(2,1)S(1)}, u32[]{:S(2)}, u32[]{:S(2)}) collective-permute-start(bf16[256,256]{1,0:T(8,128)(2,1)S(1)} %node1.1), channel_id=1, source_target_pairs={{0,2},{1,3},{2,4},{3,5},{4,6},{5,7},{6,8},{7,9},{8,10},{9,11},{10,... | collective-permute-start | bytes 393224 | tf_op jit(solution)/shard_map/ppermute | solution.py:22
  28.4 8.5 %collective-permute-start.4 = (bf16[256,256]{1,0:T(8,128)(2,1)S(1)}, bf16[256,256]{1,0:T(8,128)(2,1)S(1)}, u32[]{:S(2)}, u32[]{:S(2)}) collective-permute-start(bf16[256,256]{1,0:T(8,128)(2,1)S(1)} %node1.1), channel_id=1, source_target_pairs={{0,14},{1,15},{2,0},{3,1},{4,2},{5,3},{6,4},{7,5},{8,6},{9,7},{10,... | collective-permute-start | bytes 393224 | tf_op jit(solution)/shard_map/ppermute | solution.py:22
  37.2 8.3 %collective-permute-start.5 = (bf16[256,256]{1,0:T(8,128)(2,1)S(1)}, bf16[256,256]{1,0:T(8,128)(2,1)S(1)}, u32[]{:S(2)}, u32[]{:S(2)}) collective-permute-start(bf16[256,256]{1,0:T(8,128)(2,1)S(1)} %node2.1), channel_id=1, source_target_pairs={{0,4},{1,5},{2,6},{3,7},{4,8},{5,9},{6,10},{7,11},{8,12},{9,13},{1... | collective-permute-start | bytes 393224 | tf_op jit(solution)/shard_map/ppermute | solution.py:22
  37.2 8.2 %collective-permute-start.6 = (bf16[256,256]{1,0:T(8,128)(2,1)S(1)}, bf16[256,256]{1,0:T(8,128)(2,1)S(1)}, u32[]{:S(2)}, u32[]{:S(2)}) collective-permute-start(bf16[256,256]{1,0:T(8,128)(2,1)S(1)} %node2.1), channel_id=1, source_target_pairs={{0,12},{1,13},{2,14},{3,15},{4,0},{5,1},{6,2},{7,3},{8,4},{9,5},{1... | collective-permute-start | bytes 393224 | tf_op jit(solution)/shard_map/ppermute | solution.py:22

commit v2 on v1

v2 whole, which is shorter than its diff:
```python
import functools

import jax
import jax.numpy as jnp
from jax import lax
from jax.experimental import pallas as pl
from jax.experimental.pallas import tpu as pltpu
from jax.sharding import PartitionSpec as P

LEVEL_ROWS = 4
LEAF_LEVELS = 3
F32 = jnp.float32
BF16 = jnp.bfloat16

SMEM = pl.BlockSpec(memory_space=pltpu.SMEM)
VMEM = pl.BlockSpec(memory_space=pltpu.VMEM)
HBM = pl.BlockSpec(memory_space=pltpu.HBM)


def passed_along(value, axis, by):
    length = lax.axis_size(axis)
    return lax.ppermute(value, axis, [(i, (i + by) % length) for i in range(length)])


def in_hbm(array):
    return pltpu.with_memory_space_constraint(array, pltpu.HBM)


def mm(a, b):
    return jnp.dot(a, b, preferred_element_type=F32)


def leaf_residual(factor, solved, pattern, row, rhs):
    coupled = factor.shape[0]
    wide = jnp.concatenate([factor[k] for k in range(coupled)], axis=1)
    tall = jnp.concatenate([solved[pattern[k, row]] for k in range(coupled)], axis=0)
    return (rhs.astype(F32) - mm(wide, tall)).astype(BF16)


def pair_swap(value, axis):
    length = lax.axis_size(axis)
    return lax.ppermute(value, axis, [(i, i ^ 1) for i in range(length)])


def border_swap(value, axis):
    length = lax.axis_size(axis)
    pairs = [(i, (i + (1 if i % 2 else -1)) % length) for i in range(length)]
    return lax.ppermute(value, axis, pairs)


def on_odd():
    return lax.rem(lax.axis_index("rows"), 2) == 1


def edge_kernel(
    columns, link, rhs, inverse, factor, node_rhs, node_inverse, node_factor,
    solved, edge, sent, lower_mat, upper_mat, const,
    pattern, rhs_v, inv_v, fac_v, top_fac, left, node_r, node_i, node_f, sem,
):
    n = LEVEL_ROWS
    low = 2 * n
    slots = iter(range(sem.shape[0]))

    def load(src, dst):
        copy = pltpu.make_async_copy(src, dst, sem.at[next(slots)])
        copy.start()
        return copy

    first_inv = load(inverse.at[pl.ds(0, n)], inv_v.at[pl.ds(0, n)])
    first_rhs = load(rhs.at[pl.ds(0, n)], rhs_v.at[pl.ds(0, n)])
    pattern_in = load(columns, pattern)
    next_rhs = load(rhs.at[pl.ds(n, n)], rhs_v.at[pl.ds(n, n)])
    next_fac = [load(factor.at[r], fac_v.at[r]) for r in range(n)]
    next_inv = load(inverse.at[pl.ds(n, n)], inv_v.at[pl.ds(n, n)])
    node_in = (
        load(node_inverse.at[0, 0], node_i),
        load(node_factor.at[0, 0], node_f),
        load(node_rhs.at[0, 0], node_r),
    )
    top = link[0]
    last = (
        load(factor.at[top - n], top_fac),
        load(rhs.at[top], rhs_v.at[low]),
        load(inverse.at[top], inv_v.at[low]),
    )
    first_inv.wait()
    first_rhs.wait()
    for r in range(n):
        solved[r] = mm(inv_v[r], rhs_v[r]).astype(BF16)
    pattern_in.wait()
    next_rhs.wait()
    for r in range(n):
        next_fac[r].wait()
        left[r] = leaf_residual(fac_v.at[r], solved, pattern, r, rhs_v[n + r])
    next_inv.wait()
    for r in range(n):
        solved[n + r] = mm(inv_v[n + r], left[r]).astype(BF16)
    for copy in node_in:
        copy.wait()
    lower_mat[...] = mm(node_i[...], node_f[0]).astype(BF16)
    upper_mat[...] = mm(node_i[...], node_f[1]).astype(BF16)
    const[...] = mm(node_i[...], node_r[...])
    for copy in last:
        copy.wait()
    residual = leaf_residual(top_fac, solved, pattern, top - n, rhs_v[low])
    edge_value = mm(inv_v[low], residual).astype(BF16)
    edge[...] = edge_value
    odd = on_odd()

    @pl.when(odd)
    def _():
        sent[...] = edge_value

    @pl.when(jnp.logical_not(odd))
    def _():
        sent[...] = (const[...] - mm(upper_mat[...], edge_value)).astype(BF16)


def edge_call(pattern, link, rhs, inverse, factor, node_rhs, node_inverse, node_factor):
    n = LEVEL_ROWS
    coupled, block = factor.shape[1], factor.shape[2]
    loads = rhs.shape[-1]
    return pl.pallas_call(
        edge_kernel,
        out_shape=(
            pltpu.VMEM((2 * n, block, loads), BF16),
            pltpu.VMEM((block, loads), BF16),
            pltpu.VMEM((block, loads), BF16),
            pltpu.VMEM((block, block), BF16),
            pltpu.VMEM((block, block), BF16),
            pltpu.VMEM((block, loads), F32),
        ),
        in_specs=[HBM, SMEM] + [HBM] * 6,
        out_specs=(VMEM,) * 6,
        scratch_shapes=[
            pltpu.SMEM(pattern.shape, jnp.int32),
            pltpu.VMEM((2 * n + 1, block, loads), BF16),
            pltpu.VMEM((2 * n + 1, block, block), BF16),
            pltpu.VMEM((n, coupled, block, block), BF16),
            pltpu.VMEM((coupled, block, block), BF16),
            pltpu.VMEM((n, block, loads), BF16),
            pltpu.VMEM((block, loads), BF16),
            pltpu.VMEM((block, block), BF16),
            pltpu.VMEM((2, block, block), BF16),
            pltpu.SemaphoreType.DMA((11 + n,)),
        ],
        compiler_params=pltpu.CompilerParams(vmem_limit_bytes=16 << 20),
        name="leaf_edge",
    )(
        in_hbm(pattern), link, in_hbm(rhs), in_hbm(inverse), in_hbm(factor),
        in_hbm(node_rhs), in_hbm(node_inverse), in_hbm(node_factor),
    )


def early_kernel(lower, upper, lower_mat, upper_mat, const, out):
    odd = on_odd()

    @pl.when(odd)
    def _():
        total = const[...] - mm(upper_mat[...], upper[...]) - mm(lower_mat[...], lower[...])
        out[...] = total.astype(BF16)

    @pl.when(jnp.logical_not(odd))
    def _():
        out[...] = lower_mat[...]


def late_kernel(part, lower, early, lower_mat, *rest):
    out = rest[-1]
    odd = on_odd()

    @pl.when(odd)
    def _():
        out[...] = early[...]

    @pl.when(jnp.logical_not(odd))
    def _():
        out[...] = (part[...].astype(F32) - mm(lower_mat[...], lower[...])).astype(BF16)


def level_one_kernel(inner, came_first, came_next, edge, lower_mat, upper_mat, const, out):
    odd = on_odd()

    @pl.when(odd)
    def _():
        upper = came_first[...].astype(F32) - mm(came_next[...], edge[...])
        total = const[0] - mm(lower_mat[0], inner[...]) - mm(upper_mat[0], upper.astype(BF16))
        out[...] = total.astype(BF16)

    @pl.when(jnp.logical_not(odd))
    def _():
        total = const[0] - mm(upper_mat[0], inner[...]) - mm(lower_mat[0], came_next[...])
        out[...] = total.astype(BF16)


def small_call(kernel, name, shape, *args):
    return pl.pallas_call(
        kernel,
        out_shape=pltpu.VMEM(shape, BF16),
        in_specs=[VMEM] * len(args),
        out_specs=VMEM,
        compiler_params=pltpu.CompilerParams(vmem_limit_bytes=8 << 20),
        name=name,
    )(*args)


def rest_kernel(columns, rhs, inverse, factor, low, top, pattern, rhs_v, inv_v, fac_v, left, sem):
    n = LEVEL_ROWS

    def load(src, dst, slot):
        copy = pltpu.make_async_copy(src, dst, sem.at[slot])
        copy.start()
        return copy

    pattern_in = load(columns, pattern, 0)
    rhs_in = load(rhs.at[pl.ds(2 * n, n)], rhs_v, 1)
    fac_in = [load(factor.at[n + r], fac_v.at[r], 3 + r) for r in range(n)]
    inv_in = load(inverse.at[pl.ds(2 * n, n)], inv_v, 2)
    pattern_in.wait()
    rhs_in.wait()
    for r in range(n):
        fac_in[r].wait()
        left[r] = leaf_residual(fac_v.at[r], low, pattern, n + r, rhs_v[r])
    inv_in.wait()
    for r in range(n):
        top[r] = mm(inv_v[r], left[r]).astype(BF16)


def rest_call(pattern, rhs, inverse, factor, low):
    n = LEVEL_ROWS
    coupled, block = factor.shape[1], factor.shape[2]
    loads = rhs.shape[-1]
    flops = 2 * n * (coupled + 1) * block * block * loads
    return pl.pallas_call(
        rest_kernel,
        out_shape=pltpu.VMEM((n, block, loads), BF16),
        in_specs=[HBM] * 4 + [VMEM],
        out_specs=VMEM,
        scratch_shapes=[
            pltpu.SMEM(pattern.shape, jnp.int32),
            pltpu.VMEM((n, block, loads), BF16),
            pltpu.VMEM((n, block, block), BF16),
            pltpu.VMEM((n, coupled, block, block), BF16),
            pltpu.VMEM((n, block, loads), BF16),
            pltpu.SemaphoreType.DMA((3 + n,)),
        ],
        compiler_params=pltpu.CompilerParams(vmem_limit_bytes=12 << 20),
        cost_estimate=pl.CostEstimate(
            flops=flops, bytes_accessed=36 * block * block * 2, transcendentals=0
        ),
        name="leaf_rest",
    )(in_hbm(pattern), in_hbm(rhs), in_hbm(inverse), in_hbm(factor), low)


def fold_kernel(rhs, inverse, factor, _, lower_mat, upper_mat, const):
    for h in range(1, rhs.shape[0]):
        inv = inverse[h, 0]
        lower_mat[h - 1] = mm(inv, factor[h, 0, 0]).astype(BF16)
        upper_mat[h - 1] = mm(inv, factor[h, 0, 1]).astype(BF16)
        const[h - 1] = mm(inv, rhs[h, 0])


def fold_call(rhs, inverse, factor, after):
    depth, _, block, loads = rhs.shape
    depth = depth - 1
    return pl.pallas_call(
        fold_kernel,
        out_shape=(
            pltpu.VMEM((depth, block, block), BF16),
            pltpu.VMEM((depth, block, block), BF16),
            pltpu.VMEM((depth, block, loads), F32),
        ),
        in_specs=[VMEM] * 4,
        out_specs=(VMEM, VMEM, VMEM),
        cost_estimate=pl.CostEstimate(
            flops=6 * depth * block * block * loads,
            bytes_accessed=8 * depth * block * block * 2,
            transcendentals=0,
        ),
        compiler_params=pltpu.CompilerParams(vmem_limit_bytes=16 << 20),
        name="fold",
    )(rhs, inverse, factor, after)


def node_kernel(h, lower, upper, lower_mat, upper_mat, const, out):
    total = const[h] - mm(upper_mat[h], upper[...]) - mm(lower_mat[h], lower[...])
    out[...] = total.astype(BF16)


def collect_kernel(low, top, *refs):
    *levels, solved, out, sem = refs
    copies = [
        pltpu.make_async_copy(level, out.at[h, 0], sem.at[h]) for h, level in enumerate(levels)
    ]
    n = low.shape[0]
    h = len(levels)
    copies.append(pltpu.make_async_copy(low, solved.at[pl.ds(0, n)], sem.at[h]))
    copies.append(pltpu.make_async_copy(top, solved.at[pl.ds(n, top.shape[0])], sem.at[h + 1]))
    for copy in copies:
        copy.start()
    for copy in copies:
        copy.wait()


def collect_call(low, top, levels, shape):
    rows = low.shape[0] + top.shape[0]
    return pl.pallas_call(
        collect_kernel,
        out_shape=(
            jax.ShapeDtypeStruct((rows,) + low.shape[1:], BF16),
            jax.ShapeDtypeStruct(shape, BF16),
        ),
        in_specs=[VMEM] * (2 + len(levels)),
        out_specs=(HBM, HBM),
        scratch_shapes=[pltpu.SemaphoreType.DMA((2 + len(levels),))],
        compiler_params=pltpu.CompilerParams(vmem_limit_bytes=4 << 20),
        cost_estimate=pl.CostEstimate(
            flops=0,
            bytes_accessed=(rows + len(levels)) * shape[2] * shape[3] * 4,
            transcendentals=0,
        ),
        name="collect",
    )(low, top, *levels)


def last_kernel(lower, upper, lower_mat, upper_mat, const, _, out, piece, sem):
    h = const.shape[0] - 1
    rows = const.shape[1] // 2
    copies = []
    for half in range(2):
        part = pl.ds(half * rows, rows)
        total = (
            const[h, part]
            - mm(upper_mat[h, part], upper[...])
            - mm(lower_mat[h, part], lower[...])
        )
        piece[part] = total.astype(BF16)
        copy = pltpu.make_async_copy(
            piece.at[part], out.at[out.shape[0] - 1, 0, part], sem.at[half]
        )
        copy.start()
        copies.append(copy)
    for copy in copies:
        copy.wait()


def last_call(lower, upper, lower_mat, upper_mat, const, collected):
    return pl.pallas_call(
        last_kernel,
        out_shape=jax.ShapeDtypeStruct(collected.shape, BF16),
        in_specs=[VMEM] * 5 + [HBM],
        out_specs=HBM,
        input_output_aliases={5: 0},
        scratch_shapes=[pltpu.VMEM(lower.shape, BF16), pltpu.SemaphoreType.DMA((2,))],
        compiler_params=pltpu.CompilerParams(vmem_limit_bytes=8 << 20),
        name="node_last",
    )(lower, upper, lower_mat, upper_mat, const, collected)


def shards(
    leaf_rhs,
    separator_rhs,
    leaf_inverse,
    leaf_factor,
    separator_inverse,
    separator_factor,
    block_pattern,
    link_row,
):
    columns = block_pattern.T
    low, edge, sent, lower_mat, upper_mat, const = edge_call(
        columns, link_row, leaf_rhs, leaf_inverse, leaf_factor,
        separator_rhs, separator_inverse, separator_factor,
    )
    shape = edge.shape
    edge_inner = pair_swap(edge, "rows")
    came_first = border_swap(sent, "rows")
    early = small_call(
        early_kernel, "level0_early", shape, edge_inner, edge, lower_mat, upper_mat, const
    )
    came_next = border_swap(early, "rows")
    top = rest_call(columns, leaf_rhs, leaf_inverse, leaf_factor, low)
    mats = fold_call(separator_rhs, separator_inverse, separator_factor, early)
    block = small_call(
        late_kernel, "level0_late", shape, sent, came_first, early, lower_mat, came_next, top, mats[2],
    )
    inner = pair_swap(block, "rows")
    levels = [block]
    block = small_call(
        level_one_kernel, "level1", shape, inner, came_first, came_next, edge, *mats
    )
    levels.append(block)
    depth = separator_rhs.shape[0]
    for height in range(2, depth):
        stride = 2 ** (height - 1)
        lower = passed_along(block, "rows", stride)
        upper = passed_along(block, "rows", -stride)
        if height < depth - 1:
            step = functools.partial(node_kernel, height - 1)
            block = small_call(step, f"level{height}", shape, lower, upper, *mats)
            levels.append(block)
    solved, collected = collect_call(low, top, levels, (depth, 1) + shape)
    return solved, last_call(lower, upper, *mats, collected)


def solution(mesh):
    placed = (
        P("rows", None, None),
        P(None, "rows", None, None),
        P(("draws", "rows"), None, None),
        P(("draws", "rows"), None, None, None),
        P(None, ("draws", "rows"), None, None),
        P(None, ("draws", "rows"), None, None, None),
        P("rows", None),
        P("rows"),
    )
    return jax.shard_map(
        shards,
        mesh=mesh,
        in_specs=placed,
        out_specs=(P(("draws", "rows"), None, None), P(None, ("draws", "rows"), None, None)),
        check_vma=False,
    )
```

time: 46.8 us -> 39.3 us (0.84)
  local copies, waits for them, and re-layouts: 5.78 us -> 0.01 us
  waiting for transfers between devices: 14.2 us -> 10 us
  starting transfers between devices: 13.6 us -> 16.2 us
  other arithmetic: 0.86 us -> 0 us
  Pallas kernels: 10.7 us -> 11.5 us
    ppermute x0 -> x4, starting transfers between devices: none -> 7.53 us  [the longest x2 7.13 us: border_swap(): return lax.ppermute(value, axis, pairs)]
    ppermute x7 -> x4, waiting for transfers between devices: 14.2 us -> 6.75 us  [passed_along(): lax.ppermute(value, axis, [(i, (i + by) % length) for i in range(length)])]
    unnamed x19 -> x6, local copies, waits for them, and re-layouts: 5.78 us -> 0.01 us
    ppermute x7 -> x4, starting transfers between devices: 13.6 us -> 8.64 us  [passed_along(): lax.ppermute(value, axis, [(i, (i + by) % length) for i in range(length)])]
    ppermute x0 -> x4, waiting for transfers between devices: none -> 3.27 us  [the longest x2 1.94 us: border_swap(): return lax.ppermute(value, axis, pairs)]
    unnamed x1 -> x0, other arithmetic: 0.86 us -> none
    pallas_call x7 -> x9, Pallas kernels: 10.7 us -> 11.5 us  [the longest x1 4.81 us: edge_call(): pl.pallas_call(edge_kernel, out_shape=(pltpu.VMEM((2 * n, block, loads),...]
  transfers between devices with their start and end apart: 7 -> 8, of which waited for: 4 -> 5; matrix products, arithmetic and copies ran while one was open for 0% -> 0% of each run, Pallas kernels for 9% -> 13%
where the time goes in v2:
time: 39.3 us; the launch traced here: 39.1 us
  starting transfers between devices  16.2 us (41%)
  Pallas kernels  11.5 us (29%)
  waiting for transfers between devices  10 us (25%)
  between operations  1.39 us (4%)
    ppermute x4, starting transfers between devices, passed_along(): lax.ppermute(value, axis, [(i, (i + by) % length) for i in range(length)])  8.64 us
    ppermute x2, starting transfers between devices, border_swap(): return lax.ppermute(value, axis, pairs)  7.13 us
    ppermute x4, waiting for transfers between devices, passed_along(): lax.ppermute(value, axis, [(i, (i + by) % length) for i in range(length)])  6.75 us
    pallas_call x1, Pallas kernels, edge_call(): pl.pallas_call(edge_kernel, out_shape=(pltpu.VMEM((2 * n, block, loads),...  4.81 us
    pallas_call x1, Pallas kernels, rest_call(): pl.pallas_call(rest_kernel, out_shape=pltpu.VMEM((n, block, loads), BF16)...  3.41 us
    ppermute x2, waiting for transfers between devices, border_swap(): return lax.ppermute(value, axis, pairs)  1.94 us
    ppermute x2, waiting for transfers between devices, pair_swap(): return lax.ppermute(value, axis, [(i, i ^ 1) for i in range(length)])  1.34 us
    pallas_call x1, Pallas kernels, collect_call(): pl.pallas_call(collect_kernel, out_shape=(jax.ShapeDtypeStruct((rows,) +...  1.31 us
  transfers between devices with their start and end apart: 8, of which 5 were waited for; matrix products, arithmetic and copies ran while one was open for 0% of the time, Pallas kernels for 13%

profile of v2, /device:TPU:0, one launch (start us, length us, event | category | flops | bytes accessed | tf_op | source)
XLA Modules:
  0.0 39.1 jit_solution(15484712641884732061)
XLA Ops:
  1.3 4.8 %leaf_edge.1 = (bf16[8,256,256]{2,1,0:T(8,128)(2,1)S(1)}, bf16[256,256]{1,0:T(8,128)(2,1)S(1)}, bf16[256,256]{1,0:T(8,128)(2,1)S(1)}, bf16[256,256]{1,0:T(8,128)...) custom-call(s32[4,8]{1,0:T(4,128)} %bitcast.1, s32[1]{0:T(128)S(6)} %copy.12.link, ...), custom_call_target="tpu_custom_call" | custom-call | tf_op jit(solution)/shard_map/leaf_edge/pallas_call | solution.py:123
  6.1 0.3 collective-permute-start.1
  6.4 5.9 %collective-permute-start = (bf16[256,256]{1,0:T(8,128)(2,1)S(1)}, bf16[256,256]{1,0:T(8,128)(2,1)S(1)}, u32[]{:S(2)}, u32[]{:S(2)}) collective-permute-start(bf16[256,256]{1,0:T(8,128)(2,1)S(1)} %get-tuple-element.14.part), channel_id=1, source_target_pairs={{0,15},{1,2},{2,1},{3,4},{4,3},{5,6},{6,5},{7,8},{8,7},{9,10},{10,... | collective-permute-start | bytes 393224 | tf_op jit(solution)/shard_map/ppermute | solution.py:48
  12.3 0.0 collective-permute-done.1.lower
  12.3 1.3 %collective-permute-start.2 = (bf16[256,256]{1,0:T(8,128)(2,1)S(1)}, bf16[256,256]{1,0:T(8,128)(2,1)S(1)}, u32[]{:S(2)}, u32[]{:S(2)}) collective-permute-start(bf16[256,256]{1,0:T(8,128)(2,1)S(1)} %level0_early.1._.early), channel_id=1, source_target_pairs={{0,15},{1,2},{2,1},{3,4},{4,3},{5,6},{6,5},{7,8},{8,7},{9,10},{10,... | collective-permute-start | bytes 393224 | tf_op jit(solution)/shard_map/ppermute | solution.py:48
  13.6 3.4 %leaf_rest.1.rest_1_.top = bf16[4,256,256]{2,1,0:T(8,128)(2,1)S(1)} custom-call(s32[4,8]{1,0:T(4,128)} %bitcast.2, bf16[12,256,256]{2,1,0:T(8,128)(2,1)} %rhs.4, bf16[12,256,256]{2,1,0:T(8,128)(2,1)} %inverse.4, bf16[8,4,256,256]{3,2,1,0:T(8,128)(2,1)} %factor.4, bf16[8,256,256]{2,1,0:T(8,128)(2,1)S(1)} %get-tuple-element.13.low), custom_call_target="tpu_custom_call" | custom-call | flops 671088640 | bytes 4718592 | tf_op jit(solution)/shard_map/leaf_rest/pallas_call | solution.py:234
  17.0 0.5 %fold.1 = (bf16[3,256,256]{2,1,0:T(8,128)(2,1)S(1)}, bf16[3,256,256]{2,1,0:T(8,128)(2,1)S(1)}, f32[3,256,256]{2,1,0:T(8,128)S(1)}) custom-call(bf16[4,1,256,256]{3,2,1,0:T(8,128)(2,1)S(1)} %copy-done.1, bf16[4,1,256,256]{3,2,1,0:T(8,128)(2,1)S(1)} %copy-done.2, bf16[4,1,2,256,256]{4,3,2,1,0:T(8,128)(2,1)S(1)} %copy-done, ...), custom_call_target="tpu_custom_call" | custom-call | flops 301989888 | bytes 3145728 | tf_op jit(solution)/shard_map/fold/pallas_call | solution.py:266
  17.5 0.0 collective-permute-done.lower.came_first
  17.5 1.9 %collective-permute-done.2.rest_0_.came_next = bf16[256,256]{1,0:T(8,128)(2,1)S(1)} collective-permute-done((bf16[256,256]{1,0:T(8,128)(2,1)S(1)}, bf16[256,256]{1,0:T(8,128)(2,1)S(1)}, u32[]{:S(2)}, u32[]{:S(2)}) %collective-permute-start.2) | collective-permute-done | bytes 131104 | tf_op jit(solution)/shard_map/ppermute | solution.py:48
  19.5 0.2 level0_late.1.refs_0_
  19.6 0.1 collective-permute-start.3
  19.7 1.3 %collective-permute-done.3.inner = bf16[256,256]{1,0:T(8,128)(2,1)S(1)} collective-permute-done((bf16[256,256]{1,0:T(8,128)(2,1)S(1)}, bf16[256,256]{1,0:T(8,128)(2,1)S(1)}, u32[]{:S(2)}, u32[]{:S(2)}) %collective-permute-start.3) | collective-permute-done | bytes 131104 | tf_op jit(solution)/shard_map/ppermute | solution.py:42
  21.1 0.2 level1.1.refs_1_
  21.3 0.1 collective-permute-start.4
  21.4 4.7 %collective-permute-start.5 = (bf16[256,256]{1,0:T(8,128)(2,1)S(1)}, bf16[256,256]{1,0:T(8,128)(2,1)S(1)}, u32[]{:S(2)}, u32[]{:S(2)}) collective-permute-start(bf16[256,256]{1,0:T(8,128)(2,1)S(1)} %level1.1.refs_1_), channel_id=1, source_target_pairs={{0,14},{1,15},{2,0},{3,1},{4,2},{5,3},{6,4},{7,5},{8,6},{9,7},{10,... | collective-permute-start | bytes 393224 | tf_op jit(solution)/shard_map/ppermute | solution.py:22
  26.1 3.8 %collective-permute-done.4.lower = bf16[256,256]{1,0:T(8,128)(2,1)S(1)} collective-permute-done((bf16[256,256]{1,0:T(8,128)(2,1)S(1)}, bf16[256,256]{1,0:T(8,128)(2,1)S(1)}, u32[]{:S(2)}, u32[]{:S(2)}) %collective-permute-start.4) | collective-permute-done | bytes 131104 | tf_op jit(solution)/shard_map/ppermute | solution.py:22
  29.9 0.1 collective-permute-done.5.upper
  29.9 0.2 level2.1.refs_2_
  30.2 0.1 collective-permute-start.6
  30.2 3.8 %collective-permute-start.7 = (bf16[256,256]{1,0:T(8,128)(2,1)S(1)}, bf16[256,256]{1,0:T(8,128)(2,1)S(1)}, u32[]{:S(2)}, u32[]{:S(2)}) collective-permute-start(bf16[256,256]{1,0:T(8,128)(2,1)S(1)} %level2.1.refs_2_), channel_id=1, source_target_pairs={{0,12},{1,13},{2,14},{3,15},{4,0},{5,1},{6,2},{7,3},{8,4},{9,5},{1... | collective-permute-start | bytes 393224 | tf_op jit(solution)/shard_map/ppermute | solution.py:22
  34.0 1.3 %collect.1 = (bf16[12,256,256]{2,1,0:T(8,128)(2,1)}, bf16[4,1,256,256]{3,2,1,0:T(8,128)(2,1)}) custom-call(bf16[8,256,256]{2,1,0:T(8,128)(2,1)S(1)} %get-tuple-element.13.low, bf16[4,256,256]{2,1,0:T(8,128)(2,1)S(1)} %leaf_rest.1.rest_1_.top, bf16[256,256]{1,0:T(8,128)(2,1)S(1)} %level0_late.1.refs_0_, bf16[256,256]{1,0:T(8,128)(2,1)S(1)} %level1.1.refs_1_, ...), custom_call_target="tpu_custom_call" | custom-call | bytes 3932160 | tf_op jit(solution)/shard_map/collect/pallas_call | solution.py:307
  35.4 2.9 %collective-permute-done.6.lower = bf16[256,256]{1,0:T(8,128)(2,1)S(1)} collective-permute-done((bf16[256,256]{1,0:T(8,128)(2,1)S(1)}, bf16[256,256]{1,0:T(8,128)(2,1)S(1)}, u32[]{:S(2)}, u32[]{:S(2)}) %collective-permute-start.6) | collective-permute-done | bytes 131104 | tf_op jit(solution)/shard_map/ppermute | solution.py:22
  38.2 0.0 collective-permute-done.7.upper
  38.2 0.9 %node_last.1 = bf16[4,1,256,256]{3,2,1,0:T(8,128)(2,1)} custom-call(bf16[256,256]{1,0:T(8,128)(2,1)S(1)} %collective-permute-done.6.lower, bf16[256,256]{1,0:T(8,128)(2,1)S(1)} %collective-permute-done.7.upper, bf16[3,256,256]{2,1,0:T(8,128)(2,1)S(1)} %get-tuple-element.20.lower_mat, ...), custom_call_target="tpu_custom_call", output_to_operand_aliasing={{}: (5, {})} | custom-call | tf_op jit(solution)/shard_map/node_last/pallas_call | solution.py:348
  (7 shorter events, 0.0 us)
Async XLA Ops:
  6.1 6.2 %collective-permute-start.1 = (bf16[256,256]{1,0:T(8,128)(2,1)S(1)}, bf16[256,256]{1,0:T(8,128)(2,1)S(1)}, u32[]{:S(2)}, u32[]{:S(2)}) collective-permute-start(bf16[256,256]{1,0:T(8,128)(2,1)S(1)} %get-tuple-element.15.upper.edge), channel_id=1, source_target_pairs={{0,1},{1,0},{2,3},{3,2},{4,5},{5,4},{6,7},{7,6},{8,9},{9,8},{10,11... | collective-permute-start | bytes 393224 | tf_op jit(solution)/shard_map/ppermute | solution.py:42
  6.4 11.1 %collective-permute-start = (bf16[256,256]{1,0:T(8,128)(2,1)S(1)}, bf16[256,256]{1,0:T(8,128)(2,1)S(1)}, u32[]{:S(2)}, u32[]{:S(2)}) collective-permute-start(bf16[256,256]{1,0:T(8,128)(2,1)S(1)} %get-tuple-element.14.part), channel_id=1, source_target_pairs={{0,15},{1,2},{2,1},{3,4},{4,3},{5,6},{6,5},{7,8},{8,7},{9,10},{10,... | collective-permute-start | bytes 393224 | tf_op jit(solution)/shard_map/ppermute | solution.py:48
  12.3 7.2 %collective-permute-start.2 = (bf16[256,256]{1,0:T(8,128)(2,1)S(1)}, bf16[256,256]{1,0:T(8,128)(2,1)S(1)}, u32[]{:S(2)}, u32[]{:S(2)}) collective-permute-start(bf16[256,256]{1,0:T(8,128)(2,1)S(1)} %level0_early.1._.early), channel_id=1, source_target_pairs={{0,15},{1,2},{2,1},{3,4},{4,3},{5,6},{6,5},{7,8},{8,7},{9,10},{10,... | collective-permute-start | bytes 393224 | tf_op jit(solution)/shard_map/ppermute | solution.py:48
  13.6 3.4 %copy-start = (bf16[4,1,2,256,256]{4,3,2,1,0:T(8,128)(2,1)S(1)}, bf16[4,1,2,256,256]{4,3,2,1,0:T(8,128)(2,1)}, u32[]{:S(2)}) copy-start(bf16[4,1,2,256,256]{4,3,2,1,0:T(8,128)(2,1)} %factor.5) | copy-start | bytes 3145732
  13.6 3.4 %copy-start.1 = (bf16[4,1,256,256]{3,2,1,0:T(8,128)(2,1)S(1)}, bf16[4,1,256,256]{3,2,1,0:T(8,128)(2,1)}, u32[]{:S(2)}) copy-start(bf16[4,1,256,256]{3,2,1,0:T(8,128)(2,1)} %rhs.5) | copy-start | bytes 1572868
  13.6 3.4 %copy-start.2 = (bf16[4,1,256,256]{3,2,1,0:T(8,128)(2,1)S(1)}, bf16[4,1,256,256]{3,2,1,0:T(8,128)(2,1)}, u32[]{:S(2)}) copy-start(bf16[4,1,256,256]{3,2,1,0:T(8,128)(2,1)} %inverse.5) | copy-start | bytes 1572868
  19.6 1.4 %collective-permute-start.3 = (bf16[256,256]{1,0:T(8,128)(2,1)S(1)}, bf16[256,256]{1,0:T(8,128)(2,1)S(1)}, u32[]{:S(2)}, u32[]{:S(2)}) collective-permute-start(bf16[256,256]{1,0:T(8,128)(2,1)S(1)} %level0_late.1.refs_0_), channel_id=1, source_target_pairs={{0,1},{1,0},{2,3},{3,2},{4,5},{5,4},{6,7},{7,6},{8,9},{9,8},{10,11... | collective-permute-start | bytes 393224 | tf_op jit(solution)/shard_map/ppermute | solution.py:42
  21.3 8.6 %collective-permute-start.4 = (bf16[256,256]{1,0:T(8,128)(2,1)S(1)}, bf16[256,256]{1,0:T(8,128)(2,1)S(1)}, u32[]{:S(2)}, u32[]{:S(2)}) collective-permute-start(bf16[256,256]{1,0:T(8,128)(2,1)S(1)} %level1.1.refs_1_), channel_id=1, source_target_pairs={{0,2},{1,3},{2,4},{3,5},{4,6},{5,7},{6,8},{7,9},{8,10},{9,11},{10,... | collective-permute-start | bytes 393224 | tf_op jit(solution)/shard_map/ppermute | solution.py:22
  21.4 8.6 %collective-permute-start.5 = (bf16[256,256]{1,0:T(8,128)(2,1)S(1)}, bf16[256,256]{1,0:T(8,128)(2,1)S(1)}, u32[]{:S(2)}, u32[]{:S(2)}) collective-permute-start(bf16[256,256]{1,0:T(8,128)(2,1)S(1)} %level1.1.refs_1_), channel_id=1, source_target_pairs={{0,14},{1,15},{2,0},{3,1},{4,2},{5,3},{6,4},{7,5},{8,6},{9,7},{10,... | collective-permute-start | bytes 393224 | tf_op jit(solution)/shard_map/ppermute | solution.py:22
  30.2 8.1 %collective-permute-start.6 = (bf16[256,256]{1,0:T(8,128)(2,1)S(1)}, bf16[256,256]{1,0:T(8,128)(2,1)S(1)}, u32[]{:S(2)}, u32[]{:S(2)}) collective-permute-start(bf16[256,256]{1,0:T(8,128)(2,1)S(1)} %level2.1.refs_2_), channel_id=1, source_target_pairs={{0,4},{1,5},{2,6},{3,7},{4,8},{5,9},{6,10},{7,11},{8,12},{9,13},{1... | collective-permute-start | bytes 393224 | tf_op jit(solution)/shard_map/ppermute | solution.py:22
  30.2 8.0 %collective-permute-start.7 = (bf16[256,256]{1,0:T(8,128)(2,1)S(1)}, bf16[256,256]{1,0:T(8,128)(2,1)S(1)}, u32[]{:S(2)}, u32[]{:S(2)}) collective-permute-start(bf16[256,256]{1,0:T(8,128)(2,1)S(1)} %level2.1.refs_2_), channel_id=1, source_target_pairs={{0,12},{1,13},{2,14},{3,15},{4,0},{5,1},{6,2},{7,3},{8,4},{9,5},{1... | collective-permute-start | bytes 393224 | tf_op jit(solution)/shard_map/ppermute | solution.py:22

commit v3 on v2

--- a/solution.py
+++ b/solution.py
@@ -42,23 +42,14 @@
     return lax.ppermute(value, axis, [(i, i ^ 1) for i in range(length)])
 
 
-def border_swap(value, axis):
-    length = lax.axis_size(axis)
-    pairs = [(i, (i + (1 if i % 2 else -1)) % length) for i in range(length)]
-    return lax.ppermute(value, axis, pairs)
-
-
-def on_odd():
-    return lax.rem(lax.axis_index("rows"), 2) == 1
-
-
 def edge_kernel(
     columns, link, rhs, inverse, factor, node_rhs, node_inverse, node_factor,
-    solved, edge, sent, lower_mat, upper_mat, const,
-    pattern, rhs_v, inv_v, fac_v, top_fac, left, node_r, node_i, node_f, sem,
+    solved, edge, down,
+    pattern, rhs_v, inv_v, fac_v, top_fac, left, both, const, node_r, node_i, node_f, sem,
 ):
     n = LEVEL_ROWS
     low = 2 * n
+    block = factor.shape[2]
     slots = iter(range(sem.shape[0]))
 
     def load(src, dst):
@@ -66,54 +57,49 @@
         copy.start()
         return copy
 
-    first_inv = load(inverse.at[pl.ds(0, n)], inv_v.at[pl.ds(0, n)])
-    first_rhs = load(rhs.at[pl.ds(0, n)], rhs_v.at[pl.ds(0, n)])
-    pattern_in = load(columns, pattern)
-    next_rhs = load(rhs.at[pl.ds(n, n)], rhs_v.at[pl.ds(n, n)])
-    next_fac = [load(factor.at[r], fac_v.at[r]) for r in range(n)]
-    next_inv = load(inverse.at[pl.ds(n, n)], inv_v.at[pl.ds(n, n)])
+    top = link[0]
+    first_in = (
+        load(inverse.at[pl.ds(0, n)], inv_v.at[pl.ds(0, n)]),
+        load(rhs.at[pl.ds(0, n)], rhs_v.at[pl.ds(0, n)]),
+    )
     node_in = (
         load(node_inverse.at[0, 0], node_i),
         load(node_factor.at[0, 0], node_f),
         load(node_rhs.at[0, 0], node_r),
-    )
-    top = link[0]
-    last = (
+        load(inverse.at[top], both.at[pl.ds(0, block)]),
+    )
+    next_in = (
+        load(columns, pattern),
+        load(rhs.at[pl.ds(n, n)], rhs_v.at[pl.ds(n, n)]),
+        load(inverse.at[pl.ds(n, n)], inv_v.at[pl.ds(n, n)]),
+        load(factor.at[pl.ds(0, n)], fac_v),
+    )
+    last_in = (
+        load(rhs.at[top], rhs_v.at[low]),
         load(factor.at[top - n], top_fac),
-        load(rhs.at[top], rhs_v.at[low]),
-        load(inverse.at[top], inv_v.at[low]),
-    )
-    first_inv.wait()
-    first_rhs.wait()
+    )
+    for copy in first_in:
+        copy.wait()
     for r in range(n):
         solved[r] = mm(inv_v[r], rhs_v[r]).astype(BF16)
-    pattern_in.wait()
-    next_rhs.wait()
-    for r in range(n):
-        next_fac[r].wait()
+    for copy in node_in:
+        copy.wait()
+    down[1] = mm(node_i[...], node_f[0]).astype(BF16)
+    upper = mm(node_i[...], node_f[1]).astype(BF16)
+    const[...] = mm(node_i[...], node_r[...])
+    both[pl.ds(block, block)] = mm(upper, both[pl.ds(0, block)]).astype(BF16)
+    for copy in next_in:
+        copy.wait()
+    for r in range(n):
         left[r] = leaf_residual(fac_v.at[r], solved, pattern, r, rhs_v[n + r])
-    next_inv.wait()
     for r in range(n):
         solved[n + r] = mm(inv_v[n + r], left[r]).astype(BF16)
-    for copy in node_in:
-        copy.wait()
-    lower_mat[...] = mm(node_i[...], node_f[0]).astype(BF16)
-    upper_mat[...] = mm(node_i[...], node_f[1]).astype(BF16)
-    const[...] = mm(node_i[...], node_r[...])
-    for copy in last:
+    for copy in last_in:
         copy.wait()
     residual = leaf_residual(top_fac, solved, pattern, top - n, rhs_v[low])
-    edge_value = mm(inv_v[low], residual).astype(BF16)
-    edge[...] = edge_value
-    odd = on_odd()
-
-    @pl.when(odd)
-    def _():
-        sent[...] = edge_value
-
-    @pl.when(jnp.logical_not(odd))
-    def _():
-        sent[...] = (const[...] - mm(upper_mat[...], edge_value)).astype(BF16)
+    product = mm(both[...], residual)
+    edge[...] = product[:block].astype(BF16)
+    down[0] = (const[...] - product[block:]).astype(BF16)
 
 
 def edge_call(pattern, link, rhs, inverse, factor, node_rhs, node_inverse, node_factor):
@@ -125,24 +111,23 @@
         out_shape=(
             pltpu.VMEM((2 * n, block, loads), BF16),
             pltpu.VMEM((block, loads), BF16),
-            pltpu.VMEM((block, loads), BF16),
-            pltpu.VMEM((block, block), BF16),
-            pltpu.VMEM((block, block), BF16),
-            pltpu.VMEM((block, loads), F32),
+            pltpu.VMEM((2, block, loads), BF16),
         ),
         in_specs=[HBM, SMEM] + [HBM] * 6,
-        out_specs=(VMEM,) * 6,
+        out_specs=(VMEM,) * 3,
         scratch_shapes=[
             pltpu.SMEM(pattern.shape, jnp.int32),
             pltpu.VMEM((2 * n + 1, block, loads), BF16),
-            pltpu.VMEM((2 * n + 1, block, block), BF16),
+            pltpu.VMEM((2 * n, block, block), BF16),
             pltpu.VMEM((n, coupled, block, block), BF16),
             pltpu.VMEM((coupled, block, block), BF16),
             pltpu.VMEM((n, block, loads), BF16),
+            pltpu.VMEM((2 * block, block), BF16),
+            pltpu.VMEM((block, loads), F32),
             pltpu.VMEM((block, loads), BF16),
             pltpu.VMEM((block, block), BF16),
             pltpu.VMEM((2, block, block), BF16),
-            pltpu.SemaphoreType.DMA((11 + n,)),
+            pltpu.SemaphoreType.DMA((12,)),
         ],
         compiler_params=pltpu.CompilerParams(vmem_limit_bytes=16 << 20),
         name="leaf_edge",
@@ -152,44 +137,22 @@
     )
 
 
-def early_kernel(lower, upper, lower_mat, upper_mat, const, out):
-    odd = on_odd()
+def node_zero_kernel(down, lower, *rest):
+    rest[-1][...] = (down[0].astype(F32) - mm(down[1], lower[...])).astype(BF16)
+
+
+def level_one_kernel(inner, below, above, edge, lower_mat, upper_mat, const, out):
+    odd = lax.rem(lax.axis_index("rows"), 2) == 1
 
     @pl.when(odd)
     def _():
-        total = const[...] - mm(upper_mat[...], upper[...]) - mm(lower_mat[...], lower[...])
+        upper = (above[0].astype(F32) - mm(above[1], edge[...])).astype(BF16)
+        total = const[0] - mm(lower_mat[0], inner[...]) - mm(upper_mat[0], upper)
         out[...] = total.astype(BF16)
 
     @pl.when(jnp.logical_not(odd))
     def _():
-        out[...] = lower_mat[...]
-
-
-def late_kernel(part, lower, early, lower_mat, *rest):
-    out = rest[-1]
-    odd = on_odd()
-
-    @pl.when(odd)
-    def _():
-        out[...] = early[...]
-
-    @pl.when(jnp.logical_not(odd))
-    def _():
-        out[...] = (part[...].astype(F32) - mm(lower_mat[...], lower[...])).astype(BF16)
-
-
-def level_one_kernel(inner, came_first, came_next, edge, lower_mat, upper_mat, const, out):
-    odd = on_odd()
-
-    @pl.when(odd)
-    def _():
-        upper = came_first[...].astype(F32) - mm(came_next[...], edge[...])
-        total = const[0] - mm(lower_mat[0], inner[...]) - mm(upper_mat[0], upper.astype(BF16))
-        out[...] = total.astype(BF16)
-
-    @pl.when(jnp.logical_not(odd))
-    def _():
-        total = const[0] - mm(upper_mat[0], inner[...]) - mm(lower_mat[0], came_next[...])
+        total = const[0] - mm(upper_mat[0], inner[...]) - mm(lower_mat[0], below[...])
         out[...] = total.astype(BF16)
 
 
@@ -368,26 +331,25 @@
     link_row,
 ):
     columns = block_pattern.T
-    low, edge, sent, lower_mat, upper_mat, const = edge_call(
+    low, edge, down = edge_call(
         columns, link_row, leaf_rhs, leaf_inverse, leaf_factor,
         separator_rhs, separator_inverse, separator_factor,
     )
     shape = edge.shape
+    edge_below = passed_along(edge, "rows", 1)
     edge_inner = pair_swap(edge, "rows")
-    came_first = border_swap(sent, "rows")
-    early = small_call(
-        early_kernel, "level0_early", shape, edge_inner, edge, lower_mat, upper_mat, const
-    )
-    came_next = border_swap(early, "rows")
+    early = small_call(node_zero_kernel, "level0_early", shape, down, edge_inner)
+    below = passed_along(early, "rows", 1)
+    above = passed_along(down, "rows", -1)
     top = rest_call(columns, leaf_rhs, leaf_inverse, leaf_factor, low)
     mats = fold_call(separator_rhs, separator_inverse, separator_factor, early)
     block = small_call(
-        late_kernel, "level0_late", shape, sent, came_first, early, lower_mat, came_next, top, mats[2],
+        node_zero_kernel, "level0_late", shape, down, edge_below, top, mats[2], below
     )
     inner = pair_swap(block, "rows")
     levels = [block]
     block = small_call(
-        level_one_kernel, "level1", shape, inner, came_first, came_next, edge, *mats
+        level_one_kernel, "level1", shape, inner, below, above, edge, *mats
     )
     levels.append(block)
     depth = separator_rhs.shape[0]

time: 39.3 us -> 37.4 us (0.952)
  starting transfers between devices: 16.2 us -> 15.1 us
  Pallas kernels: 11.5 us -> 11.1 us
    ppermute x2 -> x0, starting transfers between devices: 7.13 us -> none  [border_swap(): return lax.ppermute(value, axis, pairs)]
    ppermute x4 -> x7, starting transfers between devices: 8.64 us -> 14.5 us  [passed_along(): lax.ppermute(value, axis, [(i, (i + by) % length) for i in range(length)])]
    ppermute x2 -> x0, waiting for transfers between devices: 1.94 us -> none  [border_swap(): return lax.ppermute(value, axis, pairs)]
    ppermute x2, waiting for transfers between devices: 1.34 us -> 2.24 us  [pair_swap(): return lax.ppermute(value, axis, [(i, i ^ 1) for i in range(length)])]
    ppermute x4 -> x7, waiting for transfers between devices: 6.75 us -> 7.42 us  [passed_along(): lax.ppermute(value, axis, [(i, (i + by) % length) for i in range(length)])]
    pallas_call x1, Pallas kernels: 4.81 us -> 4.15 us  [edge_call(): pl.pallas_call(edge_kernel, out_shape=(pltpu.VMEM((2 * n, block, loads),...]
  transfers between devices with their start and end apart: 8 -> 9, of which waited for: 5 -> 6; matrix products, arithmetic and copies ran while one was open for 0% -> 0% of each run, Pallas kernels for 13% -> 15%
where the time goes in v3:
time: 37.4 us; the launch traced here: 37.2 us
  starting transfers between devices  15.1 us (40%)
  Pallas kernels  11.1 us (30%)
  waiting for transfers between devices  9.66 us (26%)
  between operations  1.4 us (4%)
    ppermute x7, starting transfers between devices, passed_along(): lax.ppermute(value, axis, [(i, (i + by) % length) for i in range(length)])  14.5 us
    ppermute x7, waiting for transfers between devices, passed_along(): lax.ppermute(value, axis, [(i, (i + by) % length) for i in range(length)])  7.42 us
    pallas_call x1, Pallas kernels, edge_call(): pl.pallas_call(edge_kernel, out_shape=(pltpu.VMEM((2 * n, block, loads),...  4.15 us
    pallas_call x1, Pallas kernels, rest_call(): pl.pallas_call(rest_kernel, out_shape=pltpu.VMEM((n, block, loads), BF16)...  3.41 us
    ppermute x2, waiting for transfers between devices, pair_swap(): return lax.ppermute(value, axis, [(i, i ^ 1) for i in range(length)])  2.24 us
    pallas_call x1, Pallas kernels, collect_call(): pl.pallas_call(collect_kernel, out_shape=(jax.ShapeDtypeStruct((rows,) +...  1.31 us
    pallas_call x1, Pallas kernels, last_call(): pl.pallas_call(last_kernel, out_shape=jax.ShapeDtypeStruct(collected.shap...  0.88 us
    pallas_call x4, Pallas kernels, small_call(): pl.pallas_call(kernel, out_shape=pltpu.VMEM(shape, BF16), in_specs=[VMEM]...  0.83 us
  transfers between devices with their start and end apart: 9, of which 6 were waited for; matrix products, arithmetic and copies ran while one was open for 0% of the time, Pallas kernels for 15%

profile of v3, /device:TPU:0, one launch (start us, length us, event | category | flops | bytes accessed | tf_op | source)
XLA Modules:
  0.0 37.2 jit_solution(10376317406605712876)
XLA Ops:
  1.3 4.1 %leaf_edge.1 = (bf16[8,256,256]{2,1,0:T(8,128)(2,1)S(1)}, bf16[256,256]{1,0:T(8,128)(2,1)S(1)}, bf16[2,256,256]{2,1,0:T(8,128)(2,1)S(1)}) custom-call(s32[4,8]{1,0:T(4,128)} %bitcast.1, s32[1]{0:T(128)S(6)} %copy.12.link, bf16[12,256,256]{2,1,0:T(8,128)(2,1)} %rhs.4, bf16[12,256,256]{2,1,0:T(8,128)(2,1)} %inverse.4, bf16[8,4,256,256]{3,2,1,0:T(8,128)(2,1)} %factor.4, ...), custom_call_target="tpu_custom_call" | custom-call | tf_op jit(solution)/shard_map/leaf_edge/pallas_call | solution.py:109
  5.4 0.5 %collective-permute-start.1 = (bf16[256,256]{1,0:T(8,128)(2,1)S(1)}, bf16[256,256]{1,0:T(8,128)(2,1)S(1)}, u32[]{:S(2)}, u32[]{:S(2)}) collective-permute-start(bf16[256,256]{1,0:T(8,128)(2,1)S(1)} %get-tuple-element.12.edge), channel_id=1, source_target_pairs={{0,1},{1,0},{2,3},{3,2},{4,5},{5,4},{6,7},{7,6},{8,9},{9,8},{10,11... | collective-permute-start | bytes 393224 | tf_op jit(solution)/shard_map/ppermute | solution.py:42
  6.0 0.1 collective-permute-start
  6.0 0.9 %collective-permute-done.1.lower = bf16[256,256]{1,0:T(8,128)(2,1)S(1)} collective-permute-done((bf16[256,256]{1,0:T(8,128)(2,1)S(1)}, bf16[256,256]{1,0:T(8,128)(2,1)S(1)}, u32[]{:S(2)}, u32[]{:S(2)}) %collective-permute-start.1) | collective-permute-done | bytes 131104 | tf_op jit(solution)/shard_map/ppermute | solution.py:42
  6.9 0.2 level0_early.1._
  7.1 1.8 %collective-permute-start.2 = (bf16[256,256]{1,0:T(8,128)(2,1)S(1)}, bf16[256,256]{1,0:T(8,128)(2,1)S(1)}, u32[]{:S(2)}, u32[]{:S(2)}) collective-permute-start(bf16[256,256]{1,0:T(8,128)(2,1)S(1)} %level0_early.1._), channel_id=1, source_target_pairs={{0,1},{1,2},{2,3},{3,4},{4,5},{5,6},{6,7},{7,8},{8,9},{9,10},{10,1... | collective-permute-start | bytes 393224 | tf_op jit(solution)/shard_map/ppermute | solution.py:22
  8.9 4.0 %collective-permute-start.4 = (bf16[2,256,256]{2,1,0:T(8,128)(2,1)S(1)}, bf16[2,256,256]{2,1,0:T(8,128)(2,1)S(1)}, u32[]{:S(2)}, u32[]{:S(2)}) collective-permute-start(bf16[2,256,256]{2,1,0:T(8,128)(2,1)S(1)} %get-tuple-element.11.down), channel_id=1, source_target_pairs={{0,15},{1,0},{2,1},{3,2},{4,3},{5,4},{6,5},{7,6},{8,7},{9,8},{10,9... | collective-permute-start | bytes 786440 | tf_op jit(solution)/shard_map/ppermute | solution.py:22
  12.9 3.4 %leaf_rest.1.rest_0_.top = bf16[4,256,256]{2,1,0:T(8,128)(2,1)S(1)} custom-call(s32[4,8]{1,0:T(4,128)} %bitcast.2, bf16[12,256,256]{2,1,0:T(8,128)(2,1)} %rhs.4, bf16[12,256,256]{2,1,0:T(8,128)(2,1)} %inverse.4, bf16[8,4,256,256]{3,2,1,0:T(8,128)(2,1)} %factor.4, bf16[8,256,256]{2,1,0:T(8,128)(2,1)S(1)} %get-tuple-element.10.low), custom_call_target="tpu_custom_call" | custom-call | flops 671088640 | bytes 4718592 | tf_op jit(solution)/shard_map/leaf_rest/pallas_call | solution.py:197
  16.4 0.5 %fold.1 = (bf16[3,256,256]{2,1,0:T(8,128)(2,1)S(1)}, bf16[3,256,256]{2,1,0:T(8,128)(2,1)S(1)}, f32[3,256,256]{2,1,0:T(8,128)S(1)}) custom-call(bf16[4,1,256,256]{3,2,1,0:T(8,128)(2,1)S(1)} %copy-done.1, bf16[4,1,256,256]{3,2,1,0:T(8,128)(2,1)S(1)} %copy-done.2, bf16[4,1,2,256,256]{4,3,2,1,0:T(8,128)(2,1)S(1)} %copy-done, bf16[256,256]{1,0:T(8,128)(2,1)S(1)} %level0_early.1._), custom_call_target="tpu_custom_call" | custom-call | flops 301989888 | bytes 3145728 | tf_op jit(solution)/shard_map/fold/pallas_call | solution.py:229
  16.9 0.2 level0_late.1.refs_0_
  17.1 0.1 collective-permute-start.3
  17.2 1.3 %collective-permute-done.3.inner = bf16[256,256]{1,0:T(8,128)(2,1)S(1)} collective-permute-done((bf16[256,256]{1,0:T(8,128)(2,1)S(1)}, bf16[256,256]{1,0:T(8,128)(2,1)S(1)}, u32[]{:S(2)}, u32[]{:S(2)}) %collective-permute-start.3) | collective-permute-done | bytes 131104 | tf_op jit(solution)/shard_map/ppermute | solution.py:42
  18.5 0.2 level1.1.refs_1_
  18.7 0.1 collective-permute-start.5
  18.8 4.7 %collective-permute-start.6 = (bf16[256,256]{1,0:T(8,128)(2,1)S(1)}, bf16[256,256]{1,0:T(8,128)(2,1)S(1)}, u32[]{:S(2)}, u32[]{:S(2)}) collective-permute-start(bf16[256,256]{1,0:T(8,128)(2,1)S(1)} %level1.1.refs_1_), channel_id=1, source_target_pairs={{0,14},{1,15},{2,0},{3,1},{4,2},{5,3},{6,4},{7,5},{8,6},{9,7},{10,... | collective-permute-start | bytes 393224 | tf_op jit(solution)/shard_map/ppermute | solution.py:22
  23.5 3.8 %collective-permute-done.5.lower = bf16[256,256]{1,0:T(8,128)(2,1)S(1)} collective-permute-done((bf16[256,256]{1,0:T(8,128)(2,1)S(1)}, bf16[256,256]{1,0:T(8,128)(2,1)S(1)}, u32[]{:S(2)}, u32[]{:S(2)}) %collective-permute-start.5) | collective-permute-done | bytes 131104 | tf_op jit(solution)/shard_map/ppermute | solution.py:22
  27.3 0.1 collective-permute-done.6.upper
  27.4 0.2 level2.1.refs_2_
  27.6 0.7 %collective-permute-start.7 = (bf16[256,256]{1,0:T(8,128)(2,1)S(1)}, bf16[256,256]{1,0:T(8,128)(2,1)S(1)}, u32[]{:S(2)}, u32[]{:S(2)}) collective-permute-start(bf16[256,256]{1,0:T(8,128)(2,1)S(1)} %level2.1.refs_2_), channel_id=1, source_target_pairs={{0,4},{1,5},{2,6},{3,7},{4,8},{5,9},{6,10},{7,11},{8,12},{9,13},{1... | collective-permute-start | bytes 393224 | tf_op jit(solution)/shard_map/ppermute | solution.py:22
  28.3 3.1 %collective-permute-start.8 = (bf16[256,256]{1,0:T(8,128)(2,1)S(1)}, bf16[256,256]{1,0:T(8,128)(2,1)S(1)}, u32[]{:S(2)}, u32[]{:S(2)}) collective-permute-start(bf16[256,256]{1,0:T(8,128)(2,1)S(1)} %level2.1.refs_2_), channel_id=1, source_target_pairs={{0,12},{1,13},{2,14},{3,15},{4,0},{5,1},{6,2},{7,3},{8,4},{9,5},{1... | collective-permute-start | bytes 393224 | tf_op jit(solution)/shard_map/ppermute | solution.py:22
  31.5 1.3 %collect.1 = (bf16[12,256,256]{2,1,0:T(8,128)(2,1)}, bf16[4,1,256,256]{3,2,1,0:T(8,128)(2,1)}) custom-call(bf16[8,256,256]{2,1,0:T(8,128)(2,1)S(1)} %get-tuple-element.10.low, bf16[4,256,256]{2,1,0:T(8,128)(2,1)S(1)} %leaf_rest.1.rest_0_.top, bf16[256,256]{1,0:T(8,128)(2,1)S(1)} %level0_late.1.refs_0_, bf16[256,256]{1,0:T(8,128)(2,1)S(1)} %level1.1.refs_1_, ...), custom_call_target="tpu_custom_call" | custom-call | bytes 3932160 | tf_op jit(solution)/shard_map/collect/pallas_call | solution.py:270
  32.8 2.8 %collective-permute-done.7.lower = bf16[256,256]{1,0:T(8,128)(2,1)S(1)} collective-permute-done((bf16[256,256]{1,0:T(8,128)(2,1)S(1)}, bf16[256,256]{1,0:T(8,128)(2,1)S(1)}, u32[]{:S(2)}, u32[]{:S(2)}) %collective-permute-start.7) | collective-permute-done | bytes 131104 | tf_op jit(solution)/shard_map/ppermute | solution.py:22
  35.6 0.7 %collective-permute-done.8.upper = bf16[256,256]{1,0:T(8,128)(2,1)S(1)} collective-permute-done((bf16[256,256]{1,0:T(8,128)(2,1)S(1)}, bf16[256,256]{1,0:T(8,128)(2,1)S(1)}, u32[]{:S(2)}, u32[]{:S(2)}) %collective-permute-start.8) | collective-permute-done | bytes 131104 | tf_op jit(solution)/shard_map/ppermute | solution.py:22
  36.3 0.9 %node_last.1 = bf16[4,1,256,256]{3,2,1,0:T(8,128)(2,1)} custom-call(bf16[256,256]{1,0:T(8,128)(2,1)S(1)} %collective-permute-done.7.lower, bf16[256,256]{1,0:T(8,128)(2,1)S(1)} %collective-permute-done.8.upper, bf16[3,256,256]{2,1,0:T(8,128)(2,1)S(1)} %get-tuple-element.14.lower_mat, ...), custom_call_target="tpu_custom_call", output_to_operand_aliasing={{}: (5, {})} | custom-call | tf_op jit(solution)/shard_map/node_last/pallas_call | solution.py:311
  (9 shorter events, 0.0 us)
Async XLA Ops:
  5.4 1.5 %collective-permute-start.1 = (bf16[256,256]{1,0:T(8,128)(2,1)S(1)}, bf16[256,256]{1,0:T(8,128)(2,1)S(1)}, u32[]{:S(2)}, u32[]{:S(2)}) collective-permute-start(bf16[256,256]{1,0:T(8,128)(2,1)S(1)} %get-tuple-element.12.edge), channel_id=1, source_target_pairs={{0,1},{1,0},{2,3},{3,2},{4,5},{5,4},{6,7},{7,6},{8,9},{9,8},{10,11... | collective-permute-start | bytes 393224 | tf_op jit(solution)/shard_map/ppermute | solution.py:42
  6.0 10.9 %collective-permute-start = (bf16[256,256]{1,0:T(8,128)(2,1)S(1)}, bf16[256,256]{1,0:T(8,128)(2,1)S(1)}, u32[]{:S(2)}, u32[]{:S(2)}) collective-permute-start(bf16[256,256]{1,0:T(8,128)(2,1)S(1)} %get-tuple-element.12.edge), channel_id=1, source_target_pairs={{0,1},{1,2},{2,3},{3,4},{4,5},{5,6},{6,7},{7,8},{8,9},{9,10},{10,1... | collective-permute-start | bytes 393224 | tf_op jit(solution)/shard_map/ppermute | solution.py:22
  7.1 9.7 %collective-permute-start.2 = (bf16[256,256]{1,0:T(8,128)(2,1)S(1)}, bf16[256,256]{1,0:T(8,128)(2,1)S(1)}, u32[]{:S(2)}, u32[]{:S(2)}) collective-permute-start(bf16[256,256]{1,0:T(8,128)(2,1)S(1)} %level0_early.1._), channel_id=1, source_target_pairs={{0,1},{1,2},{2,3},{3,4},{4,5},{5,6},{6,7},{7,8},{8,9},{9,10},{10,1... | collective-permute-start | bytes 393224 | tf_op jit(solution)/shard_map/ppermute | solution.py:22
  8.9 8.3 %collective-permute-start.4 = (bf16[2,256,256]{2,1,0:T(8,128)(2,1)S(1)}, bf16[2,256,256]{2,1,0:T(8,128)(2,1)S(1)}, u32[]{:S(2)}, u32[]{:S(2)}) collective-permute-start(bf16[2,256,256]{2,1,0:T(8,128)(2,1)S(1)} %get-tuple-element.11.down), channel_id=1, source_target_pairs={{0,15},{1,0},{2,1},{3,2},{4,3},{5,4},{6,5},{7,6},{8,7},{9,8},{10,9... | collective-permute-start | bytes 786440 | tf_op jit(solution)/shard_map/ppermute | solution.py:22
  12.9 3.4 %copy-start = (bf16[4,1,2,256,256]{4,3,2,1,0:T(8,128)(2,1)S(1)}, bf16[4,1,2,256,256]{4,3,2,1,0:T(8,128)(2,1)}, u32[]{:S(2)}) copy-start(bf16[4,1,2,256,256]{4,3,2,1,0:T(8,128)(2,1)} %factor.5) | copy-start | bytes 3145732
  12.9 3.4 %copy-start.1 = (bf16[4,1,256,256]{3,2,1,0:T(8,128)(2,1)S(1)}, bf16[4,1,256,256]{3,2,1,0:T(8,128)(2,1)}, u32[]{:S(2)}) copy-start(bf16[4,1,256,256]{3,2,1,0:T(8,128)(2,1)} %rhs.5) | copy-start | bytes 1572868
  12.9 3.4 %copy-start.2 = (bf16[4,1,256,256]{3,2,1,0:T(8,128)(2,1)S(1)}, bf16[4,1,256,256]{3,2,1,0:T(8,128)(2,1)}, u32[]{:S(2)}) copy-start(bf16[4,1,256,256]{3,2,1,0:T(8,128)(2,1)} %inverse.5) | copy-start | bytes 1572868
  17.1 1.4 %collective-permute-start.3 = (bf16[256,256]{1,0:T(8,128)(2,1)S(1)}, bf16[256,256]{1,0:T(8,128)(2,1)S(1)}, u32[]{:S(2)}, u32[]{:S(2)}) collective-permute-start(bf16[256,256]{1,0:T(8,128)(2,1)S(1)} %level0_late.1.refs_0_), channel_id=1, source_target_pairs={{0,1},{1,0},{2,3},{3,2},{4,5},{5,4},{6,7},{7,6},{8,9},{9,8},{10,11... | collective-permute-start | bytes 393224 | tf_op jit(solution)/shard_map/ppermute | solution.py:42
  18.7 8.6 %collective-permute-start.5 = (bf16[256,256]{1,0:T(8,128)(2,1)S(1)}, bf16[256,256]{1,0:T(8,128)(2,1)S(1)}, u32[]{:S(2)}, u32[]{:S(2)}) collective-permute-start(bf16[256,256]{1,0:T(8,128)(2,1)S(1)} %level1.1.refs_1_), channel_id=1, source_target_pairs={{0,2},{1,3},{2,4},{3,5},{4,6},{5,7},{6,8},{7,9},{8,10},{9,11},{10,... | collective-permute-start | bytes 393224 | tf_op jit(solution)/shard_map/ppermute | solution.py:22
  18.8 8.6 %collective-permute-start.6 = (bf16[256,256]{1,0:T(8,128)(2,1)S(1)}, bf16[256,256]{1,0:T(8,128)(2,1)S(1)}, u32[]{:S(2)}, u32[]{:S(2)}) collective-permute-start(bf16[256,256]{1,0:T(8,128)(2,1)S(1)} %level1.1.refs_1_), channel_id=1, source_target_pairs={{0,14},{1,15},{2,0},{3,1},{4,2},{5,3},{6,4},{7,5},{8,6},{9,7},{10,... | collective-permute-start | bytes 393224 | tf_op jit(solution)/shard_map/ppermute | solution.py:22
  27.6 8.0 %collective-permute-start.7 = (bf16[256,256]{1,0:T(8,128)(2,1)S(1)}, bf16[256,256]{1,0:T(8,128)(2,1)S(1)}, u32[]{:S(2)}, u32[]{:S(2)}) collective-permute-start(bf16[256,256]{1,0:T(8,128)(2,1)S(1)} %level2.1.refs_2_), channel_id=1, source_target_pairs={{0,4},{1,5},{2,6},{3,7},{4,8},{5,9},{6,10},{7,11},{8,12},{9,13},{1... | collective-permute-start | bytes 393224 | tf_op jit(solution)/shard_map/ppermute | solution.py:22
  28.3 8.0 %collective-permute-start.8 = (bf16[256,256]{1,0:T(8,128)(2,1)S(1)}, bf16[256,256]{1,0:T(8,128)(2,1)S(1)}, u32[]{:S(2)}, u32[]{:S(2)}) collective-permute-start(bf16[256,256]{1,0:T(8,128)(2,1)S(1)} %level2.1.refs_2_), channel_id=1, source_target_pairs={{0,12},{1,13},{2,14},{3,15},{4,0},{5,1},{6,2},{7,3},{8,4},{9,5},{1... | collective-permute-start | bytes 393224 | tf_op jit(solution)/shard_map/ppermute | solution.py:22

commit v4 on v3

--- a/solution.py
+++ b/solution.py
@@ -44,7 +44,7 @@
 
 def edge_kernel(
     columns, link, rhs, inverse, factor, node_rhs, node_inverse, node_factor,
-    solved, edge, down,
+    solved, edge, down, lower_mat,
     pattern, rhs_v, inv_v, fac_v, top_fac, left, both, const, node_r, node_i, node_f, sem,
 ):
     n = LEVEL_ROWS
@@ -84,7 +84,7 @@
         solved[r] = mm(inv_v[r], rhs_v[r]).astype(BF16)
     for copy in node_in:
         copy.wait()
-    down[1] = mm(node_i[...], node_f[0]).astype(BF16)
+    lower_mat[...] = mm(node_i[...], node_f[0]).astype(BF16)
     upper = mm(node_i[...], node_f[1]).astype(BF16)
     const[...] = mm(node_i[...], node_r[...])
     both[pl.ds(block, block)] = mm(upper, both[pl.ds(0, block)]).astype(BF16)
@@ -99,7 +99,7 @@
     residual = leaf_residual(top_fac, solved, pattern, top - n, rhs_v[low])
     product = mm(both[...], residual)
     edge[...] = product[:block].astype(BF16)
-    down[0] = (const[...] - product[block:]).astype(BF16)
+    down[...] = (const[...] - product[block:]).astype(BF16)
 
 
 def edge_call(pattern, link, rhs, inverse, factor, node_rhs, node_inverse, node_factor):
@@ -111,10 +111,11 @@
         out_shape=(
             pltpu.VMEM((2 * n, block, loads), BF16),
             pltpu.VMEM((block, loads), BF16),
-            pltpu.VMEM((2, block, loads), BF16),
+            pltpu.VMEM((block, loads), BF16),
+            pltpu.VMEM((block, block), BF16),
         ),
         in_specs=[HBM, SMEM] + [HBM] * 6,
-        out_specs=(VMEM,) * 3,
+        out_specs=(VMEM,) * 4,
         scratch_shapes=[
             pltpu.SMEM(pattern.shape, jnp.int32),
             pltpu.VMEM((2 * n + 1, block, loads), BF16),
@@ -137,29 +138,51 @@
     )
 
 
-def node_zero_kernel(down, lower, *rest):
-    rest[-1][...] = (down[0].astype(F32) - mm(down[1], lower[...])).astype(BF16)
-
-
-def level_one_kernel(inner, below, above, edge, lower_mat, upper_mat, const, out):
+def node_zero_kernel(down, lower_mat, lower, *rest):
+    rest[-1][...] = (down[...].astype(F32) - mm(lower_mat[...], lower[...])).astype(BF16)
+
+
+def below_kernel(below, lower_mat, const, out):
     odd = lax.rem(lax.axis_index("rows"), 2) == 1
 
     @pl.when(odd)
     def _():
-        upper = (above[0].astype(F32) - mm(above[1], edge[...])).astype(BF16)
-        total = const[0] - mm(lower_mat[0], inner[...]) - mm(upper_mat[0], upper)
-        out[...] = total.astype(BF16)
+        out[...] = const[0]
 
     @pl.when(jnp.logical_not(odd))
     def _():
-        total = const[0] - mm(upper_mat[0], inner[...]) - mm(lower_mat[0], below[...])
-        out[...] = total.astype(BF16)
-
-
-def small_call(kernel, name, shape, *args):
+        out[...] = const[0] - mm(lower_mat[0], below[...])
+
+
+def across_kernel(part, above, above_mat, edge, upper_mat, out):
+    odd = lax.rem(lax.axis_index("rows"), 2) == 1
+
+    @pl.when(odd)
+    def _():
+        upper = (above[...].astype(F32) - mm(above_mat[...], edge[...])).astype(BF16)
+        out[...] = part[...] - mm(upper_mat[0], upper)
+
+    @pl.when(jnp.logical_not(odd))
+    def _():
+        out[...] = part[...]
+
+
+def level_one_kernel(inner, part, lower_mat, upper_mat, out):
+    odd = lax.rem(lax.axis_index("rows"), 2) == 1
+
+    @pl.when(odd)
+    def _():
+        out[...] = (part[...] - mm(lower_mat[0], inner[...])).astype(BF16)
+
+    @pl.when(jnp.logical_not(odd))
+    def _():
+        out[...] = (part[...] - mm(upper_mat[0], inner[...])).astype(BF16)
+
+
+def small_call(kernel, name, shape, *args, dtype=BF16):
     return pl.pallas_call(
         kernel,
-        out_shape=pltpu.VMEM(shape, BF16),
+        out_shape=pltpu.VMEM(shape, dtype),
         in_specs=[VMEM] * len(args),
         out_specs=VMEM,
         compiler_params=pltpu.CompilerParams(vmem_limit_bytes=8 << 20),
@@ -167,7 +190,7 @@
     )(*args)
 
 
-def rest_kernel(columns, rhs, inverse, factor, low, top, pattern, rhs_v, inv_v, fac_v, left, sem):
+def rest_kernel(columns, rhs, inverse, factor, low, _, top, pattern, rhs_v, inv_v, fac_v, left, sem):
     n = LEVEL_ROWS
 
     def load(src, dst, slot):
@@ -189,7 +212,7 @@
         top[r] = mm(inv_v[r], left[r]).astype(BF16)
 
 
-def rest_call(pattern, rhs, inverse, factor, low):
+def rest_call(pattern, rhs, inverse, factor, low, after):
     n = LEVEL_ROWS
     coupled, block = factor.shape[1], factor.shape[2]
     loads = rhs.shape[-1]
@@ -197,7 +220,7 @@
     return pl.pallas_call(
         rest_kernel,
         out_shape=pltpu.VMEM((n, block, loads), BF16),
-        in_specs=[HBM] * 4 + [VMEM],
+        in_specs=[HBM] * 4 + [VMEM] * 2,
         out_specs=VMEM,
         scratch_shapes=[
             pltpu.SMEM(pattern.shape, jnp.int32),
@@ -212,7 +235,7 @@
             flops=flops, bytes_accessed=36 * block * block * 2, transcendentals=0
         ),
         name="leaf_rest",
-    )(in_hbm(pattern), in_hbm(rhs), in_hbm(inverse), in_hbm(factor), low)
+    )(in_hbm(pattern), in_hbm(rhs), in_hbm(inverse), in_hbm(factor), low, after)
 
 
 def fold_kernel(rhs, inverse, factor, _, lower_mat, upper_mat, const):
@@ -245,9 +268,9 @@
     )(rhs, inverse, factor, after)
 
 
-def node_kernel(h, lower, upper, lower_mat, upper_mat, const, out):
+def node_kernel(h, lower, upper, lower_mat, upper_mat, const, *rest):
     total = const[h] - mm(upper_mat[h], upper[...]) - mm(lower_mat[h], lower[...])
-    out[...] = total.astype(BF16)
+    rest[-1][...] = total.astype(BF16)
 
 
 def collect_kernel(low, top, *refs):
@@ -331,26 +354,32 @@
     link_row,
 ):
     columns = block_pattern.T
-    low, edge, down = edge_call(
+    low, edge, down, lower_zero = edge_call(
         columns, link_row, leaf_rhs, leaf_inverse, leaf_factor,
         separator_rhs, separator_inverse, separator_factor,
     )
     shape = edge.shape
     edge_below = passed_along(edge, "rows", 1)
     edge_inner = pair_swap(edge, "rows")
-    early = small_call(node_zero_kernel, "level0_early", shape, down, edge_inner)
+    early = small_call(node_zero_kernel, "level0_early", shape, down, lower_zero, edge_inner)
     below = passed_along(early, "rows", 1)
     above = passed_along(down, "rows", -1)
-    top = rest_call(columns, leaf_rhs, leaf_inverse, leaf_factor, low)
+    above_mat = passed_along(lower_zero, "rows", -1)
     mats = fold_call(separator_rhs, separator_inverse, separator_factor, early)
     block = small_call(
-        node_zero_kernel, "level0_late", shape, down, edge_below, top, mats[2], below
+        node_zero_kernel, "level0_late", shape, down, lower_zero, edge_below
     )
     inner = pair_swap(block, "rows")
     levels = [block]
-    block = small_call(
-        level_one_kernel, "level1", shape, inner, below, above, edge, *mats
-    )
+    part = small_call(
+        below_kernel, "level1_below", shape, below, mats[0], mats[2], dtype=F32
+    )
+    part = small_call(
+        across_kernel, "level1_across", shape, part, above, above_mat, edge, mats[1],
+        dtype=F32,
+    )
+    block = small_call(level_one_kernel, "level1", shape, inner, part, *mats[:2])
+    top = rest_call(columns, leaf_rhs, leaf_inverse, leaf_factor, low, block)
     levels.append(block)
     depth = separator_rhs.shape[0]
     for height in range(2, depth):
@@ -359,7 +388,7 @@
         upper = passed_along(block, "rows", -stride)
         if height < depth - 1:
             step = functools.partial(node_kernel, height - 1)
-            block = small_call(step, f"level{height}", shape, lower, upper, *mats)
+            block = small_call(step, f"level{height}", shape, lower, upper, *mats, top)
             levels.append(block)
     solved, collected = collect_call(low, top, levels, (depth, 1) + shape)
     return solved, last_call(lower, upper, *mats, collected)

time: 37.4 us -> 36.9 us (0.987)
  waiting for transfers between devices: 9.66 us -> 8.57 us
  starting transfers between devices: 15.1 us -> 15.5 us
    ppermute x2, waiting for transfers between devices: 2.24 us -> 0.92 us  [pair_swap(): return lax.ppermute(value, axis, [(i, i ^ 1) for i in range(length)])]
    ppermute x7 -> x8, starting transfers between devices: 14.5 us -> 14.9 us  [passed_along(): lax.ppermute(value, axis, [(i, (i + by) % length) for i in range(length)])]
    ppermute x7 -> x8, waiting for transfers between devices: 7.42 us -> 7.65 us  [passed_along(): lax.ppermute(value, axis, [(i, (i + by) % length) for i in range(length)])]
    pallas_call x4 -> x6, Pallas kernels: 0.83 us -> 1.01 us  [small_call(): pl.pallas_call(kernel, out_shape=pltpu.VMEM(shape, dtype), in_specs=[VMEM...]
  transfers between devices with their start and end apart: 9 -> 10, of which waited for: 6 -> 7; matrix products, arithmetic and copies ran while one was open for 0% -> 0% of each run, Pallas kernels for 15% -> 15%
where the time goes in v4:
time: 36.9 us; the launch traced here: 36.7 us
  starting transfers between devices  15.5 us (42%)
  Pallas kernels  11.2 us (30%)
  waiting for transfers between devices  8.57 us (23%)
  between operations  1.43 us (4%)
    ppermute x8, starting transfers between devices, passed_along(): lax.ppermute(value, axis, [(i, (i + by) % length) for i in range(length)])  14.9 us
    ppermute x8, waiting for transfers between devices, passed_along(): lax.ppermute(value, axis, [(i, (i + by) % length) for i in range(length)])  7.65 us
    pallas_call x1, Pallas kernels, edge_call(): pl.pallas_call(edge_kernel, out_shape=(pltpu.VMEM((2 * n, block, loads),...  4.21 us
    pallas_call x1, Pallas kernels, rest_call(): pl.pallas_call(rest_kernel, out_shape=pltpu.VMEM((n, block, loads), BF16)...  3.27 us
    pallas_call x1, Pallas kernels, collect_call(): pl.pallas_call(collect_kernel, out_shape=(jax.ShapeDtypeStruct((rows,) +...  1.31 us
    pallas_call x6, Pallas kernels, small_call(): pl.pallas_call(kernel, out_shape=pltpu.VMEM(shape, dtype), in_specs=[VMEM...  1.01 us
    ppermute x2, waiting for transfers between devices, pair_swap(): return lax.ppermute(value, axis, [(i, i ^ 1) for i in range(length)])  0.92 us
    pallas_call x1, Pallas kernels, last_call(): pl.pallas_call(last_kernel, out_shape=jax.ShapeDtypeStruct(collected.shap...  0.88 us
  transfers between devices with their start and end apart: 10, of which 7 were waited for; matrix products, arithmetic and copies ran while one was open for 0% of the time, Pallas kernels for 15%

profile of v4, /device:TPU:0, one launch (start us, length us, event | category | flops | bytes accessed | tf_op | source)
XLA Modules:
  0.0 36.7 jit_solution(15052906386855228549)
XLA Ops:
  1.3 4.2 %leaf_edge.1 = (bf16[8,256,256]{2,1,0:T(8,128)(2,1)S(1)}, bf16[256,256]{1,0:T(8,128)(2,1)S(1)}, bf16[256,256]{1,0:T(8,128)(2,1)S(1)}, bf16[256,256]{1,0:T(8,128)(2,1)S(1)}) custom-call(s32[4,8]{1,0:T(4,128)} %bitcast.1, s32[1]{0:T(128)S(6)} %copy.12.link, bf16[12,256,256]{2,1,0:T(8,128)(2,1)} %rhs.5, bf16[12,256,256]{2,1,0:T(8,128)(2,1)} %inverse.5, ...), custom_call_target="tpu_custom_call" | custom-call | tf_op jit(solution)/shard_map/leaf_edge/pallas_call | solution.py:109
  5.5 0.5 %collective-permute-start.2 = (bf16[256,256]{1,0:T(8,128)(2,1)S(1)}, bf16[256,256]{1,0:T(8,128)(2,1)S(1)}, u32[]{:S(2)}, u32[]{:S(2)}) collective-permute-start(bf16[256,256]{1,0:T(8,128)(2,1)S(1)} %get-tuple-element.14.edge), channel_id=1, source_target_pairs={{0,1},{1,0},{2,3},{3,2},{4,5},{5,4},{6,7},{7,6},{8,9},{9,8},{10,11... | collective-permute-start | bytes 393224 | tf_op jit(solution)/shard_map/ppermute | solution.py:42
  6.1 0.9 %collective-permute-done.2.lower = bf16[256,256]{1,0:T(8,128)(2,1)S(1)} collective-permute-done((bf16[256,256]{1,0:T(8,128)(2,1)S(1)}, bf16[256,256]{1,0:T(8,128)(2,1)S(1)}, u32[]{:S(2)}, u32[]{:S(2)}) %collective-permute-start.2) | collective-permute-done | bytes 131104 | tf_op jit(solution)/shard_map/ppermute | solution.py:42
  7.0 0.2 level0_early.1._
  7.2 1.8 %collective-permute-start.3 = (bf16[256,256]{1,0:T(8,128)(2,1)S(1)}, bf16[256,256]{1,0:T(8,128)(2,1)S(1)}, u32[]{:S(2)}, u32[]{:S(2)}) collective-permute-start(bf16[256,256]{1,0:T(8,128)(2,1)S(1)} %level0_early.1._), channel_id=1, source_target_pairs={{0,1},{1,2},{2,3},{3,4},{4,5},{5,6},{6,7},{7,8},{8,9},{9,10},{10,1... | collective-permute-start | bytes 393224 | tf_op jit(solution)/shard_map/ppermute | solution.py:22
  9.0 4.0 %collective-permute-start.4 = (bf16[256,256]{1,0:T(8,128)(2,1)S(1)}, bf16[256,256]{1,0:T(8,128)(2,1)S(1)}, u32[]{:S(2)}, u32[]{:S(2)}) collective-permute-start(bf16[256,256]{1,0:T(8,128)(2,1)S(1)} %get-tuple-element.12.down), channel_id=1, source_target_pairs={{0,15},{1,0},{2,1},{3,2},{4,3},{5,4},{6,5},{7,6},{8,7},{9,8},{10,9... | collective-permute-start | bytes 393224 | tf_op jit(solution)/shard_map/ppermute | solution.py:22
  13.0 0.4 %collective-permute-start.5 = (bf16[256,256]{1,0:T(8,128)(2,1)S(1)}, bf16[256,256]{1,0:T(8,128)(2,1)S(1)}, u32[]{:S(2)}, u32[]{:S(2)}) collective-permute-start(bf16[256,256]{1,0:T(8,128)(2,1)S(1)} %get-tuple-element.13.lower_mat), channel_id=1, source_target_pairs={{0,15},{1,0},{2,1},{3,2},{4,3},{5,4},{6,5},{7,6},{8,7},{9,8},{10,9... | collective-permute-start | bytes 393224 | tf_op jit(solution)/shard_map/ppermute | solution.py:22
  13.5 1.0 %collective-permute-done.lower = bf16[256,256]{1,0:T(8,128)(2,1)S(1)} collective-permute-done((bf16[256,256]{1,0:T(8,128)(2,1)S(1)}, bf16[256,256]{1,0:T(8,128)(2,1)S(1)}, u32[]{:S(2)}, u32[]{:S(2)}) %collective-permute-start) | collective-permute-done | bytes 131104 | tf_op jit(solution)/shard_map/ppermute | solution.py:22
  14.5 0.2 level0_late.1.refs_0_
  14.8 0.5 %fold.1 = (bf16[3,256,256]{2,1,0:T(8,128)(2,1)S(1)}, bf16[3,256,256]{2,1,0:T(8,128)(2,1)S(1)}, f32[3,256,256]{2,1,0:T(8,128)S(1)}) custom-call(bf16[4,1,256,256]{3,2,1,0:T(8,128)(2,1)S(1)} %copy-done.1, bf16[4,1,256,256]{3,2,1,0:T(8,128)(2,1)S(1)} %copy-done.2, bf16[4,1,2,256,256]{4,3,2,1,0:T(8,128)(2,1)S(1)} %copy-done, bf16[256,256]{1,0:T(8,128)(2,1)S(1)} %level0_early.1._), custom_call_target="tpu_custom_call" | custom-call | flops 301989888 | bytes 3145728 | tf_op jit(solution)/shard_map/fold/pallas_call | solution.py:252
  15.2 0.6 %collective-permute-done.3.below = bf16[256,256]{1,0:T(8,128)(2,1)S(1)} collective-permute-done((bf16[256,256]{1,0:T(8,128)(2,1)S(1)}, bf16[256,256]{1,0:T(8,128)(2,1)S(1)}, u32[]{:S(2)}, u32[]{:S(2)}) %collective-permute-start.3) | collective-permute-done | bytes 131104 | tf_op jit(solution)/shard_map/ppermute | solution.py:22
  15.9 0.2 level1_below.1.part
  16.1 0.8 %collective-permute-done.5.above_mat = bf16[256,256]{1,0:T(8,128)(2,1)S(1)} collective-permute-done((bf16[256,256]{1,0:T(8,128)(2,1)S(1)}, bf16[256,256]{1,0:T(8,128)(2,1)S(1)}, u32[]{:S(2)}, u32[]{:S(2)}) %collective-permute-start.5) | collective-permute-done | bytes 131104 | tf_op jit(solution)/shard_map/ppermute | solution.py:22
  16.9 0.2 level1.1._.refs_1_
  17.1 1.3 %collective-permute-start.6 = (bf16[256,256]{1,0:T(8,128)(2,1)S(1)}, bf16[256,256]{1,0:T(8,128)(2,1)S(1)}, u32[]{:S(2)}, u32[]{:S(2)}) collective-permute-start(bf16[256,256]{1,0:T(8,128)(2,1)S(1)} %level1.1._.refs_1_), channel_id=1, source_target_pairs={{0,2},{1,3},{2,4},{3,5},{4,6},{5,7},{6,8},{7,9},{8,10},{9,11},{10,... | collective-permute-start | bytes 393224 | tf_op jit(solution)/shard_map/ppermute | solution.py:22
  18.4 3.5 %collective-permute-start.7 = (bf16[256,256]{1,0:T(8,128)(2,1)S(1)}, bf16[256,256]{1,0:T(8,128)(2,1)S(1)}, u32[]{:S(2)}, u32[]{:S(2)}) collective-permute-start(bf16[256,256]{1,0:T(8,128)(2,1)S(1)} %level1.1._.refs_1_), channel_id=1, source_target_pairs={{0,14},{1,15},{2,0},{3,1},{4,2},{5,3},{6,4},{7,5},{8,6},{9,7},{10,... | collective-permute-start | bytes 393224 | tf_op jit(solution)/shard_map/ppermute | solution.py:22
  21.9 3.3 %leaf_rest.1.rest_0_.top = bf16[4,256,256]{2,1,0:T(8,128)(2,1)S(1)} custom-call(s32[4,8]{1,0:T(4,128)} %bitcast.2, bf16[12,256,256]{2,1,0:T(8,128)(2,1)} %rhs.5, bf16[12,256,256]{2,1,0:T(8,128)(2,1)} %inverse.5, bf16[8,4,256,256]{3,2,1,0:T(8,128)(2,1)} %factor.5, bf16[8,256,256]{2,1,0:T(8,128)(2,1)S(1)} %get-tuple-element.11.low, ...), custom_call_target="tpu_custom_call" | custom-call | flops 671088640 | bytes 4718592 | tf_op jit(solution)/shard_map/leaf_rest/pallas_call | solution.py:220
  25.2 0.3 collective-permute-done.6.lower
  25.5 1.9 %collective-permute-done.7.upper = bf16[256,256]{1,0:T(8,128)(2,1)S(1)} collective-permute-done((bf16[256,256]{1,0:T(8,128)(2,1)S(1)}, bf16[256,256]{1,0:T(8,128)(2,1)S(1)}, u32[]{:S(2)}, u32[]{:S(2)}) %collective-permute-start.7) | collective-permute-done | bytes 131104 | tf_op jit(solution)/shard_map/ppermute | solution.py:22
  27.4 0.2 level2.1.refs_2_
  27.7 3.8 %collective-permute-start.9 = (bf16[256,256]{1,0:T(8,128)(2,1)S(1)}, bf16[256,256]{1,0:T(8,128)(2,1)S(1)}, u32[]{:S(2)}, u32[]{:S(2)}) collective-permute-start(bf16[256,256]{1,0:T(8,128)(2,1)S(1)} %level2.1.refs_2_), channel_id=1, source_target_pairs={{0,12},{1,13},{2,14},{3,15},{4,0},{5,1},{6,2},{7,3},{8,4},{9,5},{1... | collective-permute-start | bytes 393224 | tf_op jit(solution)/shard_map/ppermute | solution.py:22
  31.5 1.3 %collect.1 = (bf16[12,256,256]{2,1,0:T(8,128)(2,1)}, bf16[4,1,256,256]{3,2,1,0:T(8,128)(2,1)}) custom-call(bf16[8,256,256]{2,1,0:T(8,128)(2,1)S(1)} %get-tuple-element.11.low, bf16[4,256,256]{2,1,0:T(8,128)(2,1)S(1)} %leaf_rest.1.rest_0_.top, bf16[256,256]{1,0:T(8,128)(2,1)S(1)} %level0_late.1.refs_0_, bf16[256,256]{1,0:T(8,128)(2,1)S(1)} %level1.1._.refs_1_, ...), custom_call_target="tpu_custom_call" | custom-call | bytes 3932160 | tf_op jit(solution)/shard_map/collect/pallas_call | solution.py:293
  32.8 3.0 %collective-permute-done.8.lower = bf16[256,256]{1,0:T(8,128)(2,1)S(1)} collective-permute-done((bf16[256,256]{1,0:T(8,128)(2,1)S(1)}, bf16[256,256]{1,0:T(8,128)(2,1)S(1)}, u32[]{:S(2)}, u32[]{:S(2)}) %collective-permute-start.8) | collective-permute-done | bytes 131104 | tf_op jit(solution)/shard_map/ppermute | solution.py:22
  35.8 0.9 %node_last.1 = bf16[4,1,256,256]{3,2,1,0:T(8,128)(2,1)} custom-call(bf16[256,256]{1,0:T(8,128)(2,1)S(1)} %collective-permute-done.8.lower, bf16[256,256]{1,0:T(8,128)(2,1)S(1)} %collective-permute-done.9.upper, bf16[3,256,256]{2,1,0:T(8,128)(2,1)S(1)} %get-tuple-element.15.lower_mat, ...), custom_call_target="tpu_custom_call", output_to_operand_aliasing={{}: (5, {})} | custom-call | tf_op jit(solution)/shard_map/node_last/pallas_call | solution.py:334
  (13 shorter events, 0.2 us)
Async XLA Ops:
  1.3 13.5 %copy-start.1 = (bf16[4,1,256,256]{3,2,1,0:T(8,128)(2,1)S(1)}, bf16[4,1,256,256]{3,2,1,0:T(8,128)(2,1)}, u32[]{:S(2)}) copy-start(bf16[4,1,256,256]{3,2,1,0:T(8,128)(2,1)} %rhs.4) | copy-start | bytes 1572868
  1.3 13.5 %copy-start.2 = (bf16[4,1,256,256]{3,2,1,0:T(8,128)(2,1)S(1)}, bf16[4,1,256,256]{3,2,1,0:T(8,128)(2,1)}, u32[]{:S(2)}) copy-start(bf16[4,1,256,256]{3,2,1,0:T(8,128)(2,1)} %inverse.4) | copy-start | bytes 1572868
  5.5 9.2 %copy-start = (bf16[4,1,2,256,256]{4,3,2,1,0:T(8,128)(2,1)S(1)}, bf16[4,1,2,256,256]{4,3,2,1,0:T(8,128)(2,1)}, u32[]{:S(2)}) copy-start(bf16[4,1,2,256,256]{4,3,2,1,0:T(8,128)(2,1)} %factor.4) | copy-start | bytes 3145732
  5.5 1.5 %collective-permute-start.2 = (bf16[256,256]{1,0:T(8,128)(2,1)S(1)}, bf16[256,256]{1,0:T(8,128)(2,1)S(1)}, u32[]{:S(2)}, u32[]{:S(2)}) collective-permute-start(bf16[256,256]{1,0:T(8,128)(2,1)S(1)} %get-tuple-element.14.edge), channel_id=1, source_target_pairs={{0,1},{1,0},{2,3},{3,2},{4,5},{5,4},{6,7},{7,6},{8,9},{9,8},{10,11... | collective-permute-start | bytes 393224 | tf_op jit(solution)/shard_map/ppermute | solution.py:42
  6.0 8.4 %collective-permute-start = (bf16[256,256]{1,0:T(8,128)(2,1)S(1)}, bf16[256,256]{1,0:T(8,128)(2,1)S(1)}, u32[]{:S(2)}, u32[]{:S(2)}) collective-permute-start(bf16[256,256]{1,0:T(8,128)(2,1)S(1)} %get-tuple-element.14.edge), channel_id=1, source_target_pairs={{0,1},{1,2},{2,3},{3,4},{4,5},{5,6},{6,7},{7,8},{8,9},{9,10},{10,1... | collective-permute-start | bytes 393224 | tf_op jit(solution)/shard_map/ppermute | solution.py:22
  7.2 8.6 %collective-permute-start.3 = (bf16[256,256]{1,0:T(8,128)(2,1)S(1)}, bf16[256,256]{1,0:T(8,128)(2,1)S(1)}, u32[]{:S(2)}, u32[]{:S(2)}) collective-permute-start(bf16[256,256]{1,0:T(8,128)(2,1)S(1)} %level0_early.1._), channel_id=1, source_target_pairs={{0,1},{1,2},{2,3},{3,4},{4,5},{5,6},{6,7},{7,8},{8,9},{9,10},{10,1... | collective-permute-start | bytes 393224 | tf_op jit(solution)/shard_map/ppermute | solution.py:22
  9.0 7.1 %collective-permute-start.4 = (bf16[256,256]{1,0:T(8,128)(2,1)S(1)}, bf16[256,256]{1,0:T(8,128)(2,1)S(1)}, u32[]{:S(2)}, u32[]{:S(2)}) collective-permute-start(bf16[256,256]{1,0:T(8,128)(2,1)S(1)} %get-tuple-element.12.down), channel_id=1, source_target_pairs={{0,15},{1,0},{2,1},{3,2},{4,3},{5,4},{6,5},{7,6},{8,7},{9,8},{10,9... | collective-permute-start | bytes 393224 | tf_op jit(solution)/shard_map/ppermute | solution.py:22
  13.0 3.9 %collective-permute-start.5 = (bf16[256,256]{1,0:T(8,128)(2,1)S(1)}, bf16[256,256]{1,0:T(8,128)(2,1)S(1)}, u32[]{:S(2)}, u32[]{:S(2)}) collective-permute-start(bf16[256,256]{1,0:T(8,128)(2,1)S(1)} %get-tuple-element.13.lower_mat), channel_id=1, source_target_pairs={{0,15},{1,0},{2,1},{3,2},{4,3},{5,4},{6,5},{7,6},{8,7},{9,8},{10,9... | collective-permute-start | bytes 393224 | tf_op jit(solution)/shard_map/ppermute | solution.py:22
  14.7 2.3 %collective-permute-start.1 = (bf16[256,256]{1,0:T(8,128)(2,1)S(1)}, bf16[256,256]{1,0:T(8,128)(2,1)S(1)}, u32[]{:S(2)}, u32[]{:S(2)}) collective-permute-start(bf16[256,256]{1,0:T(8,128)(2,1)S(1)} %level0_late.1.refs_0_), channel_id=1, source_target_pairs={{0,1},{1,0},{2,3},{3,2},{4,5},{5,4},{6,7},{7,6},{8,9},{9,8},{10,11... | collective-permute-start | bytes 393224 | tf_op jit(solution)/shard_map/ppermute | solution.py:42
  17.1 8.3 %collective-permute-start.6 = (bf16[256,256]{1,0:T(8,128)(2,1)S(1)}, bf16[256,256]{1,0:T(8,128)(2,1)S(1)}, u32[]{:S(2)}, u32[]{:S(2)}) collective-permute-start(bf16[256,256]{1,0:T(8,128)(2,1)S(1)} %level1.1._.refs_1_), channel_id=1, source_target_pairs={{0,2},{1,3},{2,4},{3,5},{4,6},{5,7},{6,8},{7,9},{8,10},{9,11},{10,... | collective-permute-start | bytes 393224 | tf_op jit(solution)/shard_map/ppermute | solution.py:22
  18.4 8.9 %collective-permute-start.7 = (bf16[256,256]{1,0:T(8,128)(2,1)S(1)}, bf16[256,256]{1,0:T(8,128)(2,1)S(1)}, u32[]{:S(2)}, u32[]{:S(2)}) collective-permute-start(bf16[256,256]{1,0:T(8,128)(2,1)S(1)} %level1.1._.refs_1_), channel_id=1, source_target_pairs={{0,14},{1,15},{2,0},{3,1},{4,2},{5,3},{6,4},{7,5},{8,6},{9,7},{10,... | collective-permute-start | bytes 393224 | tf_op jit(solution)/shard_map/ppermute | solution.py:22
  27.6 8.2 %collective-permute-start.8 = (bf16[256,256]{1,0:T(8,128)(2,1)S(1)}, bf16[256,256]{1,0:T(8,128)(2,1)S(1)}, u32[]{:S(2)}, u32[]{:S(2)}) collective-permute-start(bf16[256,256]{1,0:T(8,128)(2,1)S(1)} %level2.1.refs_2_), channel_id=1, source_target_pairs={{0,4},{1,5},{2,6},{3,7},{4,8},{5,9},{6,10},{7,11},{8,12},{9,13},{1... | collective-permute-start | bytes 393224 | tf_op jit(solution)/shard_map/ppermute | solution.py:22
  27.7 8.2 %collective-permute-start.9 = (bf16[256,256]{1,0:T(8,128)(2,1)S(1)}, bf16[256,256]{1,0:T(8,128)(2,1)S(1)}, u32[]{:S(2)}, u32[]{:S(2)}) collective-permute-start(bf16[256,256]{1,0:T(8,128)(2,1)S(1)} %level2.1.refs_2_), channel_id=1, source_target_pairs={{0,12},{1,13},{2,14},{3,15},{4,0},{5,1},{6,2},{7,3},{8,4},{9,5},{1... | collective-permute-start | bytes 393224 | tf_op jit(solution)/shard_map/ppermute | solution.py:22

commit v5 on v4

--- a/solution.py
+++ b/solution.py
@@ -24,6 +24,19 @@
 
 def in_hbm(array):
     return pltpu.with_memory_space_constraint(array, pltpu.HBM)
+
+
+def edge_swap(value, axis, stride, odd):
+    length = lax.axis_size(axis)
+    pairs = []
+    for i in range(length):
+        step = stride if (i // stride % 2 == 0) != odd else -stride
+        pairs.append((i, (i + step) % length))
+    return lax.ppermute(value, axis, pairs)
+
+
+def stride_bit(stride):
+    return lax.rem(lax.div(lax.axis_index("rows"), stride), 2)
 
 
 def mm(a, b):
@@ -268,9 +281,29 @@
     )(rhs, inverse, factor, after)
 
 
-def node_kernel(h, lower, upper, lower_mat, upper_mat, const, *rest):
-    total = const[h] - mm(upper_mat[h], upper[...]) - mm(lower_mat[h], lower[...])
-    rest[-1][...] = total.astype(BF16)
+def node_total(h, rows, first, second, lower_mat, upper_mat, const, out, stride, swapped):
+    def total(first_mat, second_mat):
+        value = const[h, rows] - mm(first_mat[h, rows], first[...])
+        out[rows] = (value - mm(second_mat[h, rows], second[...])).astype(BF16)
+
+    if swapped is None:
+        total(upper_mat, lower_mat)
+        return
+    if not swapped:
+        total(lower_mat, upper_mat)
+        return
+    bit = stride_bit(stride)
+    pl.when(bit == 1)(lambda: total(lower_mat, upper_mat))
+    pl.when(bit == 0)(lambda: total(upper_mat, lower_mat))
+
+
+def node_kernel(
+    h, stride, swapped, first, second, lower_mat, upper_mat, const, *rest
+):
+    rows = pl.ds(0, const.shape[1])
+    node_total(
+        h, rows, first, second, lower_mat, upper_mat, const, rest[-1], stride, swapped
+    )
 
 
 def collect_kernel(low, top, *refs):
@@ -309,20 +342,19 @@
     )(low, top, *levels)
 
 
-def last_kernel(lower, upper, lower_mat, upper_mat, const, _, out, piece, sem):
+def last_kernel(
+    stride, swapped, first, second, lower_mat, upper_mat, const, _, out, piece, sem
+):
     h = const.shape[0] - 1
-    rows = const.shape[1] // 2
+    size = const.shape[1] // 2
     copies = []
     for half in range(2):
-        part = pl.ds(half * rows, rows)
-        total = (
-            const[h, part]
-            - mm(upper_mat[h, part], upper[...])
-            - mm(lower_mat[h, part], lower[...])
+        rows = pl.ds(half * size, size)
+        node_total(
+            h, rows, first, second, lower_mat, upper_mat, const, piece, stride, swapped
         )
-        piece[part] = total.astype(BF16)
         copy = pltpu.make_async_copy(
-            piece.at[part], out.at[out.shape[0] - 1, 0, part], sem.at[half]
+            piece.at[rows], out.at[out.shape[0] - 1, 0, rows], sem.at[half]
         )
         copy.start()
         copies.append(copy)
@@ -330,17 +362,17 @@
         copy.wait()
 
 
-def last_call(lower, upper, lower_mat, upper_mat, const, collected):
-    return pl.pallas_call(
-        last_kernel,
+def last_call(stride, swapped, first, second, lower_mat, upper_mat, const, collected):
+    return pl.pallas_call(
+        functools.partial(last_kernel, stride, swapped),
         out_shape=jax.ShapeDtypeStruct(collected.shape, BF16),
         in_specs=[VMEM] * 5 + [HBM],
         out_specs=HBM,
         input_output_aliases={5: 0},
-        scratch_shapes=[pltpu.VMEM(lower.shape, BF16), pltpu.SemaphoreType.DMA((2,))],
+        scratch_shapes=[pltpu.VMEM(first.shape, BF16), pltpu.SemaphoreType.DMA((2,))],
         compiler_params=pltpu.CompilerParams(vmem_limit_bytes=8 << 20),
         name="node_last",
-    )(lower, upper, lower_mat, upper_mat, const, collected)
+    )(first, second, lower_mat, upper_mat, const, collected)
 
 
 def shards(
@@ -384,14 +416,22 @@
     depth = separator_rhs.shape[0]
     for height in range(2, depth):
         stride = 2 ** (height - 1)
-        lower = passed_along(block, "rows", stride)
-        upper = passed_along(block, "rows", -stride)
-        if height < depth - 1:
-            step = functools.partial(node_kernel, height - 1)
-            block = small_call(step, f"level{height}", shape, lower, upper, *mats, top)
+        last = height == depth - 1
+        swapped = not last
+        if swapped:
+            first = edge_swap(block, "rows", stride, False)
+            second = edge_swap(block, "rows", stride, True)
+        else:
+            first = passed_along(block, "rows", -stride)
+            second = passed_along(block, "rows", stride)
+        if not swapped:
+            swapped = None
+        if not last:
+            step = functools.partial(node_kernel, height - 1, stride, swapped)
+            block = small_call(step, f"level{height}", shape, first, second, *mats, top)
             levels.append(block)
     solved, collected = collect_call(low, top, levels, (depth, 1) + shape)
-    return solved, last_call(lower, upper, *mats, collected)
+    return solved, last_call(stride, swapped, first, second, *mats, collected)
 
 
 def solution(mesh):

time: 36.9 us -> 36.7 us (level)
  starting transfers between devices: 15.5 us -> 12.3 us
  waiting for transfers between devices: 8.57 us -> 11.6 us
    ppermute x8 -> x6, starting transfers between devices: 14.9 us -> 8.37 us  [passed_along(): lax.ppermute(value, axis, [(i, (i + by) % length) for i in range(length)])]
    ppermute x0 -> x2, waiting for transfers between devices: none -> 3.46 us  [edge_swap(): return lax.ppermute(value, axis, pairs)]
    ppermute x0 -> x2, starting transfers between devices: none -> 3.39 us  [edge_swap(): return lax.ppermute(value, axis, pairs)]
    ppermute x8 -> x6, waiting for transfers between devices: 7.65 us -> 7.22 us  [passed_along(): lax.ppermute(value, axis, [(i, (i + by) % length) for i in range(length)])]
where the time goes in v5:
time: 36.7 us; the launch traced here: 36.5 us
  starting transfers between devices  12.3 us (34%)
  waiting for transfers between devices  11.6 us (32%)
  Pallas kernels  11.1 us (30%)
  between operations  1.43 us (4%)
    ppermute x6, starting transfers between devices, passed_along(): lax.ppermute(value, axis, [(i, (i + by) % length) for i in range(length)])  8.37 us
    ppermute x6, waiting for transfers between devices, passed_along(): lax.ppermute(value, axis, [(i, (i + by) % length) for i in range(length)])  7.22 us
    pallas_call x1, Pallas kernels, edge_call(): pl.pallas_call(edge_kernel, out_shape=(pltpu.VMEM((2 * n, block, loads),...  4.21 us
    ppermute x2, waiting for transfers between devices, edge_swap(): return lax.ppermute(value, axis, pairs)  3.46 us
    ppermute x2, starting transfers between devices, edge_swap(): return lax.ppermute(value, axis, pairs)  3.39 us
    pallas_call x1, Pallas kernels, rest_call(): pl.pallas_call(rest_kernel, out_shape=pltpu.VMEM((n, block, loads), BF16)...  3.26 us
    pallas_call x1, Pallas kernels, collect_call(): pl.pallas_call(collect_kernel, out_shape=(jax.ShapeDtypeStruct((rows,) +...  1.31 us
    pallas_call x6, Pallas kernels, small_call(): pl.pallas_call(kernel, out_shape=pltpu.VMEM(shape, dtype), in_specs=[VMEM...  1 us
  transfers between devices with their start and end apart: 10, of which 7 were waited for; matrix products, arithmetic and copies ran while one was open for 0% of the time, Pallas kernels for 15%

profile of v5, /device:TPU:0, one launch (start us, length us, event | category | flops | bytes accessed | tf_op | source)
XLA Modules:
  0.0 36.5 jit_solution(14813450594143453388)
XLA Ops:
  1.3 4.2 %leaf_edge.1 = (bf16[8,256,256]{2,1,0:T(8,128)(2,1)S(1)}, bf16[256,256]{1,0:T(8,128)(2,1)S(1)}, bf16[256,256]{1,0:T(8,128)(2,1)S(1)}, bf16[256,256]{1,0:T(8,128)(2,1)S(1)}) custom-call(s32[4,8]{1,0:T(4,128)} %bitcast.1, s32[1]{0:T(128)S(6)} %copy.12.link, bf16[12,256,256]{2,1,0:T(8,128)(2,1)} %rhs.5, bf16[12,256,256]{2,1,0:T(8,128)(2,1)} %inverse.5, ...), custom_call_target="tpu_custom_call" | custom-call | tf_op jit(solution)/shard_map/leaf_edge/pallas_call | solution.py:122
  5.5 0.5 %collective-permute-start.2 = (bf16[256,256]{1,0:T(8,128)(2,1)S(1)}, bf16[256,256]{1,0:T(8,128)(2,1)S(1)}, u32[]{:S(2)}, u32[]{:S(2)}) collective-permute-start(bf16[256,256]{1,0:T(8,128)(2,1)S(1)} %get-tuple-element.14.edge), channel_id=1, source_target_pairs={{0,1},{1,0},{2,3},{3,2},{4,5},{5,4},{6,7},{7,6},{8,9},{9,8},{10,11... | collective-permute-start | bytes 393224 | tf_op jit(solution)/shard_map/ppermute | solution.py:55
  6.1 0.9 %collective-permute-done.2.lower = bf16[256,256]{1,0:T(8,128)(2,1)S(1)} collective-permute-done((bf16[256,256]{1,0:T(8,128)(2,1)S(1)}, bf16[256,256]{1,0:T(8,128)(2,1)S(1)}, u32[]{:S(2)}, u32[]{:S(2)}) %collective-permute-start.2) | collective-permute-done | bytes 131104 | tf_op jit(solution)/shard_map/ppermute | solution.py:55
  7.0 0.2 level0_early.1._
  7.2 1.8 %collective-permute-start.3 = (bf16[256,256]{1,0:T(8,128)(2,1)S(1)}, bf16[256,256]{1,0:T(8,128)(2,1)S(1)}, u32[]{:S(2)}, u32[]{:S(2)}) collective-permute-start(bf16[256,256]{1,0:T(8,128)(2,1)S(1)} %level0_early.1._), channel_id=1, source_target_pairs={{0,1},{1,2},{2,3},{3,4},{4,5},{5,6},{6,7},{7,8},{8,9},{9,10},{10,1... | collective-permute-start | bytes 393224 | tf_op jit(solution)/shard_map/ppermute | solution.py:22
  9.0 4.0 %collective-permute-start.4 = (bf16[256,256]{1,0:T(8,128)(2,1)S(1)}, bf16[256,256]{1,0:T(8,128)(2,1)S(1)}, u32[]{:S(2)}, u32[]{:S(2)}) collective-permute-start(bf16[256,256]{1,0:T(8,128)(2,1)S(1)} %get-tuple-element.12.down), channel_id=1, source_target_pairs={{0,15},{1,0},{2,1},{3,2},{4,3},{5,4},{6,5},{7,6},{8,7},{9,8},{10,9... | collective-permute-start | bytes 393224 | tf_op jit(solution)/shard_map/ppermute | solution.py:22
  13.0 0.4 %collective-permute-start.5 = (bf16[256,256]{1,0:T(8,128)(2,1)S(1)}, bf16[256,256]{1,0:T(8,128)(2,1)S(1)}, u32[]{:S(2)}, u32[]{:S(2)}) collective-permute-start(bf16[256,256]{1,0:T(8,128)(2,1)S(1)} %get-tuple-element.13.lower_mat), channel_id=1, source_target_pairs={{0,15},{1,0},{2,1},{3,2},{4,3},{5,4},{6,5},{7,6},{8,7},{9,8},{10,9... | collective-permute-start | bytes 393224 | tf_op jit(solution)/shard_map/ppermute | solution.py:22
  13.5 1.0 %collective-permute-done.lower = bf16[256,256]{1,0:T(8,128)(2,1)S(1)} collective-permute-done((bf16[256,256]{1,0:T(8,128)(2,1)S(1)}, bf16[256,256]{1,0:T(8,128)(2,1)S(1)}, u32[]{:S(2)}, u32[]{:S(2)}) %collective-permute-start) | collective-permute-done | bytes 131104 | tf_op jit(solution)/shard_map/ppermute | solution.py:22
  14.5 0.2 level0_late.1.refs_0_
  14.8 0.5 %fold.1 = (bf16[3,256,256]{2,1,0:T(8,128)(2,1)S(1)}, bf16[3,256,256]{2,1,0:T(8,128)(2,1)S(1)}, f32[3,256,256]{2,1,0:T(8,128)S(1)}) custom-call(bf16[4,1,256,256]{3,2,1,0:T(8,128)(2,1)S(1)} %copy-done.1, bf16[4,1,256,256]{3,2,1,0:T(8,128)(2,1)S(1)} %copy-done.2, bf16[4,1,2,256,256]{4,3,2,1,0:T(8,128)(2,1)S(1)} %copy-done, bf16[256,256]{1,0:T(8,128)(2,1)S(1)} %level0_early.1._), custom_call_target="tpu_custom_call" | custom-call | flops 301989888 | bytes 3145728 | tf_op jit(solution)/shard_map/fold/pallas_call | solution.py:265
  15.2 0.6 %collective-permute-done.3.below = bf16[256,256]{1,0:T(8,128)(2,1)S(1)} collective-permute-done((bf16[256,256]{1,0:T(8,128)(2,1)S(1)}, bf16[256,256]{1,0:T(8,128)(2,1)S(1)}, u32[]{:S(2)}, u32[]{:S(2)}) %collective-permute-start.3) | collective-permute-done | bytes 131104 | tf_op jit(solution)/shard_map/ppermute | solution.py:22
  15.9 0.2 level1_below.1.part
  16.1 0.8 %collective-permute-done.5.above_mat = bf16[256,256]{1,0:T(8,128)(2,1)S(1)} collective-permute-done((bf16[256,256]{1,0:T(8,128)(2,1)S(1)}, bf16[256,256]{1,0:T(8,128)(2,1)S(1)}, u32[]{:S(2)}, u32[]{:S(2)}) %collective-permute-start.5) | collective-permute-done | bytes 131104 | tf_op jit(solution)/shard_map/ppermute | solution.py:22
  16.9 0.2 level1.1._.refs_1_
  17.1 1.3 %collective-permute-start.6 = (bf16[256,256]{1,0:T(8,128)(2,1)S(1)}, bf16[256,256]{1,0:T(8,128)(2,1)S(1)}, u32[]{:S(2)}, u32[]{:S(2)}) collective-permute-start(bf16[256,256]{1,0:T(8,128)(2,1)S(1)} %level1.1._.refs_1_), channel_id=1, source_target_pairs={{0,2},{1,3},{2,0},{3,1},{4,6},{5,7},{6,4},{7,5},{8,10},{9,11},{10,... | collective-permute-start | bytes 393224 | tf_op jit(solution)/shard_map/ppermute | solution.py:35
  18.4 2.1 %collective-permute-start.7 = (bf16[256,256]{1,0:T(8,128)(2,1)S(1)}, bf16[256,256]{1,0:T(8,128)(2,1)S(1)}, u32[]{:S(2)}, u32[]{:S(2)}) collective-permute-start(bf16[256,256]{1,0:T(8,128)(2,1)S(1)} %level1.1._.refs_1_), channel_id=1, source_target_pairs={{0,14},{1,15},{2,4},{3,5},{4,2},{5,3},{6,8},{7,9},{8,6},{9,7},{10,... | collective-permute-start | bytes 393224 | tf_op jit(solution)/shard_map/ppermute | solution.py:35
  20.5 3.3 %leaf_rest.1.rest_0_.top = bf16[4,256,256]{2,1,0:T(8,128)(2,1)S(1)} custom-call(s32[4,8]{1,0:T(4,128)} %bitcast.2, bf16[12,256,256]{2,1,0:T(8,128)(2,1)} %rhs.5, bf16[12,256,256]{2,1,0:T(8,128)(2,1)} %inverse.5, bf16[8,4,256,256]{3,2,1,0:T(8,128)(2,1)} %factor.5, bf16[8,256,256]{2,1,0:T(8,128)(2,1)S(1)} %get-tuple-element.11.low, ...), custom_call_target="tpu_custom_call" | custom-call | flops 671088640 | bytes 4718592 | tf_op jit(solution)/shard_map/leaf_rest/pallas_call | solution.py:233
  23.8 1.3 %collective-permute-done.6.first = bf16[256,256]{1,0:T(8,128)(2,1)S(1)} collective-permute-done((bf16[256,256]{1,0:T(8,128)(2,1)S(1)}, bf16[256,256]{1,0:T(8,128)(2,1)S(1)}, u32[]{:S(2)}, u32[]{:S(2)}) %collective-permute-start.6) | collective-permute-done | bytes 131104 | tf_op jit(solution)/shard_map/ppermute | solution.py:35
  25.1 2.1 %collective-permute-done.7.second = bf16[256,256]{1,0:T(8,128)(2,1)S(1)} collective-permute-done((bf16[256,256]{1,0:T(8,128)(2,1)S(1)}, bf16[256,256]{1,0:T(8,128)(2,1)S(1)}, u32[]{:S(2)}, u32[]{:S(2)}) %collective-permute-start.7) | collective-permute-done | bytes 131104 | tf_op jit(solution)/shard_map/ppermute | solution.py:35
  27.3 0.2 level2.1.refs_2_
  27.6 2.0 %collective-permute-start.9 = (bf16[256,256]{1,0:T(8,128)(2,1)S(1)}, bf16[256,256]{1,0:T(8,128)(2,1)S(1)}, u32[]{:S(2)}, u32[]{:S(2)}) collective-permute-start(bf16[256,256]{1,0:T(8,128)(2,1)S(1)} %level2.1.refs_2_), channel_id=1, source_target_pairs={{0,4},{1,5},{2,6},{3,7},{4,8},{5,9},{6,10},{7,11},{8,12},{9,13},{1... | collective-permute-start | bytes 393224 | tf_op jit(solution)/shard_map/ppermute | solution.py:22
  29.6 1.3 %collect.1 = (bf16[12,256,256]{2,1,0:T(8,128)(2,1)}, bf16[4,1,256,256]{3,2,1,0:T(8,128)(2,1)}) custom-call(bf16[8,256,256]{2,1,0:T(8,128)(2,1)S(1)} %get-tuple-element.11.low, bf16[4,256,256]{2,1,0:T(8,128)(2,1)S(1)} %leaf_rest.1.rest_0_.top, bf16[256,256]{1,0:T(8,128)(2,1)S(1)} %level0_late.1.refs_0_, bf16[256,256]{1,0:T(8,128)(2,1)S(1)} %level1.1._.refs_1_, ...), custom_call_target="tpu_custom_call" | custom-call | bytes 3932160 | tf_op jit(solution)/shard_map/collect/pallas_call | solution.py:326
  30.9 4.8 %collective-permute-done.8.first = bf16[256,256]{1,0:T(8,128)(2,1)S(1)} collective-permute-done((bf16[256,256]{1,0:T(8,128)(2,1)S(1)}, bf16[256,256]{1,0:T(8,128)(2,1)S(1)}, u32[]{:S(2)}, u32[]{:S(2)}) %collective-permute-start.8) | collective-permute-done | bytes 131104 | tf_op jit(solution)/shard_map/ppermute | solution.py:22
  35.7 0.9 %node_last.1 = bf16[4,1,256,256]{3,2,1,0:T(8,128)(2,1)} custom-call(bf16[256,256]{1,0:T(8,128)(2,1)S(1)} %collective-permute-done.8.first, bf16[256,256]{1,0:T(8,128)(2,1)S(1)} %collective-permute-done.9.second, bf16[3,256,256]{2,1,0:T(8,128)(2,1)S(1)} %get-tuple-element.15.lower_mat, ...), custom_call_target="tpu_custom_call", output_to_operand_aliasing={{}: (5, {})} | custom-call | tf_op jit(solution)/shard_map/node_last/pallas_call | solution.py:366
  (13 shorter events, 0.2 us)
Async XLA Ops:
  1.3 13.5 %copy-start.1 = (bf16[4,1,256,256]{3,2,1,0:T(8,128)(2,1)S(1)}, bf16[4,1,256,256]{3,2,1,0:T(8,128)(2,1)}, u32[]{:S(2)}) copy-start(bf16[4,1,256,256]{3,2,1,0:T(8,128)(2,1)} %rhs.4) | copy-start | bytes 1572868
  1.3 13.5 %copy-start.2 = (bf16[4,1,256,256]{3,2,1,0:T(8,128)(2,1)S(1)}, bf16[4,1,256,256]{3,2,1,0:T(8,128)(2,1)}, u32[]{:S(2)}) copy-start(bf16[4,1,256,256]{3,2,1,0:T(8,128)(2,1)} %inverse.4) | copy-start | bytes 1572868
  5.5 9.2 %copy-start = (bf16[4,1,2,256,256]{4,3,2,1,0:T(8,128)(2,1)S(1)}, bf16[4,1,2,256,256]{4,3,2,1,0:T(8,128)(2,1)}, u32[]{:S(2)}) copy-start(bf16[4,1,2,256,256]{4,3,2,1,0:T(8,128)(2,1)} %factor.4) | copy-start | bytes 3145732
  5.5 1.5 %collective-permute-start.2 = (bf16[256,256]{1,0:T(8,128)(2,1)S(1)}, bf16[256,256]{1,0:T(8,128)(2,1)S(1)}, u32[]{:S(2)}, u32[]{:S(2)}) collective-permute-start(bf16[256,256]{1,0:T(8,128)(2,1)S(1)} %get-tuple-element.14.edge), channel_id=1, source_target_pairs={{0,1},{1,0},{2,3},{3,2},{4,5},{5,4},{6,7},{7,6},{8,9},{9,8},{10,11... | collective-permute-start | bytes 393224 | tf_op jit(solution)/shard_map/ppermute | solution.py:55
  6.0 8.4 %collective-permute-start = (bf16[256,256]{1,0:T(8,128)(2,1)S(1)}, bf16[256,256]{1,0:T(8,128)(2,1)S(1)}, u32[]{:S(2)}, u32[]{:S(2)}) collective-permute-start(bf16[256,256]{1,0:T(8,128)(2,1)S(1)} %get-tuple-element.14.edge), channel_id=1, source_target_pairs={{0,1},{1,2},{2,3},{3,4},{4,5},{5,6},{6,7},{7,8},{8,9},{9,10},{10,1... | collective-permute-start | bytes 393224 | tf_op jit(solution)/shard_map/ppermute | solution.py:22
  7.2 8.6 %collective-permute-start.3 = (bf16[256,256]{1,0:T(8,128)(2,1)S(1)}, bf16[256,256]{1,0:T(8,128)(2,1)S(1)}, u32[]{:S(2)}, u32[]{:S(2)}) collective-permute-start(bf16[256,256]{1,0:T(8,128)(2,1)S(1)} %level0_early.1._), channel_id=1, source_target_pairs={{0,1},{1,2},{2,3},{3,4},{4,5},{5,6},{6,7},{7,8},{8,9},{9,10},{10,1... | collective-permute-start | bytes 393224 | tf_op jit(solution)/shard_map/ppermute | solution.py:22
  9.0 7.1 %collective-permute-start.4 = (bf16[256,256]{1,0:T(8,128)(2,1)S(1)}, bf16[256,256]{1,0:T(8,128)(2,1)S(1)}, u32[]{:S(2)}, u32[]{:S(2)}) collective-permute-start(bf16[256,256]{1,0:T(8,128)(2,1)S(1)} %get-tuple-element.12.down), channel_id=1, source_target_pairs={{0,15},{1,0},{2,1},{3,2},{4,3},{5,4},{6,5},{7,6},{8,7},{9,8},{10,9... | collective-permute-start | bytes 393224 | tf_op jit(solution)/shard_map/ppermute | solution.py:22
  13.0 3.9 %collective-permute-start.5 = (bf16[256,256]{1,0:T(8,128)(2,1)S(1)}, bf16[256,256]{1,0:T(8,128)(2,1)S(1)}, u32[]{:S(2)}, u32[]{:S(2)}) collective-permute-start(bf16[256,256]{1,0:T(8,128)(2,1)S(1)} %get-tuple-element.13.lower_mat), channel_id=1, source_target_pairs={{0,15},{1,0},{2,1},{3,2},{4,3},{5,4},{6,5},{7,6},{8,7},{9,8},{10,9... | collective-permute-start | bytes 393224 | tf_op jit(solution)/shard_map/ppermute | solution.py:22
  14.7 2.3 %collective-permute-start.1 = (bf16[256,256]{1,0:T(8,128)(2,1)S(1)}, bf16[256,256]{1,0:T(8,128)(2,1)S(1)}, u32[]{:S(2)}, u32[]{:S(2)}) collective-permute-start(bf16[256,256]{1,0:T(8,128)(2,1)S(1)} %level0_late.1.refs_0_), channel_id=1, source_target_pairs={{0,1},{1,0},{2,3},{3,2},{4,5},{5,4},{6,7},{7,6},{8,9},{9,8},{10,11... | collective-permute-start | bytes 393224 | tf_op jit(solution)/shard_map/ppermute | solution.py:55
  17.1 8.0 %collective-permute-start.6 = (bf16[256,256]{1,0:T(8,128)(2,1)S(1)}, bf16[256,256]{1,0:T(8,128)(2,1)S(1)}, u32[]{:S(2)}, u32[]{:S(2)}) collective-permute-start(bf16[256,256]{1,0:T(8,128)(2,1)S(1)} %level1.1._.refs_1_), channel_id=1, source_target_pairs={{0,2},{1,3},{2,0},{3,1},{4,6},{5,7},{6,4},{7,5},{8,10},{9,11},{10,... | collective-permute-start | bytes 393224 | tf_op jit(solution)/shard_map/ppermute | solution.py:35
  18.4 8.8 %collective-permute-start.7 = (bf16[256,256]{1,0:T(8,128)(2,1)S(1)}, bf16[256,256]{1,0:T(8,128)(2,1)S(1)}, u32[]{:S(2)}, u32[]{:S(2)}) collective-permute-start(bf16[256,256]{1,0:T(8,128)(2,1)S(1)} %level1.1._.refs_1_), channel_id=1, source_target_pairs={{0,14},{1,15},{2,4},{3,5},{4,2},{5,3},{6,8},{7,9},{8,6},{9,7},{10,... | collective-permute-start | bytes 393224 | tf_op jit(solution)/shard_map/ppermute | solution.py:35
  27.5 8.2 %collective-permute-start.8 = (bf16[256,256]{1,0:T(8,128)(2,1)S(1)}, bf16[256,256]{1,0:T(8,128)(2,1)S(1)}, u32[]{:S(2)}, u32[]{:S(2)}) collective-permute-start(bf16[256,256]{1,0:T(8,128)(2,1)S(1)} %level2.1.refs_2_), channel_id=1, source_target_pairs={{0,12},{1,13},{2,14},{3,15},{4,0},{5,1},{6,2},{7,3},{8,4},{9,5},{1... | collective-permute-start | bytes 393224 | tf_op jit(solution)/shard_map/ppermute | solution.py:22
  27.6 8.1 %collective-permute-start.9 = (bf16[256,256]{1,0:T(8,128)(2,1)S(1)}, bf16[256,256]{1,0:T(8,128)(2,1)S(1)}, u32[]{:S(2)}, u32[]{:S(2)}) collective-permute-start(bf16[256,256]{1,0:T(8,128)(2,1)S(1)} %level2.1.refs_2_), channel_id=1, source_target_pairs={{0,4},{1,5},{2,6},{3,7},{4,8},{5,9},{6,10},{7,11},{8,12},{9,13},{1... | collective-permute-start | bytes 393224 | tf_op jit(solution)/shard_map/ppermute | solution.py:22

commit v6 on v5

--- a/solution.py
+++ b/solution.py
@@ -167,25 +167,14 @@
         out[...] = const[0] - mm(lower_mat[0], below[...])
 
 
-def across_kernel(part, above, above_mat, edge, upper_mat, out):
+def level_one_kernel(part, above, above_mat, edge, inner, lower_mat, upper_mat, out):
     odd = lax.rem(lax.axis_index("rows"), 2) == 1
 
     @pl.when(odd)
     def _():
+        total = part[...] - mm(lower_mat[0], inner[...])
         upper = (above[...].astype(F32) - mm(above_mat[...], edge[...])).astype(BF16)
-        out[...] = part[...] - mm(upper_mat[0], upper)
-
-    @pl.when(jnp.logical_not(odd))
-    def _():
-        out[...] = part[...]
-
-
-def level_one_kernel(inner, part, lower_mat, upper_mat, out):
-    odd = lax.rem(lax.axis_index("rows"), 2) == 1
-
-    @pl.when(odd)
-    def _():
-        out[...] = (part[...] - mm(lower_mat[0], inner[...])).astype(BF16)
+        out[...] = (total - mm(upper_mat[0], upper)).astype(BF16)
 
     @pl.when(jnp.logical_not(odd))
     def _():
@@ -406,11 +395,10 @@
     part = small_call(
         below_kernel, "level1_below", shape, below, mats[0], mats[2], dtype=F32
     )
-    part = small_call(
-        across_kernel, "level1_across", shape, part, above, above_mat, edge, mats[1],
-        dtype=F32,
-    )
-    block = small_call(level_one_kernel, "level1", shape, inner, part, *mats[:2])
+    block = small_call(
+        level_one_kernel, "level1", shape,
+        part, above, above_mat, edge, inner, mats[0], mats[1],
+    )
     top = rest_call(columns, leaf_rhs, leaf_inverse, leaf_factor, low, block)
     levels.append(block)
     depth = separator_rhs.shape[0]

time: 36.7 us -> 36.5 us (level)
    pallas_call x6 -> x5, Pallas kernels: 1 us -> 0.97 us  [small_call(): pl.pallas_call(kernel, out_shape=pltpu.VMEM(shape, dtype), in_specs=[VMEM...]
where the time goes in v6:
time: 36.5 us; the launch traced here: 36.3 us
  starting transfers between devices  12.4 us (34%)
  waiting for transfers between devices  11.4 us (31%)
  Pallas kernels  11.1 us (30%)
  between operations  1.42 us (4%)
    ppermute x6, starting transfers between devices, passed_along(): lax.ppermute(value, axis, [(i, (i + by) % length) for i in range(length)])  8.37 us
    ppermute x6, waiting for transfers between devices, passed_along(): lax.ppermute(value, axis, [(i, (i + by) % length) for i in range(length)])  7.18 us
    pallas_call x1, Pallas kernels, edge_call(): pl.pallas_call(edge_kernel, out_shape=(pltpu.VMEM((2 * n, block, loads),...  4.21 us
    ppermute x2, starting transfers between devices, edge_swap(): return lax.ppermute(value, axis, pairs)  3.4 us
    ppermute x2, waiting for transfers between devices, edge_swap(): return lax.ppermute(value, axis, pairs)  3.33 us
    pallas_call x1, Pallas kernels, rest_call(): pl.pallas_call(rest_kernel, out_shape=pltpu.VMEM((n, block, loads), BF16)...  3.26 us
    pallas_call x1, Pallas kernels, collect_call(): pl.pallas_call(collect_kernel, out_shape=(jax.ShapeDtypeStruct((rows,) +...  1.31 us
    pallas_call x5, Pallas kernels, small_call(): pl.pallas_call(kernel, out_shape=pltpu.VMEM(shape, dtype), in_specs=[VMEM...  0.97 us
  transfers between devices with their start and end apart: 10, of which 7 were waited for; matrix products, arithmetic and copies ran while one was open for 0% of the time, Pallas kernels for 15%

profile of v6, /device:TPU:0, one launch (start us, length us, event | category | flops | bytes accessed | tf_op | source)
XLA Modules:
  0.0 36.3 jit_solution(13898245068190394070)
XLA Ops:
  1.3 4.2 %leaf_edge.1 = (bf16[8,256,256]{2,1,0:T(8,128)(2,1)S(1)}, bf16[256,256]{1,0:T(8,128)(2,1)S(1)}, bf16[256,256]{1,0:T(8,128)(2,1)S(1)}, bf16[256,256]{1,0:T(8,128)(2,1)S(1)}) custom-call(s32[4,8]{1,0:T(4,128)} %bitcast.1, s32[1]{0:T(128)S(6)} %copy.12.link, bf16[12,256,256]{2,1,0:T(8,128)(2,1)} %rhs.5, bf16[12,256,256]{2,1,0:T(8,128)(2,1)} %inverse.5, ...), custom_call_target="tpu_custom_call" | custom-call | tf_op jit(solution)/shard_map/leaf_edge/pallas_call | solution.py:122
  5.5 0.5 %collective-permute-start = (bf16[256,256]{1,0:T(8,128)(2,1)S(1)}, bf16[256,256]{1,0:T(8,128)(2,1)S(1)}, u32[]{:S(2)}, u32[]{:S(2)}) collective-permute-start(bf16[256,256]{1,0:T(8,128)(2,1)S(1)} %get-tuple-element.14.edge), channel_id=1, source_target_pairs={{0,1},{1,0},{2,3},{3,2},{4,5},{5,4},{6,7},{7,6},{8,9},{9,8},{10,11... | collective-permute-start | bytes 393224 | tf_op jit(solution)/shard_map/ppermute | solution.py:55
  6.1 0.9 %collective-permute-done.lower = bf16[256,256]{1,0:T(8,128)(2,1)S(1)} collective-permute-done((bf16[256,256]{1,0:T(8,128)(2,1)S(1)}, bf16[256,256]{1,0:T(8,128)(2,1)S(1)}, u32[]{:S(2)}, u32[]{:S(2)}) %collective-permute-start) | collective-permute-done | bytes 131104 | tf_op jit(solution)/shard_map/ppermute | solution.py:55
  7.0 0.2 level0_early.1._
  7.2 1.8 %collective-permute-start.1 = (bf16[256,256]{1,0:T(8,128)(2,1)S(1)}, bf16[256,256]{1,0:T(8,128)(2,1)S(1)}, u32[]{:S(2)}, u32[]{:S(2)}) collective-permute-start(bf16[256,256]{1,0:T(8,128)(2,1)S(1)} %level0_early.1._), channel_id=1, source_target_pairs={{0,1},{1,2},{2,3},{3,4},{4,5},{5,6},{6,7},{7,8},{8,9},{9,10},{10,1... | collective-permute-start | bytes 393224 | tf_op jit(solution)/shard_map/ppermute | solution.py:22
  9.0 4.0 %collective-permute-start.2 = (bf16[256,256]{1,0:T(8,128)(2,1)S(1)}, bf16[256,256]{1,0:T(8,128)(2,1)S(1)}, u32[]{:S(2)}, u32[]{:S(2)}) collective-permute-start(bf16[256,256]{1,0:T(8,128)(2,1)S(1)} %get-tuple-element.12.down), channel_id=1, source_target_pairs={{0,15},{1,0},{2,1},{3,2},{4,3},{5,4},{6,5},{7,6},{8,7},{9,8},{10,9... | collective-permute-start | bytes 393224 | tf_op jit(solution)/shard_map/ppermute | solution.py:22
  13.0 0.4 %collective-permute-start.3 = (bf16[256,256]{1,0:T(8,128)(2,1)S(1)}, bf16[256,256]{1,0:T(8,128)(2,1)S(1)}, u32[]{:S(2)}, u32[]{:S(2)}) collective-permute-start(bf16[256,256]{1,0:T(8,128)(2,1)S(1)} %get-tuple-element.13.lower_mat), channel_id=1, source_target_pairs={{0,15},{1,0},{2,1},{3,2},{4,3},{5,4},{6,5},{7,6},{8,7},{9,8},{10,9... | collective-permute-start | bytes 393224 | tf_op jit(solution)/shard_map/ppermute | solution.py:22
  13.5 1.0 %collective-permute-done.4.lower = bf16[256,256]{1,0:T(8,128)(2,1)S(1)} collective-permute-done((bf16[256,256]{1,0:T(8,128)(2,1)S(1)}, bf16[256,256]{1,0:T(8,128)(2,1)S(1)}, u32[]{:S(2)}, u32[]{:S(2)}) %collective-permute-start.4) | collective-permute-done | bytes 131104 | tf_op jit(solution)/shard_map/ppermute | solution.py:22
  14.5 0.2 level0_late.1.refs_0_
  14.8 0.5 %fold.1 = (bf16[3,256,256]{2,1,0:T(8,128)(2,1)S(1)}, bf16[3,256,256]{2,1,0:T(8,128)(2,1)S(1)}, f32[3,256,256]{2,1,0:T(8,128)S(1)}) custom-call(bf16[4,1,256,256]{3,2,1,0:T(8,128)(2,1)S(1)} %copy-done.1, bf16[4,1,256,256]{3,2,1,0:T(8,128)(2,1)S(1)} %copy-done.2, bf16[4,1,2,256,256]{4,3,2,1,0:T(8,128)(2,1)S(1)} %copy-done, bf16[256,256]{1,0:T(8,128)(2,1)S(1)} %level0_early.1._), custom_call_target="tpu_custom_call" | custom-call | flops 301989888 | bytes 3145728 | tf_op jit(solution)/shard_map/fold/pallas_call | solution.py:254
  15.2 0.6 %collective-permute-done.1.below = bf16[256,256]{1,0:T(8,128)(2,1)S(1)} collective-permute-done((bf16[256,256]{1,0:T(8,128)(2,1)S(1)}, bf16[256,256]{1,0:T(8,128)(2,1)S(1)}, u32[]{:S(2)}, u32[]{:S(2)}) %collective-permute-start.1) | collective-permute-done | bytes 131104 | tf_op jit(solution)/shard_map/ppermute | solution.py:22
  15.9 0.2 level1_below.1.part
  16.1 0.8 %collective-permute-done.3.above_mat = bf16[256,256]{1,0:T(8,128)(2,1)S(1)} collective-permute-done((bf16[256,256]{1,0:T(8,128)(2,1)S(1)}, bf16[256,256]{1,0:T(8,128)(2,1)S(1)}, u32[]{:S(2)}, u32[]{:S(2)}) %collective-permute-start.3) | collective-permute-done | bytes 131104 | tf_op jit(solution)/shard_map/ppermute | solution.py:22
  16.9 0.2 level1.1._.refs_1_
  17.1 1.3 %collective-permute-start.6 = (bf16[256,256]{1,0:T(8,128)(2,1)S(1)}, bf16[256,256]{1,0:T(8,128)(2,1)S(1)}, u32[]{:S(2)}, u32[]{:S(2)}) collective-permute-start(bf16[256,256]{1,0:T(8,128)(2,1)S(1)} %level1.1._.refs_1_), channel_id=1, source_target_pairs={{0,2},{1,3},{2,0},{3,1},{4,6},{5,7},{6,4},{7,5},{8,10},{9,11},{10,... | collective-permute-start | bytes 393224 | tf_op jit(solution)/shard_map/ppermute | solution.py:35
  18.4 2.1 %collective-permute-start.7 = (bf16[256,256]{1,0:T(8,128)(2,1)S(1)}, bf16[256,256]{1,0:T(8,128)(2,1)S(1)}, u32[]{:S(2)}, u32[]{:S(2)}) collective-permute-start(bf16[256,256]{1,0:T(8,128)(2,1)S(1)} %level1.1._.refs_1_), channel_id=1, source_target_pairs={{0,14},{1,15},{2,4},{3,5},{4,2},{5,3},{6,8},{7,9},{8,6},{9,7},{10,... | collective-permute-start | bytes 393224 | tf_op jit(solution)/shard_map/ppermute | solution.py:35
  20.5 3.3 %leaf_rest.1.rest_0_.top = bf16[4,256,256]{2,1,0:T(8,128)(2,1)S(1)} custom-call(s32[4,8]{1,0:T(4,128)} %bitcast.2, bf16[12,256,256]{2,1,0:T(8,128)(2,1)} %rhs.5, bf16[12,256,256]{2,1,0:T(8,128)(2,1)} %inverse.5, bf16[8,4,256,256]{3,2,1,0:T(8,128)(2,1)} %factor.5, bf16[8,256,256]{2,1,0:T(8,128)(2,1)S(1)} %get-tuple-element.11.low, ...), custom_call_target="tpu_custom_call" | custom-call | flops 671088640 | bytes 4718592 | tf_op jit(solution)/shard_map/leaf_rest/pallas_call | solution.py:222
  23.8 1.2 %collective-permute-done.6.first = bf16[256,256]{1,0:T(8,128)(2,1)S(1)} collective-permute-done((bf16[256,256]{1,0:T(8,128)(2,1)S(1)}, bf16[256,256]{1,0:T(8,128)(2,1)S(1)}, u32[]{:S(2)}, u32[]{:S(2)}) %collective-permute-start.6) | collective-permute-done | bytes 131104 | tf_op jit(solution)/shard_map/ppermute | solution.py:35
  24.9 2.2 %collective-permute-done.7.second = bf16[256,256]{1,0:T(8,128)(2,1)S(1)} collective-permute-done((bf16[256,256]{1,0:T(8,128)(2,1)S(1)}, bf16[256,256]{1,0:T(8,128)(2,1)S(1)}, u32[]{:S(2)}, u32[]{:S(2)}) %collective-permute-start.7) | collective-permute-done | bytes 131104 | tf_op jit(solution)/shard_map/ppermute | solution.py:35
  27.1 0.2 level2.1.refs_2_
  27.4 2.0 %collective-permute-start.9 = (bf16[256,256]{1,0:T(8,128)(2,1)S(1)}, bf16[256,256]{1,0:T(8,128)(2,1)S(1)}, u32[]{:S(2)}, u32[]{:S(2)}) collective-permute-start(bf16[256,256]{1,0:T(8,128)(2,1)S(1)} %level2.1.refs_2_), channel_id=1, source_target_pairs={{0,4},{1,5},{2,6},{3,7},{4,8},{5,9},{6,10},{7,11},{8,12},{9,13},{1... | collective-permute-start | bytes 393224 | tf_op jit(solution)/shard_map/ppermute | solution.py:22
  29.4 1.3 %collect.1 = (bf16[12,256,256]{2,1,0:T(8,128)(2,1)}, bf16[4,1,256,256]{3,2,1,0:T(8,128)(2,1)}) custom-call(bf16[8,256,256]{2,1,0:T(8,128)(2,1)S(1)} %get-tuple-element.11.low, bf16[4,256,256]{2,1,0:T(8,128)(2,1)S(1)} %leaf_rest.1.rest_0_.top, bf16[256,256]{1,0:T(8,128)(2,1)S(1)} %level0_late.1.refs_0_, bf16[256,256]{1,0:T(8,128)(2,1)S(1)} %level1.1._.refs_1_, ...), custom_call_target="tpu_custom_call" | custom-call | bytes 3932160 | tf_op jit(solution)/shard_map/collect/pallas_call | solution.py:315
  30.7 4.7 %collective-permute-done.8.first = bf16[256,256]{1,0:T(8,128)(2,1)S(1)} collective-permute-done((bf16[256,256]{1,0:T(8,128)(2,1)S(1)}, bf16[256,256]{1,0:T(8,128)(2,1)S(1)}, u32[]{:S(2)}, u32[]{:S(2)}) %collective-permute-start.8) | collective-permute-done | bytes 131104 | tf_op jit(solution)/shard_map/ppermute | solution.py:22
  35.5 0.9 %node_last.1 = bf16[4,1,256,256]{3,2,1,0:T(8,128)(2,1)} custom-call(bf16[256,256]{1,0:T(8,128)(2,1)S(1)} %collective-permute-done.8.first, bf16[256,256]{1,0:T(8,128)(2,1)S(1)} %collective-permute-done.9.second, bf16[3,256,256]{2,1,0:T(8,128)(2,1)S(1)} %get-tuple-element.15.lower_mat, ...), custom_call_target="tpu_custom_call", output_to_operand_aliasing={{}: (5, {})} | custom-call | tf_op jit(solution)/shard_map/node_last/pallas_call | solution.py:355
  (12 shorter events, 0.2 us)
Async XLA Ops:
  1.3 13.5 %copy-start.1 = (bf16[4,1,256,256]{3,2,1,0:T(8,128)(2,1)S(1)}, bf16[4,1,256,256]{3,2,1,0:T(8,128)(2,1)}, u32[]{:S(2)}) copy-start(bf16[4,1,256,256]{3,2,1,0:T(8,128)(2,1)} %rhs.4) | copy-start | bytes 1572868
  1.3 13.5 %copy-start.2 = (bf16[4,1,256,256]{3,2,1,0:T(8,128)(2,1)S(1)}, bf16[4,1,256,256]{3,2,1,0:T(8,128)(2,1)}, u32[]{:S(2)}) copy-start(bf16[4,1,256,256]{3,2,1,0:T(8,128)(2,1)} %inverse.4) | copy-start | bytes 1572868
  5.5 9.2 %copy-start = (bf16[4,1,2,256,256]{4,3,2,1,0:T(8,128)(2,1)S(1)}, bf16[4,1,2,256,256]{4,3,2,1,0:T(8,128)(2,1)}, u32[]{:S(2)}) copy-start(bf16[4,1,2,256,256]{4,3,2,1,0:T(8,128)(2,1)} %factor.4) | copy-start | bytes 3145732
  5.5 1.5 %collective-permute-start = (bf16[256,256]{1,0:T(8,128)(2,1)S(1)}, bf16[256,256]{1,0:T(8,128)(2,1)S(1)}, u32[]{:S(2)}, u32[]{:S(2)}) collective-permute-start(bf16[256,256]{1,0:T(8,128)(2,1)S(1)} %get-tuple-element.14.edge), channel_id=1, source_target_pairs={{0,1},{1,0},{2,3},{3,2},{4,5},{5,4},{6,7},{7,6},{8,9},{9,8},{10,11... | collective-permute-start | bytes 393224 | tf_op jit(solution)/shard_map/ppermute | solution.py:55
  6.0 8.4 %collective-permute-start.4 = (bf16[256,256]{1,0:T(8,128)(2,1)S(1)}, bf16[256,256]{1,0:T(8,128)(2,1)S(1)}, u32[]{:S(2)}, u32[]{:S(2)}) collective-permute-start(bf16[256,256]{1,0:T(8,128)(2,1)S(1)} %get-tuple-element.14.edge), channel_id=1, source_target_pairs={{0,1},{1,2},{2,3},{3,4},{4,5},{5,6},{6,7},{7,8},{8,9},{9,10},{10,1... | collective-permute-start | bytes 393224 | tf_op jit(solution)/shard_map/ppermute | solution.py:22
  7.2 8.6 %collective-permute-start.1 = (bf16[256,256]{1,0:T(8,128)(2,1)S(1)}, bf16[256,256]{1,0:T(8,128)(2,1)S(1)}, u32[]{:S(2)}, u32[]{:S(2)}) collective-permute-start(bf16[256,256]{1,0:T(8,128)(2,1)S(1)} %level0_early.1._), channel_id=1, source_target_pairs={{0,1},{1,2},{2,3},{3,4},{4,5},{5,6},{6,7},{7,8},{8,9},{9,10},{10,1... | collective-permute-start | bytes 393224 | tf_op jit(solution)/shard_map/ppermute | solution.py:22
  9.0 7.1 %collective-permute-start.2 = (bf16[256,256]{1,0:T(8,128)(2,1)S(1)}, bf16[256,256]{1,0:T(8,128)(2,1)S(1)}, u32[]{:S(2)}, u32[]{:S(2)}) collective-permute-start(bf16[256,256]{1,0:T(8,128)(2,1)S(1)} %get-tuple-element.12.down), channel_id=1, source_target_pairs={{0,15},{1,0},{2,1},{3,2},{4,3},{5,4},{6,5},{7,6},{8,7},{9,8},{10,9... | collective-permute-start | bytes 393224 | tf_op jit(solution)/shard_map/ppermute | solution.py:22
  13.0 3.9 %collective-permute-start.3 = (bf16[256,256]{1,0:T(8,128)(2,1)S(1)}, bf16[256,256]{1,0:T(8,128)(2,1)S(1)}, u32[]{:S(2)}, u32[]{:S(2)}) collective-permute-start(bf16[256,256]{1,0:T(8,128)(2,1)S(1)} %get-tuple-element.13.lower_mat), channel_id=1, source_target_pairs={{0,15},{1,0},{2,1},{3,2},{4,3},{5,4},{6,5},{7,6},{8,7},{9,8},{10,9... | collective-permute-start | bytes 393224 | tf_op jit(solution)/shard_map/ppermute | solution.py:22
  14.7 2.2 %collective-permute-start.5 = (bf16[256,256]{1,0:T(8,128)(2,1)S(1)}, bf16[256,256]{1,0:T(8,128)(2,1)S(1)}, u32[]{:S(2)}, u32[]{:S(2)}) collective-permute-start(bf16[256,256]{1,0:T(8,128)(2,1)S(1)} %level0_late.1.refs_0_), channel_id=1, source_target_pairs={{0,1},{1,0},{2,3},{3,2},{4,5},{5,4},{6,7},{7,6},{8,9},{9,8},{10,11... | collective-permute-start | bytes 393224 | tf_op jit(solution)/shard_map/ppermute | solution.py:55
  17.1 7.8 %collective-permute-start.6 = (bf16[256,256]{1,0:T(8,128)(2,1)S(1)}, bf16[256,256]{1,0:T(8,128)(2,1)S(1)}, u32[]{:S(2)}, u32[]{:S(2)}) collective-permute-start(bf16[256,256]{1,0:T(8,128)(2,1)S(1)} %level1.1._.refs_1_), channel_id=1, source_target_pairs={{0,2},{1,3},{2,0},{3,1},{4,6},{5,7},{6,4},{7,5},{8,10},{9,11},{10,... | collective-permute-start | bytes 393224 | tf_op jit(solution)/shard_map/ppermute | solution.py:35
  18.4 8.7 %collective-permute-start.7 = (bf16[256,256]{1,0:T(8,128)(2,1)S(1)}, bf16[256,256]{1,0:T(8,128)(2,1)S(1)}, u32[]{:S(2)}, u32[]{:S(2)}) collective-permute-start(bf16[256,256]{1,0:T(8,128)(2,1)S(1)} %level1.1._.refs_1_), channel_id=1, source_target_pairs={{0,14},{1,15},{2,4},{3,5},{4,2},{5,3},{6,8},{7,9},{8,6},{9,7},{10,... | collective-permute-start | bytes 393224 | tf_op jit(solution)/shard_map/ppermute | solution.py:35
  27.3 8.1 %collective-permute-start.8 = (bf16[256,256]{1,0:T(8,128)(2,1)S(1)}, bf16[256,256]{1,0:T(8,128)(2,1)S(1)}, u32[]{:S(2)}, u32[]{:S(2)}) collective-permute-start(bf16[256,256]{1,0:T(8,128)(2,1)S(1)} %level2.1.refs_2_), channel_id=1, source_target_pairs={{0,12},{1,13},{2,14},{3,15},{4,0},{5,1},{6,2},{7,3},{8,4},{9,5},{1... | collective-permute-start | bytes 393224 | tf_op jit(solution)/shard_map/ppermute | solution.py:22
  27.4 8.1 %collective-permute-start.9 = (bf16[256,256]{1,0:T(8,128)(2,1)S(1)}, bf16[256,256]{1,0:T(8,128)(2,1)S(1)}, u32[]{:S(2)}, u32[]{:S(2)}) collective-permute-start(bf16[256,256]{1,0:T(8,128)(2,1)S(1)} %level2.1.refs_2_), channel_id=1, source_target_pairs={{0,4},{1,5},{2,6},{3,7},{4,8},{5,9},{6,10},{7,11},{8,12},{9,13},{1... | collective-permute-start | bytes 393224 | tf_op jit(solution)/shard_map/ppermute | solution.py:22

commit v7 on v6

--- a/solution.py
+++ b/solution.py
@@ -85,8 +85,10 @@
         load(columns, pattern),
         load(rhs.at[pl.ds(n, n)], rhs_v.at[pl.ds(n, n)]),
         load(inverse.at[pl.ds(n, n)], inv_v.at[pl.ds(n, n)]),
-        load(factor.at[pl.ds(0, n)], fac_v),
-    )
+    )
+    fac_in = [
+        load(factor.at[pl.ds(r, 2)], fac_v.at[pl.ds(r, 2)]) for r in range(0, n, 2)
+    ]
     last_in = (
         load(rhs.at[top], rhs_v.at[low]),
         load(factor.at[top - n], top_fac),
@@ -104,6 +106,8 @@
     for copy in next_in:
         copy.wait()
     for r in range(n):
+        if r % 2 == 0:
+            fac_in[r // 2].wait()
         left[r] = leaf_residual(fac_v.at[r], solved, pattern, r, rhs_v[n + r])
     for r in range(n):
         solved[n + r] = mm(inv_v[n + r], left[r]).astype(BF16)
@@ -141,7 +145,7 @@
             pltpu.VMEM((block, loads), BF16),
             pltpu.VMEM((block, block), BF16),
             pltpu.VMEM((2, block, block), BF16),
-            pltpu.SemaphoreType.DMA((12,)),
+            pltpu.SemaphoreType.DMA((12 + n,)),
         ],
         compiler_params=pltpu.CompilerParams(vmem_limit_bytes=16 << 20),
         name="leaf_edge",

time: 36.5 us -> 36.3 us (level)
  no operation moved by 1% of the time
where the time goes in v7:
time: 36.3 us; the launch traced here: 36.2 us
  starting transfers between devices  12.4 us (34%)
  waiting for transfers between devices  11.4 us (31%)
  Pallas kernels  11 us (30%)
  between operations  1.42 us (4%)
    ppermute x6, starting transfers between devices, passed_along(): lax.ppermute(value, axis, [(i, (i + by) % length) for i in range(length)])  8.37 us
    ppermute x6, waiting for transfers between devices, passed_along(): lax.ppermute(value, axis, [(i, (i + by) % length) for i in range(length)])  7.18 us
    pallas_call x1, Pallas kernels, edge_call(): pl.pallas_call(edge_kernel, out_shape=(pltpu.VMEM((2 * n, block, loads),...  4.05 us
    ppermute x2, starting transfers between devices, edge_swap(): return lax.ppermute(value, axis, pairs)  3.4 us
    ppermute x2, waiting for transfers between devices, edge_swap(): return lax.ppermute(value, axis, pairs)  3.32 us
    pallas_call x1, Pallas kernels, rest_call(): pl.pallas_call(rest_kernel, out_shape=pltpu.VMEM((n, block, loads), BF16)...  3.27 us
    pallas_call x1, Pallas kernels, collect_call(): pl.pallas_call(collect_kernel, out_shape=(jax.ShapeDtypeStruct((rows,) +...  1.31 us
    pallas_call x5, Pallas kernels, small_call(): pl.pallas_call(kernel, out_shape=pltpu.VMEM(shape, dtype), in_specs=[VMEM...  0.97 us
  transfers between devices with their start and end apart: 10, of which 7 were waited for; matrix products, arithmetic and copies ran while one was open for 0% of the time, Pallas kernels for 15%

profile of v7, /device:TPU:0, one launch (start us, length us, event | category | flops | bytes accessed | tf_op | source)
XLA Modules:
  0.0 36.2 jit_solution(461189739110308376)
XLA Ops:
  1.3 4.0 %leaf_edge.1 = (bf16[8,256,256]{2,1,0:T(8,128)(2,1)S(1)}, bf16[256,256]{1,0:T(8,128)(2,1)S(1)}, bf16[256,256]{1,0:T(8,128)(2,1)S(1)}, bf16[256,256]{1,0:T(8,128)(2,1)S(1)}) custom-call(s32[4,8]{1,0:T(4,128)} %bitcast.1, s32[1]{0:T(128)S(6)} %copy.12.link, bf16[12,256,256]{2,1,0:T(8,128)(2,1)} %rhs.5, bf16[12,256,256]{2,1,0:T(8,128)(2,1)} %inverse.5, ...), custom_call_target="tpu_custom_call" | custom-call | tf_op jit(solution)/shard_map/leaf_edge/pallas_call | solution.py:126
  5.4 0.5 %collective-permute-start = (bf16[256,256]{1,0:T(8,128)(2,1)S(1)}, bf16[256,256]{1,0:T(8,128)(2,1)S(1)}, u32[]{:S(2)}, u32[]{:S(2)}) collective-permute-start(bf16[256,256]{1,0:T(8,128)(2,1)S(1)} %get-tuple-element.14.edge), channel_id=1, source_target_pairs={{0,1},{1,0},{2,3},{3,2},{4,5},{5,4},{6,7},{7,6},{8,9},{9,8},{10,11... | collective-permute-start | bytes 393224 | tf_op jit(solution)/shard_map/ppermute | solution.py:55
  6.0 0.9 %collective-permute-done.lower = bf16[256,256]{1,0:T(8,128)(2,1)S(1)} collective-permute-done((bf16[256,256]{1,0:T(8,128)(2,1)S(1)}, bf16[256,256]{1,0:T(8,128)(2,1)S(1)}, u32[]{:S(2)}, u32[]{:S(2)}) %collective-permute-start) | collective-permute-done | bytes 131104 | tf_op jit(solution)/shard_map/ppermute | solution.py:55
  6.9 0.2 level0_early.1._
  7.1 1.8 %collective-permute-start.1 = (bf16[256,256]{1,0:T(8,128)(2,1)S(1)}, bf16[256,256]{1,0:T(8,128)(2,1)S(1)}, u32[]{:S(2)}, u32[]{:S(2)}) collective-permute-start(bf16[256,256]{1,0:T(8,128)(2,1)S(1)} %level0_early.1._), channel_id=1, source_target_pairs={{0,1},{1,2},{2,3},{3,4},{4,5},{5,6},{6,7},{7,8},{8,9},{9,10},{10,1... | collective-permute-start | bytes 393224 | tf_op jit(solution)/shard_map/ppermute | solution.py:22
  8.8 4.0 %collective-permute-start.2 = (bf16[256,256]{1,0:T(8,128)(2,1)S(1)}, bf16[256,256]{1,0:T(8,128)(2,1)S(1)}, u32[]{:S(2)}, u32[]{:S(2)}) collective-permute-start(bf16[256,256]{1,0:T(8,128)(2,1)S(1)} %get-tuple-element.12.down), channel_id=1, source_target_pairs={{0,15},{1,0},{2,1},{3,2},{4,3},{5,4},{6,5},{7,6},{8,7},{9,8},{10,9... | collective-permute-start | bytes 393224 | tf_op jit(solution)/shard_map/ppermute | solution.py:22
  12.8 0.4 %collective-permute-start.3 = (bf16[256,256]{1,0:T(8,128)(2,1)S(1)}, bf16[256,256]{1,0:T(8,128)(2,1)S(1)}, u32[]{:S(2)}, u32[]{:S(2)}) collective-permute-start(bf16[256,256]{1,0:T(8,128)(2,1)S(1)} %get-tuple-element.13.lower_mat), channel_id=1, source_target_pairs={{0,15},{1,0},{2,1},{3,2},{4,3},{5,4},{6,5},{7,6},{8,7},{9,8},{10,9... | collective-permute-start | bytes 393224 | tf_op jit(solution)/shard_map/ppermute | solution.py:22
  13.3 1.0 %collective-permute-done.4.lower = bf16[256,256]{1,0:T(8,128)(2,1)S(1)} collective-permute-done((bf16[256,256]{1,0:T(8,128)(2,1)S(1)}, bf16[256,256]{1,0:T(8,128)(2,1)S(1)}, u32[]{:S(2)}, u32[]{:S(2)}) %collective-permute-start.4) | collective-permute-done | bytes 131104 | tf_op jit(solution)/shard_map/ppermute | solution.py:22
  14.3 0.2 level0_late.1.refs_0_
  14.6 0.5 %fold.1 = (bf16[3,256,256]{2,1,0:T(8,128)(2,1)S(1)}, bf16[3,256,256]{2,1,0:T(8,128)(2,1)S(1)}, f32[3,256,256]{2,1,0:T(8,128)S(1)}) custom-call(bf16[4,1,256,256]{3,2,1,0:T(8,128)(2,1)S(1)} %copy-done.1, bf16[4,1,256,256]{3,2,1,0:T(8,128)(2,1)S(1)} %copy-done.2, bf16[4,1,2,256,256]{4,3,2,1,0:T(8,128)(2,1)S(1)} %copy-done, bf16[256,256]{1,0:T(8,128)(2,1)S(1)} %level0_early.1._), custom_call_target="tpu_custom_call" | custom-call | flops 301989888 | bytes 3145728 | tf_op jit(solution)/shard_map/fold/pallas_call | solution.py:258
  15.1 0.6 %collective-permute-done.1.below = bf16[256,256]{1,0:T(8,128)(2,1)S(1)} collective-permute-done((bf16[256,256]{1,0:T(8,128)(2,1)S(1)}, bf16[256,256]{1,0:T(8,128)(2,1)S(1)}, u32[]{:S(2)}, u32[]{:S(2)}) %collective-permute-start.1) | collective-permute-done | bytes 131104 | tf_op jit(solution)/shard_map/ppermute | solution.py:22
  15.7 0.2 level1_below.1.part
  15.9 0.8 %collective-permute-done.3.above_mat = bf16[256,256]{1,0:T(8,128)(2,1)S(1)} collective-permute-done((bf16[256,256]{1,0:T(8,128)(2,1)S(1)}, bf16[256,256]{1,0:T(8,128)(2,1)S(1)}, u32[]{:S(2)}, u32[]{:S(2)}) %collective-permute-start.3) | collective-permute-done | bytes 131104 | tf_op jit(solution)/shard_map/ppermute | solution.py:22
  16.7 0.2 level1.1._.refs_1_
  16.9 1.3 %collective-permute-start.6 = (bf16[256,256]{1,0:T(8,128)(2,1)S(1)}, bf16[256,256]{1,0:T(8,128)(2,1)S(1)}, u32[]{:S(2)}, u32[]{:S(2)}) collective-permute-start(bf16[256,256]{1,0:T(8,128)(2,1)S(1)} %level1.1._.refs_1_), channel_id=1, source_target_pairs={{0,2},{1,3},{2,0},{3,1},{4,6},{5,7},{6,4},{7,5},{8,10},{9,11},{10,... | collective-permute-start | bytes 393224 | tf_op jit(solution)/shard_map/ppermute | solution.py:35
  18.2 2.1 %collective-permute-start.7 = (bf16[256,256]{1,0:T(8,128)(2,1)S(1)}, bf16[256,256]{1,0:T(8,128)(2,1)S(1)}, u32[]{:S(2)}, u32[]{:S(2)}) collective-permute-start(bf16[256,256]{1,0:T(8,128)(2,1)S(1)} %level1.1._.refs_1_), channel_id=1, source_target_pairs={{0,14},{1,15},{2,4},{3,5},{4,2},{5,3},{6,8},{7,9},{8,6},{9,7},{10,... | collective-permute-start | bytes 393224 | tf_op jit(solution)/shard_map/ppermute | solution.py:35
  20.3 3.3 %leaf_rest.1.rest_0_.top = bf16[4,256,256]{2,1,0:T(8,128)(2,1)S(1)} custom-call(s32[4,8]{1,0:T(4,128)} %bitcast.2, bf16[12,256,256]{2,1,0:T(8,128)(2,1)} %rhs.5, bf16[12,256,256]{2,1,0:T(8,128)(2,1)} %inverse.5, bf16[8,4,256,256]{3,2,1,0:T(8,128)(2,1)} %factor.5, bf16[8,256,256]{2,1,0:T(8,128)(2,1)S(1)} %get-tuple-element.11.low, ...), custom_call_target="tpu_custom_call" | custom-call | flops 671088640 | bytes 4718592 | tf_op jit(solution)/shard_map/leaf_rest/pallas_call | solution.py:226
  23.6 1.2 %collective-permute-done.6.first = bf16[256,256]{1,0:T(8,128)(2,1)S(1)} collective-permute-done((bf16[256,256]{1,0:T(8,128)(2,1)S(1)}, bf16[256,256]{1,0:T(8,128)(2,1)S(1)}, u32[]{:S(2)}, u32[]{:S(2)}) %collective-permute-start.6) | collective-permute-done | bytes 131104 | tf_op jit(solution)/shard_map/ppermute | solution.py:35
  24.8 2.2 %collective-permute-done.7.second = bf16[256,256]{1,0:T(8,128)(2,1)S(1)} collective-permute-done((bf16[256,256]{1,0:T(8,128)(2,1)S(1)}, bf16[256,256]{1,0:T(8,128)(2,1)S(1)}, u32[]{:S(2)}, u32[]{:S(2)}) %collective-permute-start.7) | collective-permute-done | bytes 131104 | tf_op jit(solution)/shard_map/ppermute | solution.py:35
  26.9 0.2 level2.1.refs_2_
  27.2 2.0 %collective-permute-start.9 = (bf16[256,256]{1,0:T(8,128)(2,1)S(1)}, bf16[256,256]{1,0:T(8,128)(2,1)S(1)}, u32[]{:S(2)}, u32[]{:S(2)}) collective-permute-start(bf16[256,256]{1,0:T(8,128)(2,1)S(1)} %level2.1.refs_2_), channel_id=1, source_target_pairs={{0,4},{1,5},{2,6},{3,7},{4,8},{5,9},{6,10},{7,11},{8,12},{9,13},{1... | collective-permute-start | bytes 393224 | tf_op jit(solution)/shard_map/ppermute | solution.py:22
  29.2 1.3 %collect.1 = (bf16[12,256,256]{2,1,0:T(8,128)(2,1)}, bf16[4,1,256,256]{3,2,1,0:T(8,128)(2,1)}) custom-call(bf16[8,256,256]{2,1,0:T(8,128)(2,1)S(1)} %get-tuple-element.11.low, bf16[4,256,256]{2,1,0:T(8,128)(2,1)S(1)} %leaf_rest.1.rest_0_.top, bf16[256,256]{1,0:T(8,128)(2,1)S(1)} %level0_late.1.refs_0_, bf16[256,256]{1,0:T(8,128)(2,1)S(1)} %level1.1._.refs_1_, ...), custom_call_target="tpu_custom_call" | custom-call | bytes 3932160 | tf_op jit(solution)/shard_map/collect/pallas_call | solution.py:319
  30.6 4.7 %collective-permute-done.8.first = bf16[256,256]{1,0:T(8,128)(2,1)S(1)} collective-permute-done((bf16[256,256]{1,0:T(8,128)(2,1)S(1)}, bf16[256,256]{1,0:T(8,128)(2,1)S(1)}, u32[]{:S(2)}, u32[]{:S(2)}) %collective-permute-start.8) | collective-permute-done | bytes 131104 | tf_op jit(solution)/shard_map/ppermute | solution.py:22
  35.3 0.9 %node_last.1 = bf16[4,1,256,256]{3,2,1,0:T(8,128)(2,1)} custom-call(bf16[256,256]{1,0:T(8,128)(2,1)S(1)} %collective-permute-done.8.first, bf16[256,256]{1,0:T(8,128)(2,1)S(1)} %collective-permute-done.9.second, bf16[3,256,256]{2,1,0:T(8,128)(2,1)S(1)} %get-tuple-element.15.lower_mat, ...), custom_call_target="tpu_custom_call", output_to_operand_aliasing={{}: (5, {})} | custom-call | tf_op jit(solution)/shard_map/node_last/pallas_call | solution.py:359
  (12 shorter events, 0.2 us)
Async XLA Ops:
  1.3 13.3 %copy-start.1 = (bf16[4,1,256,256]{3,2,1,0:T(8,128)(2,1)S(1)}, bf16[4,1,256,256]{3,2,1,0:T(8,128)(2,1)}, u32[]{:S(2)}) copy-start(bf16[4,1,256,256]{3,2,1,0:T(8,128)(2,1)} %rhs.4) | copy-start | bytes 1572868
  1.3 13.3 %copy-start.2 = (bf16[4,1,256,256]{3,2,1,0:T(8,128)(2,1)S(1)}, bf16[4,1,256,256]{3,2,1,0:T(8,128)(2,1)}, u32[]{:S(2)}) copy-start(bf16[4,1,256,256]{3,2,1,0:T(8,128)(2,1)} %inverse.4) | copy-start | bytes 1572868
  5.4 9.2 %copy-start = (bf16[4,1,2,256,256]{4,3,2,1,0:T(8,128)(2,1)S(1)}, bf16[4,1,2,256,256]{4,3,2,1,0:T(8,128)(2,1)}, u32[]{:S(2)}) copy-start(bf16[4,1,2,256,256]{4,3,2,1,0:T(8,128)(2,1)} %factor.4) | copy-start | bytes 3145732
  5.4 1.5 %collective-permute-start = (bf16[256,256]{1,0:T(8,128)(2,1)S(1)}, bf16[256,256]{1,0:T(8,128)(2,1)S(1)}, u32[]{:S(2)}, u32[]{:S(2)}) collective-permute-start(bf16[256,256]{1,0:T(8,128)(2,1)S(1)} %get-tuple-element.14.edge), channel_id=1, source_target_pairs={{0,1},{1,0},{2,3},{3,2},{4,5},{5,4},{6,7},{7,6},{8,9},{9,8},{10,11... | collective-permute-start | bytes 393224 | tf_op jit(solution)/shard_map/ppermute | solution.py:55
  5.9 8.4 %collective-permute-start.4 = (bf16[256,256]{1,0:T(8,128)(2,1)S(1)}, bf16[256,256]{1,0:T(8,128)(2,1)S(1)}, u32[]{:S(2)}, u32[]{:S(2)}) collective-permute-start(bf16[256,256]{1,0:T(8,128)(2,1)S(1)} %get-tuple-element.14.edge), channel_id=1, source_target_pairs={{0,1},{1,2},{2,3},{3,4},{4,5},{5,6},{6,7},{7,8},{8,9},{9,10},{10,1... | collective-permute-start | bytes 393224 | tf_op jit(solution)/shard_map/ppermute | solution.py:22
  7.1 8.6 %collective-permute-start.1 = (bf16[256,256]{1,0:T(8,128)(2,1)S(1)}, bf16[256,256]{1,0:T(8,128)(2,1)S(1)}, u32[]{:S(2)}, u32[]{:S(2)}) collective-permute-start(bf16[256,256]{1,0:T(8,128)(2,1)S(1)} %level0_early.1._), channel_id=1, source_target_pairs={{0,1},{1,2},{2,3},{3,4},{4,5},{5,6},{6,7},{7,8},{8,9},{9,10},{10,1... | collective-permute-start | bytes 393224 | tf_op jit(solution)/shard_map/ppermute | solution.py:22
  8.8 7.1 %collective-permute-start.2 = (bf16[256,256]{1,0:T(8,128)(2,1)S(1)}, bf16[256,256]{1,0:T(8,128)(2,1)S(1)}, u32[]{:S(2)}, u32[]{:S(2)}) collective-permute-start(bf16[256,256]{1,0:T(8,128)(2,1)S(1)} %get-tuple-element.12.down), channel_id=1, source_target_pairs={{0,15},{1,0},{2,1},{3,2},{4,3},{5,4},{6,5},{7,6},{8,7},{9,8},{10,9... | collective-permute-start | bytes 393224 | tf_op jit(solution)/shard_map/ppermute | solution.py:22
  12.8 3.9 %collective-permute-start.3 = (bf16[256,256]{1,0:T(8,128)(2,1)S(1)}, bf16[256,256]{1,0:T(8,128)(2,1)S(1)}, u32[]{:S(2)}, u32[]{:S(2)}) collective-permute-start(bf16[256,256]{1,0:T(8,128)(2,1)S(1)} %get-tuple-element.13.lower_mat), channel_id=1, source_target_pairs={{0,15},{1,0},{2,1},{3,2},{4,3},{5,4},{6,5},{7,6},{8,7},{9,8},{10,9... | collective-permute-start | bytes 393224 | tf_op jit(solution)/shard_map/ppermute | solution.py:22
  14.5 2.2 %collective-permute-start.5 = (bf16[256,256]{1,0:T(8,128)(2,1)S(1)}, bf16[256,256]{1,0:T(8,128)(2,1)S(1)}, u32[]{:S(2)}, u32[]{:S(2)}) collective-permute-start(bf16[256,256]{1,0:T(8,128)(2,1)S(1)} %level0_late.1.refs_0_), channel_id=1, source_target_pairs={{0,1},{1,0},{2,3},{3,2},{4,5},{5,4},{6,7},{7,6},{8,9},{9,8},{10,11... | collective-permute-start | bytes 393224 | tf_op jit(solution)/shard_map/ppermute | solution.py:55
  16.9 7.8 %collective-permute-start.6 = (bf16[256,256]{1,0:T(8,128)(2,1)S(1)}, bf16[256,256]{1,0:T(8,128)(2,1)S(1)}, u32[]{:S(2)}, u32[]{:S(2)}) collective-permute-start(bf16[256,256]{1,0:T(8,128)(2,1)S(1)} %level1.1._.refs_1_), channel_id=1, source_target_pairs={{0,2},{1,3},{2,0},{3,1},{4,6},{5,7},{6,4},{7,5},{8,10},{9,11},{10,... | collective-permute-start | bytes 393224 | tf_op jit(solution)/shard_map/ppermute | solution.py:35
  18.2 8.7 %collective-permute-start.7 = (bf16[256,256]{1,0:T(8,128)(2,1)S(1)}, bf16[256,256]{1,0:T(8,128)(2,1)S(1)}, u32[]{:S(2)}, u32[]{:S(2)}) collective-permute-start(bf16[256,256]{1,0:T(8,128)(2,1)S(1)} %level1.1._.refs_1_), channel_id=1, source_target_pairs={{0,14},{1,15},{2,4},{3,5},{4,2},{5,3},{6,8},{7,9},{8,6},{9,7},{10,... | collective-permute-start | bytes 393224 | tf_op jit(solution)/shard_map/ppermute | solution.py:35
  27.2 8.1 %collective-permute-start.8 = (bf16[256,256]{1,0:T(8,128)(2,1)S(1)}, bf16[256,256]{1,0:T(8,128)(2,1)S(1)}, u32[]{:S(2)}, u32[]{:S(2)}) collective-permute-start(bf16[256,256]{1,0:T(8,128)(2,1)S(1)} %level2.1.refs_2_), channel_id=1, source_target_pairs={{0,12},{1,13},{2,14},{3,15},{4,0},{5,1},{6,2},{7,3},{8,4},{9,5},{1... | collective-permute-start | bytes 393224 | tf_op jit(solution)/shard_map/ppermute | solution.py:22
  27.2 8.1 %collective-permute-start.9 = (bf16[256,256]{1,0:T(8,128)(2,1)S(1)}, bf16[256,256]{1,0:T(8,128)(2,1)S(1)}, u32[]{:S(2)}, u32[]{:S(2)}) collective-permute-start(bf16[256,256]{1,0:T(8,128)(2,1)S(1)} %level2.1.refs_2_), channel_id=1, source_target_pairs={{0,4},{1,5},{2,6},{3,7},{4,8},{5,9},{6,10},{7,11},{8,12},{9,13},{1... | collective-permute-start | bytes 393224 | tf_op jit(solution)/shard_map/ppermute | solution.py:22

commit v8 on v7

--- a/solution.py
+++ b/solution.py
@@ -84,11 +84,11 @@
     next_in = (
         load(columns, pattern),
         load(rhs.at[pl.ds(n, n)], rhs_v.at[pl.ds(n, n)]),
-        load(inverse.at[pl.ds(n, n)], inv_v.at[pl.ds(n, n)]),
     )
     fac_in = [
         load(factor.at[pl.ds(r, 2)], fac_v.at[pl.ds(r, 2)]) for r in range(0, n, 2)
     ]
+    inv_in = load(inverse.at[pl.ds(n, n)], inv_v.at[pl.ds(n, n)])
     last_in = (
         load(rhs.at[top], rhs_v.at[low]),
         load(factor.at[top - n], top_fac),
@@ -109,6 +109,7 @@
         if r % 2 == 0:
             fac_in[r // 2].wait()
         left[r] = leaf_residual(fac_v.at[r], solved, pattern, r, rhs_v[n + r])
+    inv_in.wait()
     for r in range(n):
         solved[n + r] = mm(inv_v[n + r], left[r]).astype(BF16)
     for copy in last_in:

time: 36.3 us -> 36.3 us (level)
  no operation moved by 1% of the time
where the time goes in v8:
time: 36.3 us; the launch traced here: 36.2 us
  starting transfers between devices  12.4 us (34%)
  waiting for transfers between devices  11.4 us (31%)
  Pallas kernels  10.9 us (30%)
  between operations  1.42 us (4%)
    ppermute x6, starting transfers between devices, passed_along(): lax.ppermute(value, axis, [(i, (i + by) % length) for i in range(length)])  8.36 us
    ppermute x6, waiting for transfers between devices, passed_along(): lax.ppermute(value, axis, [(i, (i + by) % length) for i in range(length)])  7.18 us
    pallas_call x1, Pallas kernels, edge_call(): pl.pallas_call(edge_kernel, out_shape=(pltpu.VMEM((2 * n, block, loads),...  4.04 us
    ppermute x2, starting transfers between devices, edge_swap(): return lax.ppermute(value, axis, pairs)  3.4 us
    ppermute x2, waiting for transfers between devices, edge_swap(): return lax.ppermute(value, axis, pairs)  3.33 us
    pallas_call x1, Pallas kernels, rest_call(): pl.pallas_call(rest_kernel, out_shape=pltpu.VMEM((n, block, loads), BF16)...  3.26 us
    pallas_call x1, Pallas kernels, collect_call(): pl.pallas_call(collect_kernel, out_shape=(jax.ShapeDtypeStruct((rows,) +...  1.31 us
    pallas_call x5, Pallas kernels, small_call(): pl.pallas_call(kernel, out_shape=pltpu.VMEM(shape, dtype), in_specs=[VMEM...  0.97 us
  transfers between devices with their start and end apart: 10, of which 7 were waited for; matrix products, arithmetic and copies ran while one was open for 0% of the time, Pallas kernels for 15%

profile of v8, /device:TPU:0, one launch (start us, length us, event | category | flops | bytes accessed | tf_op | source)
XLA Modules:
  0.0 36.2 jit_solution(9671033911852090669)
XLA Ops:
  1.3 4.0 %leaf_edge.1 = (bf16[8,256,256]{2,1,0:T(8,128)(2,1)S(1)}, bf16[256,256]{1,0:T(8,128)(2,1)S(1)}, bf16[256,256]{1,0:T(8,128)(2,1)S(1)}, bf16[256,256]{1,0:T(8,128)(2,1)S(1)}) custom-call(s32[4,8]{1,0:T(4,128)} %bitcast.1, s32[1]{0:T(128)S(6)} %copy.12.link, bf16[12,256,256]{2,1,0:T(8,128)(2,1)} %rhs.5, bf16[12,256,256]{2,1,0:T(8,128)(2,1)} %inverse.5, ...), custom_call_target="tpu_custom_call" | custom-call | tf_op jit(solution)/shard_map/leaf_edge/pallas_call | solution.py:127
  5.4 0.5 %collective-permute-start = (bf16[256,256]{1,0:T(8,128)(2,1)S(1)}, bf16[256,256]{1,0:T(8,128)(2,1)S(1)}, u32[]{:S(2)}, u32[]{:S(2)}) collective-permute-start(bf16[256,256]{1,0:T(8,128)(2,1)S(1)} %get-tuple-element.14.edge), channel_id=1, source_target_pairs={{0,1},{1,0},{2,3},{3,2},{4,5},{5,4},{6,7},{7,6},{8,9},{9,8},{10,11... | collective-permute-start | bytes 393224 | tf_op jit(solution)/shard_map/ppermute | solution.py:55
  6.0 0.9 %collective-permute-done.lower = bf16[256,256]{1,0:T(8,128)(2,1)S(1)} collective-permute-done((bf16[256,256]{1,0:T(8,128)(2,1)S(1)}, bf16[256,256]{1,0:T(8,128)(2,1)S(1)}, u32[]{:S(2)}, u32[]{:S(2)}) %collective-permute-start) | collective-permute-done | bytes 131104 | tf_op jit(solution)/shard_map/ppermute | solution.py:55
  6.9 0.2 level0_early.1._
  7.1 1.8 %collective-permute-start.1 = (bf16[256,256]{1,0:T(8,128)(2,1)S(1)}, bf16[256,256]{1,0:T(8,128)(2,1)S(1)}, u32[]{:S(2)}, u32[]{:S(2)}) collective-permute-start(bf16[256,256]{1,0:T(8,128)(2,1)S(1)} %level0_early.1._), channel_id=1, source_target_pairs={{0,1},{1,2},{2,3},{3,4},{4,5},{5,6},{6,7},{7,8},{8,9},{9,10},{10,1... | collective-permute-start | bytes 393224 | tf_op jit(solution)/shard_map/ppermute | solution.py:22
  8.8 4.0 %collective-permute-start.2 = (bf16[256,256]{1,0:T(8,128)(2,1)S(1)}, bf16[256,256]{1,0:T(8,128)(2,1)S(1)}, u32[]{:S(2)}, u32[]{:S(2)}) collective-permute-start(bf16[256,256]{1,0:T(8,128)(2,1)S(1)} %get-tuple-element.12.down), channel_id=1, source_target_pairs={{0,15},{1,0},{2,1},{3,2},{4,3},{5,4},{6,5},{7,6},{8,7},{9,8},{10,9... | collective-permute-start | bytes 393224 | tf_op jit(solution)/shard_map/ppermute | solution.py:22
  12.8 0.4 %collective-permute-start.3 = (bf16[256,256]{1,0:T(8,128)(2,1)S(1)}, bf16[256,256]{1,0:T(8,128)(2,1)S(1)}, u32[]{:S(2)}, u32[]{:S(2)}) collective-permute-start(bf16[256,256]{1,0:T(8,128)(2,1)S(1)} %get-tuple-element.13.lower_mat), channel_id=1, source_target_pairs={{0,15},{1,0},{2,1},{3,2},{4,3},{5,4},{6,5},{7,6},{8,7},{9,8},{10,9... | collective-permute-start | bytes 393224 | tf_op jit(solution)/shard_map/ppermute | solution.py:22
  13.3 1.0 %collective-permute-done.4.lower = bf16[256,256]{1,0:T(8,128)(2,1)S(1)} collective-permute-done((bf16[256,256]{1,0:T(8,128)(2,1)S(1)}, bf16[256,256]{1,0:T(8,128)(2,1)S(1)}, u32[]{:S(2)}, u32[]{:S(2)}) %collective-permute-start.4) | collective-permute-done | bytes 131104 | tf_op jit(solution)/shard_map/ppermute | solution.py:22
  14.3 0.2 level0_late.1.refs_0_
  14.6 0.5 %fold.1 = (bf16[3,256,256]{2,1,0:T(8,128)(2,1)S(1)}, bf16[3,256,256]{2,1,0:T(8,128)(2,1)S(1)}, f32[3,256,256]{2,1,0:T(8,128)S(1)}) custom-call(bf16[4,1,256,256]{3,2,1,0:T(8,128)(2,1)S(1)} %copy-done.1, bf16[4,1,256,256]{3,2,1,0:T(8,128)(2,1)S(1)} %copy-done.2, bf16[4,1,2,256,256]{4,3,2,1,0:T(8,128)(2,1)S(1)} %copy-done, bf16[256,256]{1,0:T(8,128)(2,1)S(1)} %level0_early.1._), custom_call_target="tpu_custom_call" | custom-call | flops 301989888 | bytes 3145728 | tf_op jit(solution)/shard_map/fold/pallas_call | solution.py:259
  15.1 0.6 %collective-permute-done.1.below = bf16[256,256]{1,0:T(8,128)(2,1)S(1)} collective-permute-done((bf16[256,256]{1,0:T(8,128)(2,1)S(1)}, bf16[256,256]{1,0:T(8,128)(2,1)S(1)}, u32[]{:S(2)}, u32[]{:S(2)}) %collective-permute-start.1) | collective-permute-done | bytes 131104 | tf_op jit(solution)/shard_map/ppermute | solution.py:22
  15.7 0.2 level1_below.1.part
  15.9 0.8 %collective-permute-done.3.above_mat = bf16[256,256]{1,0:T(8,128)(2,1)S(1)} collective-permute-done((bf16[256,256]{1,0:T(8,128)(2,1)S(1)}, bf16[256,256]{1,0:T(8,128)(2,1)S(1)}, u32[]{:S(2)}, u32[]{:S(2)}) %collective-permute-start.3) | collective-permute-done | bytes 131104 | tf_op jit(solution)/shard_map/ppermute | solution.py:22
  16.7 0.2 level1.1._.refs_1_
  16.9 1.3 %collective-permute-start.6 = (bf16[256,256]{1,0:T(8,128)(2,1)S(1)}, bf16[256,256]{1,0:T(8,128)(2,1)S(1)}, u32[]{:S(2)}, u32[]{:S(2)}) collective-permute-start(bf16[256,256]{1,0:T(8,128)(2,1)S(1)} %level1.1._.refs_1_), channel_id=1, source_target_pairs={{0,2},{1,3},{2,0},{3,1},{4,6},{5,7},{6,4},{7,5},{8,10},{9,11},{10,... | collective-permute-start | bytes 393224 | tf_op jit(solution)/shard_map/ppermute | solution.py:35
  18.2 2.1 %collective-permute-start.7 = (bf16[256,256]{1,0:T(8,128)(2,1)S(1)}, bf16[256,256]{1,0:T(8,128)(2,1)S(1)}, u32[]{:S(2)}, u32[]{:S(2)}) collective-permute-start(bf16[256,256]{1,0:T(8,128)(2,1)S(1)} %level1.1._.refs_1_), channel_id=1, source_target_pairs={{0,14},{1,15},{2,4},{3,5},{4,2},{5,3},{6,8},{7,9},{8,6},{9,7},{10,... | collective-permute-start | bytes 393224 | tf_op jit(solution)/shard_map/ppermute | solution.py:35
  20.3 3.3 %leaf_rest.1.rest_0_.top = bf16[4,256,256]{2,1,0:T(8,128)(2,1)S(1)} custom-call(s32[4,8]{1,0:T(4,128)} %bitcast.2, bf16[12,256,256]{2,1,0:T(8,128)(2,1)} %rhs.5, bf16[12,256,256]{2,1,0:T(8,128)(2,1)} %inverse.5, bf16[8,4,256,256]{3,2,1,0:T(8,128)(2,1)} %factor.5, bf16[8,256,256]{2,1,0:T(8,128)(2,1)S(1)} %get-tuple-element.11.low, ...), custom_call_target="tpu_custom_call" | custom-call | flops 671088640 | bytes 4718592 | tf_op jit(solution)/shard_map/leaf_rest/pallas_call | solution.py:227
  23.6 1.2 %collective-permute-done.6.first = bf16[256,256]{1,0:T(8,128)(2,1)S(1)} collective-permute-done((bf16[256,256]{1,0:T(8,128)(2,1)S(1)}, bf16[256,256]{1,0:T(8,128)(2,1)S(1)}, u32[]{:S(2)}, u32[]{:S(2)}) %collective-permute-start.6) | collective-permute-done | bytes 131104 | tf_op jit(solution)/shard_map/ppermute | solution.py:35
  24.8 2.2 %collective-permute-done.7.second = bf16[256,256]{1,0:T(8,128)(2,1)S(1)} collective-permute-done((bf16[256,256]{1,0:T(8,128)(2,1)S(1)}, bf16[256,256]{1,0:T(8,128)(2,1)S(1)}, u32[]{:S(2)}, u32[]{:S(2)}) %collective-permute-start.7) | collective-permute-done | bytes 131104 | tf_op jit(solution)/shard_map/ppermute | solution.py:35
  26.9 0.2 level2.1.refs_2_
  27.2 2.0 %collective-permute-start.9 = (bf16[256,256]{1,0:T(8,128)(2,1)S(1)}, bf16[256,256]{1,0:T(8,128)(2,1)S(1)}, u32[]{:S(2)}, u32[]{:S(2)}) collective-permute-start(bf16[256,256]{1,0:T(8,128)(2,1)S(1)} %level2.1.refs_2_), channel_id=1, source_target_pairs={{0,4},{1,5},{2,6},{3,7},{4,8},{5,9},{6,10},{7,11},{8,12},{9,13},{1... | collective-permute-start | bytes 393224 | tf_op jit(solution)/shard_map/ppermute | solution.py:22
  29.2 1.3 %collect.1 = (bf16[12,256,256]{2,1,0:T(8,128)(2,1)}, bf16[4,1,256,256]{3,2,1,0:T(8,128)(2,1)}) custom-call(bf16[8,256,256]{2,1,0:T(8,128)(2,1)S(1)} %get-tuple-element.11.low, bf16[4,256,256]{2,1,0:T(8,128)(2,1)S(1)} %leaf_rest.1.rest_0_.top, bf16[256,256]{1,0:T(8,128)(2,1)S(1)} %level0_late.1.refs_0_, bf16[256,256]{1,0:T(8,128)(2,1)S(1)} %level1.1._.refs_1_, ...), custom_call_target="tpu_custom_call" | custom-call | bytes 3932160 | tf_op jit(solution)/shard_map/collect/pallas_call | solution.py:320
  30.6 4.7 %collective-permute-done.8.first = bf16[256,256]{1,0:T(8,128)(2,1)S(1)} collective-permute-done((bf16[256,256]{1,0:T(8,128)(2,1)S(1)}, bf16[256,256]{1,0:T(8,128)(2,1)S(1)}, u32[]{:S(2)}, u32[]{:S(2)}) %collective-permute-start.8) | collective-permute-done | bytes 131104 | tf_op jit(solution)/shard_map/ppermute | solution.py:22
  35.3 0.9 %node_last.1 = bf16[4,1,256,256]{3,2,1,0:T(8,128)(2,1)} custom-call(bf16[256,256]{1,0:T(8,128)(2,1)S(1)} %collective-permute-done.8.first, bf16[256,256]{1,0:T(8,128)(2,1)S(1)} %collective-permute-done.9.second, bf16[3,256,256]{2,1,0:T(8,128)(2,1)S(1)} %get-tuple-element.15.lower_mat, ...), custom_call_target="tpu_custom_call", output_to_operand_aliasing={{}: (5, {})} | custom-call | tf_op jit(solution)/shard_map/node_last/pallas_call | solution.py:360
  (12 shorter events, 0.2 us)
Async XLA Ops:
  1.3 13.3 %copy-start.1 = (bf16[4,1,256,256]{3,2,1,0:T(8,128)(2,1)S(1)}, bf16[4,1,256,256]{3,2,1,0:T(8,128)(2,1)}, u32[]{:S(2)}) copy-start(bf16[4,1,256,256]{3,2,1,0:T(8,128)(2,1)} %rhs.4) | copy-start | bytes 1572868
  1.3 13.3 %copy-start.2 = (bf16[4,1,256,256]{3,2,1,0:T(8,128)(2,1)S(1)}, bf16[4,1,256,256]{3,2,1,0:T(8,128)(2,1)}, u32[]{:S(2)}) copy-start(bf16[4,1,256,256]{3,2,1,0:T(8,128)(2,1)} %inverse.4) | copy-start | bytes 1572868
  5.3 9.2 %copy-start = (bf16[4,1,2,256,256]{4,3,2,1,0:T(8,128)(2,1)S(1)}, bf16[4,1,2,256,256]{4,3,2,1,0:T(8,128)(2,1)}, u32[]{:S(2)}) copy-start(bf16[4,1,2,256,256]{4,3,2,1,0:T(8,128)(2,1)} %factor.4) | copy-start | bytes 3145732
  5.4 1.5 %collective-permute-start = (bf16[256,256]{1,0:T(8,128)(2,1)S(1)}, bf16[256,256]{1,0:T(8,128)(2,1)S(1)}, u32[]{:S(2)}, u32[]{:S(2)}) collective-permute-start(bf16[256,256]{1,0:T(8,128)(2,1)S(1)} %get-tuple-element.14.edge), channel_id=1, source_target_pairs={{0,1},{1,0},{2,3},{3,2},{4,5},{5,4},{6,7},{7,6},{8,9},{9,8},{10,11... | collective-permute-start | bytes 393224 | tf_op jit(solution)/shard_map/ppermute | solution.py:55
  5.9 8.4 %collective-permute-start.4 = (bf16[256,256]{1,0:T(8,128)(2,1)S(1)}, bf16[256,256]{1,0:T(8,128)(2,1)S(1)}, u32[]{:S(2)}, u32[]{:S(2)}) collective-permute-start(bf16[256,256]{1,0:T(8,128)(2,1)S(1)} %get-tuple-element.14.edge), channel_id=1, source_target_pairs={{0,1},{1,2},{2,3},{3,4},{4,5},{5,6},{6,7},{7,8},{8,9},{9,10},{10,1... | collective-permute-start | bytes 393224 | tf_op jit(solution)/shard_map/ppermute | solution.py:22
  7.1 8.6 %collective-permute-start.1 = (bf16[256,256]{1,0:T(8,128)(2,1)S(1)}, bf16[256,256]{1,0:T(8,128)(2,1)S(1)}, u32[]{:S(2)}, u32[]{:S(2)}) collective-permute-start(bf16[256,256]{1,0:T(8,128)(2,1)S(1)} %level0_early.1._), channel_id=1, source_target_pairs={{0,1},{1,2},{2,3},{3,4},{4,5},{5,6},{6,7},{7,8},{8,9},{9,10},{10,1... | collective-permute-start | bytes 393224 | tf_op jit(solution)/shard_map/ppermute | solution.py:22
  8.8 7.1 %collective-permute-start.2 = (bf16[256,256]{1,0:T(8,128)(2,1)S(1)}, bf16[256,256]{1,0:T(8,128)(2,1)S(1)}, u32[]{:S(2)}, u32[]{:S(2)}) collective-permute-start(bf16[256,256]{1,0:T(8,128)(2,1)S(1)} %get-tuple-element.12.down), channel_id=1, source_target_pairs={{0,15},{1,0},{2,1},{3,2},{4,3},{5,4},{6,5},{7,6},{8,7},{9,8},{10,9... | collective-permute-start | bytes 393224 | tf_op jit(solution)/shard_map/ppermute | solution.py:22
  12.8 3.9 %collective-permute-start.3 = (bf16[256,256]{1,0:T(8,128)(2,1)S(1)}, bf16[256,256]{1,0:T(8,128)(2,1)S(1)}, u32[]{:S(2)}, u32[]{:S(2)}) collective-permute-start(bf16[256,256]{1,0:T(8,128)(2,1)S(1)} %get-tuple-element.13.lower_mat), channel_id=1, source_target_pairs={{0,15},{1,0},{2,1},{3,2},{4,3},{5,4},{6,5},{7,6},{8,7},{9,8},{10,9... | collective-permute-start | bytes 393224 | tf_op jit(solution)/shard_map/ppermute | solution.py:22
  14.5 2.3 %collective-permute-start.5 = (bf16[256,256]{1,0:T(8,128)(2,1)S(1)}, bf16[256,256]{1,0:T(8,128)(2,1)S(1)}, u32[]{:S(2)}, u32[]{:S(2)}) collective-permute-start(bf16[256,256]{1,0:T(8,128)(2,1)S(1)} %level0_late.1.refs_0_), channel_id=1, source_target_pairs={{0,1},{1,0},{2,3},{3,2},{4,5},{5,4},{6,7},{7,6},{8,9},{9,8},{10,11... | collective-permute-start | bytes 393224 | tf_op jit(solution)/shard_map/ppermute | solution.py:55
  16.9 7.8 %collective-permute-start.6 = (bf16[256,256]{1,0:T(8,128)(2,1)S(1)}, bf16[256,256]{1,0:T(8,128)(2,1)S(1)}, u32[]{:S(2)}, u32[]{:S(2)}) collective-permute-start(bf16[256,256]{1,0:T(8,128)(2,1)S(1)} %level1.1._.refs_1_), channel_id=1, source_target_pairs={{0,2},{1,3},{2,0},{3,1},{4,6},{5,7},{6,4},{7,5},{8,10},{9,11},{10,... | collective-permute-start | bytes 393224 | tf_op jit(solution)/shard_map/ppermute | solution.py:35
  18.2 8.7 %collective-permute-start.7 = (bf16[256,256]{1,0:T(8,128)(2,1)S(1)}, bf16[256,256]{1,0:T(8,128)(2,1)S(1)}, u32[]{:S(2)}, u32[]{:S(2)}) collective-permute-start(bf16[256,256]{1,0:T(8,128)(2,1)S(1)} %level1.1._.refs_1_), channel_id=1, source_target_pairs={{0,14},{1,15},{2,4},{3,5},{4,2},{5,3},{6,8},{7,9},{8,6},{9,7},{10,... | collective-permute-start | bytes 393224 | tf_op jit(solution)/shard_map/ppermute | solution.py:35
  27.2 8.1 %collective-permute-start.8 = (bf16[256,256]{1,0:T(8,128)(2,1)S(1)}, bf16[256,256]{1,0:T(8,128)(2,1)S(1)}, u32[]{:S(2)}, u32[]{:S(2)}) collective-permute-start(bf16[256,256]{1,0:T(8,128)(2,1)S(1)} %level2.1.refs_2_), channel_id=1, source_target_pairs={{0,12},{1,13},{2,14},{3,15},{4,0},{5,1},{6,2},{7,3},{8,4},{9,5},{1... | collective-permute-start | bytes 393224 | tf_op jit(solution)/shard_map/ppermute | solution.py:22
  27.2 8.1 %collective-permute-start.9 = (bf16[256,256]{1,0:T(8,128)(2,1)S(1)}, bf16[256,256]{1,0:T(8,128)(2,1)S(1)}, u32[]{:S(2)}, u32[]{:S(2)}) collective-permute-start(bf16[256,256]{1,0:T(8,128)(2,1)S(1)} %level2.1.refs_2_), channel_id=1, source_target_pairs={{0,4},{1,5},{2,6},{3,7},{4,8},{5,9},{6,10},{7,11},{8,12},{9,13},{1... | collective-permute-start | bytes 393224 | tf_op jit(solution)/shard_map/ppermute | solution.py:22

commit v9 on v8

--- a/solution.py
+++ b/solution.py
@@ -342,8 +342,7 @@
     h = const.shape[0] - 1
     size = const.shape[1] // 2
     copies = []
-    for half in range(2):
-        rows = pl.ds(half * size, size)
+    for half, rows in enumerate((pl.ds(0, 3 * size // 2), pl.ds(3 * size // 2, size // 2))):
         node_total(
             h, rows, first, second, lower_mat, upper_mat, const, piece, stride, swapped
         )

time: 36.3 us -> 36.3 us (level)
  no operation moved by 1% of the time
where the time goes in v9:
time: 36.3 us; the launch traced here: 36.2 us
  starting transfers between devices  12.4 us (34%)
  waiting for transfers between devices  11.4 us (31%)
  Pallas kernels  10.9 us (30%)
  between operations  1.42 us (4%)
    ppermute x6, starting transfers between devices, passed_along(): lax.ppermute(value, axis, [(i, (i + by) % length) for i in range(length)])  8.36 us
    ppermute x6, waiting for transfers between devices, passed_along(): lax.ppermute(value, axis, [(i, (i + by) % length) for i in range(length)])  7.18 us
    pallas_call x1, Pallas kernels, edge_call(): pl.pallas_call(edge_kernel, out_shape=(pltpu.VMEM((2 * n, block, loads),...  4.04 us
    ppermute x2, starting transfers between devices, edge_swap(): return lax.ppermute(value, axis, pairs)  3.4 us
    ppermute x2, waiting for transfers between devices, edge_swap(): return lax.ppermute(value, axis, pairs)  3.33 us
    pallas_call x1, Pallas kernels, rest_call(): pl.pallas_call(rest_kernel, out_shape=pltpu.VMEM((n, block, loads), BF16)...  3.26 us
    pallas_call x1, Pallas kernels, collect_call(): pl.pallas_call(collect_kernel, out_shape=(jax.ShapeDtypeStruct((rows,) +...  1.31 us
    pallas_call x5, Pallas kernels, small_call(): pl.pallas_call(kernel, out_shape=pltpu.VMEM(shape, dtype), in_specs=[VMEM...  0.97 us
  transfers between devices with their start and end apart: 10, of which 7 were waited for; matrix products, arithmetic and copies ran while one was open for 0% of the time, Pallas kernels for 15%

profile of v9, /device:TPU:0, one launch (start us, length us, event | category | flops | bytes accessed | tf_op | source)
XLA Modules:
  0.0 36.2 jit_solution(1059034238720454297)
XLA Ops:
  1.3 4.0 %leaf_edge.1 = (bf16[8,256,256]{2,1,0:T(8,128)(2,1)S(1)}, bf16[256,256]{1,0:T(8,128)(2,1)S(1)}, bf16[256,256]{1,0:T(8,128)(2,1)S(1)}, bf16[256,256]{1,0:T(8,128)(2,1)S(1)}) custom-call(s32[4,8]{1,0:T(4,128)} %bitcast.1, s32[1]{0:T(128)S(6)} %copy.12.link, bf16[12,256,256]{2,1,0:T(8,128)(2,1)} %rhs.5, bf16[12,256,256]{2,1,0:T(8,128)(2,1)} %inverse.5, ...), custom_call_target="tpu_custom_call" | custom-call | tf_op jit(solution)/shard_map/leaf_edge/pallas_call | solution.py:127
  5.4 0.5 %collective-permute-start = (bf16[256,256]{1,0:T(8,128)(2,1)S(1)}, bf16[256,256]{1,0:T(8,128)(2,1)S(1)}, u32[]{:S(2)}, u32[]{:S(2)}) collective-permute-start(bf16[256,256]{1,0:T(8,128)(2,1)S(1)} %get-tuple-element.14.edge), channel_id=1, source_target_pairs={{0,1},{1,0},{2,3},{3,2},{4,5},{5,4},{6,7},{7,6},{8,9},{9,8},{10,11... | collective-permute-start | bytes 393224 | tf_op jit(solution)/shard_map/ppermute | solution.py:55
  6.0 0.9 %collective-permute-done.lower = bf16[256,256]{1,0:T(8,128)(2,1)S(1)} collective-permute-done((bf16[256,256]{1,0:T(8,128)(2,1)S(1)}, bf16[256,256]{1,0:T(8,128)(2,1)S(1)}, u32[]{:S(2)}, u32[]{:S(2)}) %collective-permute-start) | collective-permute-done | bytes 131104 | tf_op jit(solution)/shard_map/ppermute | solution.py:55
  6.9 0.2 level0_early.1._
  7.1 1.8 %collective-permute-start.1 = (bf16[256,256]{1,0:T(8,128)(2,1)S(1)}, bf16[256,256]{1,0:T(8,128)(2,1)S(1)}, u32[]{:S(2)}, u32[]{:S(2)}) collective-permute-start(bf16[256,256]{1,0:T(8,128)(2,1)S(1)} %level0_early.1._), channel_id=1, source_target_pairs={{0,1},{1,2},{2,3},{3,4},{4,5},{5,6},{6,7},{7,8},{8,9},{9,10},{10,1... | collective-permute-start | bytes 393224 | tf_op jit(solution)/shard_map/ppermute | solution.py:22
  8.8 4.0 %collective-permute-start.2 = (bf16[256,256]{1,0:T(8,128)(2,1)S(1)}, bf16[256,256]{1,0:T(8,128)(2,1)S(1)}, u32[]{:S(2)}, u32[]{:S(2)}) collective-permute-start(bf16[256,256]{1,0:T(8,128)(2,1)S(1)} %get-tuple-element.12.down), channel_id=1, source_target_pairs={{0,15},{1,0},{2,1},{3,2},{4,3},{5,4},{6,5},{7,6},{8,7},{9,8},{10,9... | collective-permute-start | bytes 393224 | tf_op jit(solution)/shard_map/ppermute | solution.py:22
  12.8 0.4 %collective-permute-start.3 = (bf16[256,256]{1,0:T(8,128)(2,1)S(1)}, bf16[256,256]{1,0:T(8,128)(2,1)S(1)}, u32[]{:S(2)}, u32[]{:S(2)}) collective-permute-start(bf16[256,256]{1,0:T(8,128)(2,1)S(1)} %get-tuple-element.13.lower_mat), channel_id=1, source_target_pairs={{0,15},{1,0},{2,1},{3,2},{4,3},{5,4},{6,5},{7,6},{8,7},{9,8},{10,9... | collective-permute-start | bytes 393224 | tf_op jit(solution)/shard_map/ppermute | solution.py:22
  13.3 1.0 %collective-permute-done.4.lower = bf16[256,256]{1,0:T(8,128)(2,1)S(1)} collective-permute-done((bf16[256,256]{1,0:T(8,128)(2,1)S(1)}, bf16[256,256]{1,0:T(8,128)(2,1)S(1)}, u32[]{:S(2)}, u32[]{:S(2)}) %collective-permute-start.4) | collective-permute-done | bytes 131104 | tf_op jit(solution)/shard_map/ppermute | solution.py:22
  14.3 0.2 level0_late.1.refs_0_
  14.6 0.5 %fold.1 = (bf16[3,256,256]{2,1,0:T(8,128)(2,1)S(1)}, bf16[3,256,256]{2,1,0:T(8,128)(2,1)S(1)}, f32[3,256,256]{2,1,0:T(8,128)S(1)}) custom-call(bf16[4,1,256,256]{3,2,1,0:T(8,128)(2,1)S(1)} %copy-done.1, bf16[4,1,256,256]{3,2,1,0:T(8,128)(2,1)S(1)} %copy-done.2, bf16[4,1,2,256,256]{4,3,2,1,0:T(8,128)(2,1)S(1)} %copy-done, bf16[256,256]{1,0:T(8,128)(2,1)S(1)} %level0_early.1._), custom_call_target="tpu_custom_call" | custom-call | flops 301989888 | bytes 3145728 | tf_op jit(solution)/shard_map/fold/pallas_call | solution.py:259
  15.1 0.6 %collective-permute-done.1.below = bf16[256,256]{1,0:T(8,128)(2,1)S(1)} collective-permute-done((bf16[256,256]{1,0:T(8,128)(2,1)S(1)}, bf16[256,256]{1,0:T(8,128)(2,1)S(1)}, u32[]{:S(2)}, u32[]{:S(2)}) %collective-permute-start.1) | collective-permute-done | bytes 131104 | tf_op jit(solution)/shard_map/ppermute | solution.py:22
  15.7 0.2 level1_below.1.part
  15.9 0.8 %collective-permute-done.3.above_mat = bf16[256,256]{1,0:T(8,128)(2,1)S(1)} collective-permute-done((bf16[256,256]{1,0:T(8,128)(2,1)S(1)}, bf16[256,256]{1,0:T(8,128)(2,1)S(1)}, u32[]{:S(2)}, u32[]{:S(2)}) %collective-permute-start.3) | collective-permute-done | bytes 131104 | tf_op jit(solution)/shard_map/ppermute | solution.py:22
  16.7 0.2 level1.1._.refs_1_
  16.9 1.3 %collective-permute-start.6 = (bf16[256,256]{1,0:T(8,128)(2,1)S(1)}, bf16[256,256]{1,0:T(8,128)(2,1)S(1)}, u32[]{:S(2)}, u32[]{:S(2)}) collective-permute-start(bf16[256,256]{1,0:T(8,128)(2,1)S(1)} %level1.1._.refs_1_), channel_id=1, source_target_pairs={{0,2},{1,3},{2,0},{3,1},{4,6},{5,7},{6,4},{7,5},{8,10},{9,11},{10,... | collective-permute-start | bytes 393224 | tf_op jit(solution)/shard_map/ppermute | solution.py:35
  18.2 2.1 %collective-permute-start.7 = (bf16[256,256]{1,0:T(8,128)(2,1)S(1)}, bf16[256,256]{1,0:T(8,128)(2,1)S(1)}, u32[]{:S(2)}, u32[]{:S(2)}) collective-permute-start(bf16[256,256]{1,0:T(8,128)(2,1)S(1)} %level1.1._.refs_1_), channel_id=1, source_target_pairs={{0,14},{1,15},{2,4},{3,5},{4,2},{5,3},{6,8},{7,9},{8,6},{9,7},{10,... | collective-permute-start | bytes 393224 | tf_op jit(solution)/shard_map/ppermute | solution.py:35
  20.3 3.3 %leaf_rest.1.rest_0_.top = bf16[4,256,256]{2,1,0:T(8,128)(2,1)S(1)} custom-call(s32[4,8]{1,0:T(4,128)} %bitcast.2, bf16[12,256,256]{2,1,0:T(8,128)(2,1)} %rhs.5, bf16[12,256,256]{2,1,0:T(8,128)(2,1)} %inverse.5, bf16[8,4,256,256]{3,2,1,0:T(8,128)(2,1)} %factor.5, bf16[8,256,256]{2,1,0:T(8,128)(2,1)S(1)} %get-tuple-element.11.low, ...), custom_call_target="tpu_custom_call" | custom-call | flops 671088640 | bytes 4718592 | tf_op jit(solution)/shard_map/leaf_rest/pallas_call | solution.py:227
  23.6 1.2 %collective-permute-done.6.first = bf16[256,256]{1,0:T(8,128)(2,1)S(1)} collective-permute-done((bf16[256,256]{1,0:T(8,128)(2,1)S(1)}, bf16[256,256]{1,0:T(8,128)(2,1)S(1)}, u32[]{:S(2)}, u32[]{:S(2)}) %collective-permute-start.6) | collective-permute-done | bytes 131104 | tf_op jit(solution)/shard_map/ppermute | solution.py:35
  24.8 2.2 %collective-permute-done.7.second = bf16[256,256]{1,0:T(8,128)(2,1)S(1)} collective-permute-done((bf16[256,256]{1,0:T(8,128)(2,1)S(1)}, bf16[256,256]{1,0:T(8,128)(2,1)S(1)}, u32[]{:S(2)}, u32[]{:S(2)}) %collective-permute-start.7) | collective-permute-done | bytes 131104 | tf_op jit(solution)/shard_map/ppermute | solution.py:35
  26.9 0.2 level2.1.refs_2_
  27.2 2.0 %collective-permute-start.9 = (bf16[256,256]{1,0:T(8,128)(2,1)S(1)}, bf16[256,256]{1,0:T(8,128)(2,1)S(1)}, u32[]{:S(2)}, u32[]{:S(2)}) collective-permute-start(bf16[256,256]{1,0:T(8,128)(2,1)S(1)} %level2.1.refs_2_), channel_id=1, source_target_pairs={{0,4},{1,5},{2,6},{3,7},{4,8},{5,9},{6,10},{7,11},{8,12},{9,13},{1... | collective-permute-start | bytes 393224 | tf_op jit(solution)/shard_map/ppermute | solution.py:22
  29.2 1.3 %collect.1 = (bf16[12,256,256]{2,1,0:T(8,128)(2,1)}, bf16[4,1,256,256]{3,2,1,0:T(8,128)(2,1)}) custom-call(bf16[8,256,256]{2,1,0:T(8,128)(2,1)S(1)} %get-tuple-element.11.low, bf16[4,256,256]{2,1,0:T(8,128)(2,1)S(1)} %leaf_rest.1.rest_0_.top, bf16[256,256]{1,0:T(8,128)(2,1)S(1)} %level0_late.1.refs_0_, bf16[256,256]{1,0:T(8,128)(2,1)S(1)} %level1.1._.refs_1_, ...), custom_call_target="tpu_custom_call" | custom-call | bytes 3932160 | tf_op jit(solution)/shard_map/collect/pallas_call | solution.py:320
  30.6 4.7 %collective-permute-done.8.first = bf16[256,256]{1,0:T(8,128)(2,1)S(1)} collective-permute-done((bf16[256,256]{1,0:T(8,128)(2,1)S(1)}, bf16[256,256]{1,0:T(8,128)(2,1)S(1)}, u32[]{:S(2)}, u32[]{:S(2)}) %collective-permute-start.8) | collective-permute-done | bytes 131104 | tf_op jit(solution)/shard_map/ppermute | solution.py:22
  35.3 0.9 %node_last.1 = bf16[4,1,256,256]{3,2,1,0:T(8,128)(2,1)} custom-call(bf16[256,256]{1,0:T(8,128)(2,1)S(1)} %collective-permute-done.8.first, bf16[256,256]{1,0:T(8,128)(2,1)S(1)} %collective-permute-done.9.second, bf16[3,256,256]{2,1,0:T(8,128)(2,1)S(1)} %get-tuple-element.15.lower_mat, ...), custom_call_target="tpu_custom_call", output_to_operand_aliasing={{}: (5, {})} | custom-call | tf_op jit(solution)/shard_map/node_last/pallas_call | solution.py:359
  (12 shorter events, 0.2 us)
Async XLA Ops:
  1.3 13.3 %copy-start.1 = (bf16[4,1,256,256]{3,2,1,0:T(8,128)(2,1)S(1)}, bf16[4,1,256,256]{3,2,1,0:T(8,128)(2,1)}, u32[]{:S(2)}) copy-start(bf16[4,1,256,256]{3,2,1,0:T(8,128)(2,1)} %rhs.4) | copy-start | bytes 1572868
  1.3 13.3 %copy-start.2 = (bf16[4,1,256,256]{3,2,1,0:T(8,128)(2,1)S(1)}, bf16[4,1,256,256]{3,2,1,0:T(8,128)(2,1)}, u32[]{:S(2)}) copy-start(bf16[4,1,256,256]{3,2,1,0:T(8,128)(2,1)} %inverse.4) | copy-start | bytes 1572868
  5.3 9.2 %copy-start = (bf16[4,1,2,256,256]{4,3,2,1,0:T(8,128)(2,1)S(1)}, bf16[4,1,2,256,256]{4,3,2,1,0:T(8,128)(2,1)}, u32[]{:S(2)}) copy-start(bf16[4,1,2,256,256]{4,3,2,1,0:T(8,128)(2,1)} %factor.4) | copy-start | bytes 3145732
  5.4 1.5 %collective-permute-start = (bf16[256,256]{1,0:T(8,128)(2,1)S(1)}, bf16[256,256]{1,0:T(8,128)(2,1)S(1)}, u32[]{:S(2)}, u32[]{:S(2)}) collective-permute-start(bf16[256,256]{1,0:T(8,128)(2,1)S(1)} %get-tuple-element.14.edge), channel_id=1, source_target_pairs={{0,1},{1,0},{2,3},{3,2},{4,5},{5,4},{6,7},{7,6},{8,9},{9,8},{10,11... | collective-permute-start | bytes 393224 | tf_op jit(solution)/shard_map/ppermute | solution.py:55
  5.9 8.4 %collective-permute-start.4 = (bf16[256,256]{1,0:T(8,128)(2,1)S(1)}, bf16[256,256]{1,0:T(8,128)(2,1)S(1)}, u32[]{:S(2)}, u32[]{:S(2)}) collective-permute-start(bf16[256,256]{1,0:T(8,128)(2,1)S(1)} %get-tuple-element.14.edge), channel_id=1, source_target_pairs={{0,1},{1,2},{2,3},{3,4},{4,5},{5,6},{6,7},{7,8},{8,9},{9,10},{10,1... | collective-permute-start | bytes 393224 | tf_op jit(solution)/shard_map/ppermute | solution.py:22
  7.1 8.6 %collective-permute-start.1 = (bf16[256,256]{1,0:T(8,128)(2,1)S(1)}, bf16[256,256]{1,0:T(8,128)(2,1)S(1)}, u32[]{:S(2)}, u32[]{:S(2)}) collective-permute-start(bf16[256,256]{1,0:T(8,128)(2,1)S(1)} %level0_early.1._), channel_id=1, source_target_pairs={{0,1},{1,2},{2,3},{3,4},{4,5},{5,6},{6,7},{7,8},{8,9},{9,10},{10,1... | collective-permute-start | bytes 393224 | tf_op jit(solution)/shard_map/ppermute | solution.py:22
  8.8 7.1 %collective-permute-start.2 = (bf16[256,256]{1,0:T(8,128)(2,1)S(1)}, bf16[256,256]{1,0:T(8,128)(2,1)S(1)}, u32[]{:S(2)}, u32[]{:S(2)}) collective-permute-start(bf16[256,256]{1,0:T(8,128)(2,1)S(1)} %get-tuple-element.12.down), channel_id=1, source_target_pairs={{0,15},{1,0},{2,1},{3,2},{4,3},{5,4},{6,5},{7,6},{8,7},{9,8},{10,9... | collective-permute-start | bytes 393224 | tf_op jit(solution)/shard_map/ppermute | solution.py:22
  12.8 3.9 %collective-permute-start.3 = (bf16[256,256]{1,0:T(8,128)(2,1)S(1)}, bf16[256,256]{1,0:T(8,128)(2,1)S(1)}, u32[]{:S(2)}, u32[]{:S(2)}) collective-permute-start(bf16[256,256]{1,0:T(8,128)(2,1)S(1)} %get-tuple-element.13.lower_mat), channel_id=1, source_target_pairs={{0,15},{1,0},{2,1},{3,2},{4,3},{5,4},{6,5},{7,6},{8,7},{9,8},{10,9... | collective-permute-start | bytes 393224 | tf_op jit(solution)/shard_map/ppermute | solution.py:22
  14.5 2.3 %collective-permute-start.5 = (bf16[256,256]{1,0:T(8,128)(2,1)S(1)}, bf16[256,256]{1,0:T(8,128)(2,1)S(1)}, u32[]{:S(2)}, u32[]{:S(2)}) collective-permute-start(bf16[256,256]{1,0:T(8,128)(2,1)S(1)} %level0_late.1.refs_0_), channel_id=1, source_target_pairs={{0,1},{1,0},{2,3},{3,2},{4,5},{5,4},{6,7},{7,6},{8,9},{9,8},{10,11... | collective-permute-start | bytes 393224 | tf_op jit(solution)/shard_map/ppermute | solution.py:55
  16.9 7.8 %collective-permute-start.6 = (bf16[256,256]{1,0:T(8,128)(2,1)S(1)}, bf16[256,256]{1,0:T(8,128)(2,1)S(1)}, u32[]{:S(2)}, u32[]{:S(2)}) collective-permute-start(bf16[256,256]{1,0:T(8,128)(2,1)S(1)} %level1.1._.refs_1_), channel_id=1, source_target_pairs={{0,2},{1,3},{2,0},{3,1},{4,6},{5,7},{6,4},{7,5},{8,10},{9,11},{10,... | collective-permute-start | bytes 393224 | tf_op jit(solution)/shard_map/ppermute | solution.py:35
  18.2 8.7 %collective-permute-start.7 = (bf16[256,256]{1,0:T(8,128)(2,1)S(1)}, bf16[256,256]{1,0:T(8,128)(2,1)S(1)}, u32[]{:S(2)}, u32[]{:S(2)}) collective-permute-start(bf16[256,256]{1,0:T(8,128)(2,1)S(1)} %level1.1._.refs_1_), channel_id=1, source_target_pairs={{0,14},{1,15},{2,4},{3,5},{4,2},{5,3},{6,8},{7,9},{8,6},{9,7},{10,... | collective-permute-start | bytes 393224 | tf_op jit(solution)/shard_map/ppermute | solution.py:35
  27.2 8.1 %collective-permute-start.8 = (bf16[256,256]{1,0:T(8,128)(2,1)S(1)}, bf16[256,256]{1,0:T(8,128)(2,1)S(1)}, u32[]{:S(2)}, u32[]{:S(2)}) collective-permute-start(bf16[256,256]{1,0:T(8,128)(2,1)S(1)} %level2.1.refs_2_), channel_id=1, source_target_pairs={{0,12},{1,13},{2,14},{3,15},{4,0},{5,1},{6,2},{7,3},{8,4},{9,5},{1... | collective-permute-start | bytes 393224 | tf_op jit(solution)/shard_map/ppermute | solution.py:22
  27.2 8.1 %collective-permute-start.9 = (bf16[256,256]{1,0:T(8,128)(2,1)S(1)}, bf16[256,256]{1,0:T(8,128)(2,1)S(1)}, u32[]{:S(2)}, u32[]{:S(2)}) collective-permute-start(bf16[256,256]{1,0:T(8,128)(2,1)S(1)} %level2.1.refs_2_), channel_id=1, source_target_pairs={{0,4},{1,5},{2,6},{3,7},{4,8},{5,9},{6,10},{7,11},{8,12},{9,13},{1... | collective-permute-start | bytes 393224 | tf_op jit(solution)/shard_map/ppermute | solution.py:22
